TPU v7x, 256 devices: a whole 4x4x8 slice. The times are simulated.
256 devices in a mesh: dp: 32 (over x, z_lo, core), tensor: 8 (over z_hi, y).
Axes of the slice: x: 4, y: 4, z: 8 (z_hi: 2, z_lo: 4; z = z_hi * 4 + z_lo), core: 2. Of those that a mesh axis runs over, the one named last changes fastest.
Arguments:
- tokens: bfloat16 [512, 64, 1536], P('tensor', 'dp'), may hold values from -6 to 6
- cached_len: int32 [64], P('dp'), may hold values from 0 to 32768, as said below
- prompt_group: int32 [64], P('dp'), may hold values from 0 to 7, as said below
- attn_gain: float32 [1536], replicated, may hold values from 0.1 to 1.9
- w_query: bfloat16 [1536, 1536], P(None, 'tensor'), may hold values from -0.15625 to 0.15625
- key_matrix: bfloat16 [1536, 768], P(None, 'tensor'), may hold values from -0.15625 to 0.15625
- value_matrix: bfloat16 [1536, 768], P(None, 'tensor'), may hold values from -0.15625 to 0.15625
- w_out: bfloat16 [1536, 1536], P('tensor'), may hold values from -1.25 to 1.25
- window_cache_keys: bfloat16 [64, 4096, 768], P('dp', None, 'tensor'), may hold values from -400 to 400
- window_cache_values: bfloat16 [64, 4096, 768], P('dp', None, 'tensor'), may hold values from -6 to 6
- prompt_keys: bfloat16 [8, 4096, 768], P(None, 'dp', 'tensor'), may hold values from -6 to 6
- prompt_values: bfloat16 [8, 4096, 768], P(None, 'dp', 'tensor'), may hold values from -6 to 6
- mlp_gain: float32 [1536], replicated, may hold values from 0.1 to 1.9
- w_gate: bfloat16 [1536, 4096], P(None, 'tensor'), may hold values from -0.15625 to 0.15625
- w_up: bfloat16 [1536, 4096], P(None, 'tensor'), may hold values from -0.15625 to 0.15625
- w_down: bfloat16 [4096, 1536], P('tensor'), may hold values from -0.09375 to 0.09375
Outputs:
- output: bfloat16 [512, 64, 1536], P('tensor', 'dp')
Inputs may be any that keep to these rules, and one draw needn't show every extreme that they name: `cached_len`: in each prompt group some request has no cached tokens, and exactly one request in all has 32768. `prompt_group`: every group holds 8 requests.
All inputs are finite; a program needn't handle non-finite values.
Results may differ from a plain program's by a relative error of at most 0.024.
Values may be sent and summed in bfloat16 or wider, within the bound.
A program may use at most 128 MiB of HBM per device.

v0:
```python
import math

import jax
import jax.numpy as jnp
from jax import lax
from jax.sharding import PartitionSpec as P

MODEL_WIDTH = 1536
HEAD_SIZE = 96
FRESH_TOKENS = 512
WINDOW_SPAN = 4096
SINKS = 4
PROMPT_TOKENS = 4096


rope_base = 10000.0
epsilon = 1e-05
far_below = -1e30


def norm_rows(values, gain_vec):
    widened = values.astype(jnp.float32)
    factor = lax.rsqrt(jnp.mean(widened * widened, axis=-1, keepdims=True) + epsilon)
    return (widened * factor * gain_vec).astype(jnp.bfloat16)


def rotate(values, positions):
    half_dim = values.shape[-1] // 2
    frequency = rope_base ** (-2.0 * jnp.arange(half_dim, dtype=jnp.float32) / values.shape[-1])
    angles = positions.astype(jnp.float32)[..., None, None] * frequency
    cosine = jnp.cos(angles)
    sine_part = jnp.sin(angles)
    first_half = values[..., :half_dim]
    second_half = values[..., half_dim:]
    return jnp.concatenate(
        [
            first_half * cosine - second_half * sine_part,
            second_half * cosine + first_half * sine_part,
        ],
        axis=-1,
    )


def absorb(soft_state, queries, key_block, value_block, visible, score_scale):
    row_peak, row_sum, accumulated = soft_state
    scores = (
        jnp.einsum("irhgd,rkhd->rhgik", queries, key_block, preferred_element_type=jnp.float32)
        * score_scale
    )
    scores = jnp.where(visible[:, None, None], scores, -jnp.inf)
    new_peak = jnp.maximum(row_peak, jnp.max(scores, axis=-1))
    factor = jnp.exp(row_peak - new_peak)
    weights = jnp.exp(scores - new_peak[..., None])
    blended = jnp.einsum(
        "rhgik,rkhd->rhgid",
        weights.astype(jnp.bfloat16),
        value_block,
        preferred_element_type=jnp.float32,
    )
    return (
        new_peak,
        row_sum * factor + jnp.sum(weights, axis=-1),
        accumulated * factor[..., None] + blended,
    )


def shared_block(soft_state, pieces, queries, selector, horizon, score_scale):
    key_piece, value_piece = pieces
    row_count = key_piece.shape[1]
    key_heads = key_piece.shape[2] // HEAD_SIZE
    local_reqs = queries.shape[1]
    picked_keys = jnp.take(key_piece, selector, axis=0).reshape(
        local_reqs, row_count, key_heads, HEAD_SIZE
    )
    picked_values = jnp.take(value_piece, selector, axis=0).reshape(
        local_reqs, row_count, key_heads, HEAD_SIZE
    )
    block_len = math.gcd(row_count, FRESH_TOKENS)

    def block_step(running, block_index):
        block_start = block_index * block_len
        key_block = lax.dynamic_slice_in_dim(picked_keys, block_start, block_len, 1)
        value_block = lax.dynamic_slice_in_dim(picked_values, block_start, block_len, 1)
        prompt_pos = block_start + jnp.arange(block_len, dtype=jnp.int32)
        visible = (prompt_pos[None, None, :] < SINKS) | (
            prompt_pos[None, None, :] > horizon[:, :, None]
        )
        return (absorb(running, queries, key_block, value_block, visible, score_scale), None)

    return lax.scan(block_step, soft_state, jnp.arange(row_count // block_len, dtype=jnp.int32))[0]


def body(
    tokens,
    cached_len,
    prompt_group,
    attn_gain,
    w_query,
    key_matrix,
    value_matrix,
    w_out,
    window_cache_keys,
    window_cache_values,
    prompt_keys,
    prompt_values,
    mlp_gain,
    w_gate,
    w_up,
    w_down,
):
    local_rows = tokens.shape[0]
    local_reqs = tokens.shape[1]
    query_cols = w_query.shape[1]
    key_cols = key_matrix.shape[1]
    hidden_cols = w_gate.shape[1]
    key_heads = key_cols // HEAD_SIZE
    query_group_width = query_cols // key_cols
    score_scale = 1.0 / math.sqrt(HEAD_SIZE)
    source = norm_rows(tokens, attn_gain)
    offset = 0
    row_piece = lax.all_gather(source, "tensor", axis=0, tiled=True)
    row_count = row_piece.shape[0]
    normed = row_piece
    flattened_rows = normed.reshape(row_count * local_reqs, MODEL_WIDTH)
    positions = (
        PROMPT_TOKENS + cached_len[None, :] + jnp.arange(row_count, dtype=jnp.int32)[:, None]
    )
    project_queries = jnp.dot(flattened_rows, w_query, preferred_element_type=jnp.float32).reshape(
        row_count, local_reqs, query_cols // HEAD_SIZE, HEAD_SIZE
    )
    fresh_keys = jnp.dot(flattened_rows, key_matrix, preferred_element_type=jnp.float32).reshape(
        row_count, local_reqs, key_heads, HEAD_SIZE
    )
    fresh_values = (
        jnp.dot(flattened_rows, value_matrix, preferred_element_type=jnp.float32)
        .astype(jnp.bfloat16)
        .reshape(row_count, local_reqs, key_cols)
    )
    project_queries = (
        rotate(project_queries, positions)
        .astype(jnp.bfloat16)
        .reshape(row_count, local_reqs, query_cols)
    )
    fresh_keys = (
        rotate(fresh_keys, positions).astype(jnp.bfloat16).reshape(row_count, local_reqs, key_cols)
    )
    gathered = jnp.concatenate([project_queries, fresh_keys, fresh_values], axis=2)
    queries = gathered[:, :, offset : offset + query_cols].reshape(
        FRESH_TOKENS, local_reqs, key_heads, query_group_width, HEAD_SIZE
    )
    own_keys = jnp.swapaxes(
        gathered[:, :, offset + query_cols : offset + query_cols + key_cols], 0, 1
    ).reshape(local_reqs, FRESH_TOKENS, key_heads, HEAD_SIZE)
    own_values = jnp.swapaxes(
        gathered[:, :, offset + query_cols + key_cols : offset + query_cols + 2 * key_cols], 0, 1
    ).reshape(local_reqs, FRESH_TOKENS, key_heads, HEAD_SIZE)
    state_shape = (local_reqs, key_heads, query_group_width, FRESH_TOKENS)
    soft_state = (
        jnp.full(state_shape, far_below, jnp.float32),
        jnp.zeros(state_shape, jnp.float32),
        jnp.zeros(state_shape + (HEAD_SIZE,), jnp.float32),
    )
    row_ids = jnp.arange(FRESH_TOKENS, dtype=jnp.int32)
    causal = jnp.broadcast_to(
        row_ids[None, None, :] <= row_ids[None, :, None], (local_reqs, FRESH_TOKENS, FRESH_TOKENS)
    )
    soft_state = absorb(soft_state, queries, own_keys, own_values, causal, score_scale)
    past_keys = window_cache_keys.reshape(local_reqs, WINDOW_SPAN, key_heads, HEAD_SIZE)
    past_values = window_cache_values.reshape(local_reqs, WINDOW_SPAN, key_heads, HEAD_SIZE)

    def window_step(running, block_index):
        block_start = block_index * FRESH_TOKENS
        key_block = lax.dynamic_slice_in_dim(past_keys, block_start, FRESH_TOKENS, 1)
        value_block = lax.dynamic_slice_in_dim(past_values, block_start, FRESH_TOKENS, 1)
        slot_ids = block_start + row_ids
        visible = (slot_ids[None, None, :] >= WINDOW_SPAN - cached_len[:, None, None]) & (
            slot_ids[None, None, :] > row_ids[None, :, None]
        )
        return (absorb(running, queries, key_block, value_block, visible, score_scale), None)

    soft_state = lax.scan(
        window_step, soft_state, jnp.arange(WINDOW_SPAN // FRESH_TOKENS, dtype=jnp.int32)
    )[0]
    horizon = PROMPT_TOKENS + cached_len[:, None] + row_ids[None, :] - WINDOW_SPAN
    soft_state = shared_block(
        soft_state,
        (
            lax.all_gather(prompt_keys, "dp", axis=1, tiled=True),
            lax.all_gather(prompt_values, "dp", axis=1, tiled=True),
        ),
        queries,
        prompt_group,
        horizon,
        score_scale,
    )
    row_peak, row_sum, accumulated = soft_state
    attended = (accumulated / row_sum[..., None]).astype(jnp.bfloat16)
    attended = attended.transpose(3, 0, 1, 2, 4).reshape(FRESH_TOKENS, local_reqs, query_cols)
    picked = attended
    attn_part = lax.psum_scatter(
        jnp.dot(
            picked.reshape(lax.axis_size("tensor") * local_rows * local_reqs, query_cols),
            w_out,
            preferred_element_type=jnp.float32,
        )
        .reshape(lax.axis_size("tensor") * local_rows, local_reqs, MODEL_WIDTH)
        .astype(jnp.bfloat16),
        "tensor",
        scatter_dimension=0,
        tiled=True,
    ).astype(jnp.float32)
    residual = (tokens.astype(jnp.float32) + attn_part).astype(jnp.bfloat16)
    row_piece = lax.all_gather(norm_rows(residual, mlp_gain), "tensor", axis=0, tiled=True)
    row_count = row_piece.shape[0]
    flattened_rows = row_piece.reshape(row_count * local_reqs, MODEL_WIDTH)
    gate_part = jnp.dot(flattened_rows, w_gate, preferred_element_type=jnp.float32)
    up_part = jnp.dot(flattened_rows, w_up, preferred_element_type=jnp.float32)
    hidden = (
        (jax.nn.silu(gate_part) * up_part)
        .astype(jnp.bfloat16)
        .reshape(row_count, local_reqs, hidden_cols)
    )
    picked = hidden
    mlp_part = lax.psum_scatter(
        jnp.dot(
            picked.reshape(lax.axis_size("tensor") * local_rows * local_reqs, hidden_cols),
            w_down,
            preferred_element_type=jnp.float32,
        )
        .reshape(lax.axis_size("tensor") * local_rows, local_reqs, MODEL_WIDTH)
        .astype(jnp.bfloat16),
        "tensor",
        scatter_dimension=0,
        tiled=True,
    ).astype(jnp.float32)
    return (residual.astype(jnp.float32) + mlp_part).astype(jnp.bfloat16)


def solution(mesh):
    in_specs = (
        P("tensor", "dp", None),
        P("dp"),
        P("dp"),
        P(),
        P(None, "tensor"),
        P(None, "tensor"),
        P(None, "tensor"),
        P("tensor", None),
        P("dp", None, "tensor"),
        P("dp", None, "tensor"),
        P(None, "dp", "tensor"),
        P(None, "dp", "tensor"),
        P(),
        P(None, "tensor"),
        P(None, "tensor"),
        P("tensor", None),
    )
    out_specs = P("tensor", "dp", None)
    return jax.shard_map(body, mesh=mesh, in_specs=in_specs, out_specs=out_specs, check_vma=False)
```

profile of v0, /device:TPU:65, one launch (start us, length us, event | category | flops | bytes accessed | tf_op | source)
XLA Modules:
  0.0 684.4 jit_solution(3983258544674495673)
XLA Ops:
  15.8 85.5 %all-gather.5.cloned.1.call-done = bf16[512,2,1536]{2,0,1:T(8,128)(2,1)} async-done(((bf16[64,2,1536]{2,0,1:T(8,128)(2,1)}), bf16[512,2,1536]{2,0,1:T(8,128)(2,1)}) %all-gather.5.cloned.1.call-update) | async-done | bytes 3145744 | tf_op jit(solution)/shard_map/all_gather | solution.py:121
  101.3 3.1 convolution_bitcast_fusion
  106.5 2.8 fusion.54
  109.4 4.9 copy.26
  114.3 7.6 %reshape.377 = bf16[1024,1536]{1,0:T(8,128)(2,1)} reshape(bf16[512,2,1536]{2,1,0:T(2,128)(2,1)} %copy.26) | data formatting | bytes 6291456 | tf_op jit(solution)/shard_map/reshape | solution.py:124
  121.9 3.0 convolution_convert_fusion.2
  125.0 3.4 fusion.53
  130.0 57.7 %while.32 = (s32[]{:T(128)}, f32[2,1,2,512]{3,2,0,1:T(2,128)S(1)}, f32[2,1,2,512]{3,2,0,1:T(2,128)S(1)}, f32[2,1,2,512,96]{3,4,2,0,1:T(8,128)S(1)}, s32[8]{0:T(1...) while((s32[]{:T(128)}, f32[2,1,2,512]{3,2,0,1:T(2,128)S(1)}, ...), condition=%wide.region_6.7_spmd.clone.clone, body=%wide.region_3.6_spmd.clone.clone.sunk | while | flops 415374848 | bytes 17703132 | solution.py:181
  162.7 2.4 fusion.133
  188.7 3.6 gather_fusion
  192.3 67.0 %all-gather.9.cloned.1.call-done = bf16[8,4096,96]{1,2,0:T(8,128)(2,1)} async-done(((bf16[8,128,96]{1,2,0:T(8,128)(2,1)}), bf16[8,4096,96]{1,2,0:T(8,128)(2,1)}) %all-gather.9.cloned.1.call-update) | async-done | bytes 6291472 | tf_op jit(solution)/shard_map/all_gather | solution.py:189
  259.2 4.7 gather_fusion.1
  263.9 3.4 select_bitcast_fusion
  267.4 61.9 %while.31 = (s32[]{:T(128)}, f32[2,1,2,512]{3,2,0,1:T(2,128)S(1)}, f32[2,1,2,512]{3,2,0,1:T(2,128)S(1)}, f32[2,1,2,512,96]{3,4,2,0,1:T(8,128)}, s32[8]{0:T(128)S...) while((s32[]{:T(128)}, f32[2,1,2,512]{3,2,0,1:T(2,128)S(1)}, ...), condition=%wide.region_10.12_spmd.clone, body=%wide.region_7.0_spmd.clone.sunk | while | flops 415639040 | bytes 23475464 | solution.py:90
  330.6 2.7 convolution_convert_fusion
  333.3 106.3 %reduce-scatter.3.cloned.1.call-done = bf16[64,2,1536]{2,0,1:T(8,128)(2,1)} async-done(((bf16[512,2,1536]{2,0,1:T(8,128)(2,1)}), bf16[64,2,1536]{2,0,1:T(8,128)(2,1)}) %reduce-scatter.3.cloned.1.call-update) | async-done | bytes 393232 | tf_op jit(solution)/shard_map/reduce_scatter | solution.py:200
  442.7 88.2 %all-gather.11.cloned.1.call-done = bf16[512,2,1536]{2,0,1:T(8,128)(2,1)} async-done(((bf16[64,2,1536]{2,0,1:T(8,128)(2,1)}), bf16[512,2,1536]{2,0,1:T(8,128)(2,1)}) %all-gather.11.cloned.1.call-update) | async-done | bytes 3145744 | tf_op jit(solution)/shard_map/all_gather | solution.py:213
  531.0 6.8 copy.30
  537.8 7.6 %reshape.383 = bf16[1024,1536]{1,0:T(8,128)(2,1)} reshape(bf16[512,2,1536]{2,1,0:T(2,128)(2,1)} %copy.30) | data formatting | bytes 6291456 | tf_op jit(solution)/shard_map/reshape | solution.py:215
  545.4 5.0 fusion.99
  550.4 8.2 %convolution_convert_fusion.1 = bf16[1024,1536]{1,0:T(8,128)(2,1)} fusion(bf16[512,1536]{1,0:T(8,128)(2,1)S(1)} %copy-done, f32[1024,512]{1,0:T(8,128)} %fusion.99, bf16[1024,1536]{1,0:T(8,128)(2,1)} %reshape.383, bf16[1536,512]{1,0:T(8,128)(2,1)} %param.36), kind=kOutput, calls=%fused_computation.64 | convolution fusion | flops 3225944064 | bytes 11534336 | tf_op jit(solution)/shard_map/dot_general | solution.py:225
  558.6 7.2 %convert_element_type.87 = bf16[512,2,1536]{2,1,0:T(2,128)(2,1)} reshape(bf16[1024,1536]{1,0:T(8,128)(2,1)} %convolution_convert_fusion.1) | data formatting | bytes 6291456 | tf_op jit(solution)/shard_map/convert_element_type | solution.py:231
  565.9 4.0 copy.31
  569.9 105.3 %reduce-scatter.5.cloned.1.call-done = bf16[64,2,1536]{2,0,1:T(8,128)(2,1)} async-done(((bf16[512,2,1536]{2,0,1:T(8,128)(2,1)}), bf16[64,2,1536]{2,0,1:T(8,128)(2,1)}) %reduce-scatter.5.cloned.1.call-update) | async-done | bytes 393232 | tf_op jit(solution)/shard_map/reduce_scatter | solution.py:224
  (281 shorter events, 126.0 us)
Async XLA Ops:
  6.5 543.9 %copy-start = (bf16[512,1536]{1,0:T(8,128)(2,1)S(1)}, bf16[512,1536]{1,0:T(8,128)(2,1)}, u32[]{:S(2)}) copy-start(bf16[512,1536]{1,0:T(8,128)(2,1)} %param.37) | copy-start | bytes 4718596
  6.5 94.7 %all-gather.5.cloned.1.call-start = ((), (), s32[]{:S(2)}) async-start(), calls=%async_computation.2 | async-start | bytes 3538944 | tf_op jit(solution)/shard_map/all_gather | solution.py:121
  9.7 95.4 %copy-start.13 = (bf16[1536,192]{0,1:T(8,128)(2,1)S(1)}, bf16[1536,192]{0,1:T(8,128)(2,1)}, u32[]{:S(2)}) copy-start(bf16[1536,192]{0,1:T(8,128)(2,1)} %param.26) | copy-start | bytes 1769476
  9.8 178.9 %all-gather.7.cloned.1.call-start = ((), (), s32[]{:S(2)}) async-start(), calls=%async_computation.3 | async-start | bytes 6488064 | tf_op jit(solution)/shard_map/all_gather | solution.py:188
  10.5 248.7 %all-gather.9.cloned.1.call-start = ((), (), s32[]{:S(2)}) async-start(), calls=%async_computation.4 | async-start | bytes 6488064 | tf_op jit(solution)/shard_map/all_gather | solution.py:189
  11.3 428.3 %reduce-scatter.3.cloned.1.call-start = ((), (), s32[]{:S(2)}) async-start(), calls=%async_computation.5 | async-start | bytes 3538944 | tf_op jit(solution)/shard_map/reduce_scatter | solution.py:200
  101.3 4.0 copy-start.1
  114.2 7.6 %copy-start.9 = (bf16[1536,96]{0,1:T(8,128)(2,1)S(1)}, bf16[1536,96]{0,1:T(8,128)(2,1)}, u32[]{:S(2)}) copy-start(bf16[1536,96]{0,1:T(8,128)(2,1)} %param.28) | copy-start | bytes 884740
  125.0 3.6 copy-start.3
  267.4 63.1 %copy-start.8 = (bf16[192,1536]{1,0:T(8,128)(2,1)S(1)}, bf16[192,1536]{1,0:T(8,128)(2,1)}, u32[]{:S(2)}) copy-start(bf16[192,1536]{1,0:T(8,128)(2,1)} %param.29) | copy-start | bytes 1769476
  267.4 4.3 copy-start.6
  275.1 4.3 copy-start.6
  282.9 4.3 copy-start.6
  290.6 4.3 copy-start.6
  298.4 4.3 copy-start.6
  306.1 4.3 copy-start.6
  313.8 4.3 copy-start.6
  321.6 4.3 copy-start.6
  330.5 109.0 %copy-start.2 = (bf16[64,2,1536]{2,1,0:T(2,128)(2,1)S(1)}, bf16[64,2,1536]{2,1,0:T(2,128)(2,1)}, u32[]{:S(2)}) copy-start(bf16[64,2,1536]{2,1,0:T(2,128)(2,1)} %param.22) | copy-start | bytes 1179652
  330.5 110.2 %copy-start.11 = (f32[1536]{0:T(1024)S(1)}, f32[1536]{0:T(1024)}, u32[]{:S(2)}) copy-start(f32[1536]{0:T(1024)} %param.34) | copy-start | bytes 18436
  333.3 197.7 %all-gather.11.cloned.1.call-start = ((), (), s32[]{:S(2)}) async-start(), calls=%async_computation.6 | async-start | bytes 3538944 | tf_op jit(solution)/shard_map/all_gather | solution.py:213
  442.7 232.6 %reduce-scatter.5.cloned.1.call-start = ((), (), s32[]{:S(2)}) async-start(), calls=%async_computation.7 | async-start | bytes 3538944 | tf_op jit(solution)/shard_map/reduce_scatter | solution.py:224
  537.8 7.6 %copy-start.12 = (bf16[1536,512]{1,0:T(8,128)(2,1)S(1)}, bf16[1536,512]{1,0:T(8,128)(2,1)}, u32[]{:S(2)}) copy-start(bf16[1536,512]{1,0:T(8,128)(2,1)} %param.35) | copy-start | bytes 4718596
  569.9 105.3 %copy-start.4 = (bf16[64,2,1536]{2,0,1:T(8,128)(2,1)S(1)}, bf16[64,2,1536]{2,0,1:T(8,128)(2,1)}, u32[]{:S(2)}) copy-start(bf16[64,2,1536]{2,0,1:T(8,128)(2,1)} %reduce-scatter.3.cloned.1.call-done) | copy-start | bytes 1179652
  (11 other events, 11.1 us)
Sparse Core Ops, SparseCore 0:
  9.9 91.2 all-gather.4
  103.0 76.6 all-gather.6
  181.4 77.7 all-gather.8
  333.4 106.1 reduce-scatter.2
  442.8 88.1 all-gather.10
  570.1 105.1 reduce-scatter.4
where the time goes:
time: 690 us; the launch traced here: 684 us
  waiting for transfers between devices  454 us (66%)
  matrix products  95.5 us (14%)
  local copies, waits for them, and re-layouts  58.9 us (9%)
  other arithmetic  50.4 us (7%)
  between operations  13.7 us (2%)
  loops' own time  11.9 us (2%)
    reduce_scatter x2, waiting for transfers between devices, body(): lax.psum_scatter(jnp.dot(picked.reshape(lax.axis_size('tensor') * local_r...  212 us
    all_gather x1, waiting for transfers between devices, body(): lax.all_gather(norm_rows(residual, mlp_gain), 'tensor', axis=0, tiled=True)  88.2 us
    all_gather x1, waiting for transfers between devices, body(): row_piece = lax.all_gather(source, 'tensor', axis=0, tiled=True)  85.5 us
    all_gather x1, waiting for transfers between devices, body(): lax.all_gather(prompt_values, 'dp', axis=1, tiled=True)  67 us
    dot_general x17, matrix products, absorb(): jnp.einsum('rhgik,rkhd->rhgid', weights.astype(jnp.bfloat16), value_block...  38.8 us
    dot_general x17, matrix products, absorb(): jnp.einsum('irhgd,rkhd->rhgik', queries, key_block, preferred_element_typ...  33.6 us
    reduce_sum x17, other arithmetic, absorb(): jnp.sum(weights, axis=-1)  19 us
  transfers between devices with their start and end apart: 6, of which 5 were waited for; matrix products, arithmetic and copies ran while one was open for 13% of the time, Pallas kernels for 0%

commit v1 on v0

--- a/solution.py
+++ b/solution.py
@@ -69,12 +69,8 @@
     row_count = key_piece.shape[1]
     key_heads = key_piece.shape[2] // HEAD_SIZE
     local_reqs = queries.shape[1]
-    picked_keys = jnp.take(key_piece, selector, axis=0).reshape(
-        local_reqs, row_count, key_heads, HEAD_SIZE
-    )
-    picked_values = jnp.take(value_piece, selector, axis=0).reshape(
-        local_reqs, row_count, key_heads, HEAD_SIZE
-    )
+    picked_keys = key_piece.reshape(local_reqs, row_count, key_heads, HEAD_SIZE)
+    picked_values = value_piece.reshape(local_reqs, row_count, key_heads, HEAD_SIZE)
     block_len = math.gcd(row_count, FRESH_TOKENS)
 
     def block_step(running, block_index):
@@ -88,6 +84,36 @@
         return (absorb(running, queries, key_block, value_block, visible, score_scale), None)
 
     return lax.scan(block_step, soft_state, jnp.arange(row_count // block_len, dtype=jnp.int32))[0]
+
+
+def gather_rows(piece):
+    across = lax.all_gather(piece, "zh", axis=0, tiled=False)
+    both = lax.all_gather(across, "y", axis=0, tiled=False)
+    both = jnp.swapaxes(both, 0, 1)
+    return both.reshape((-1,) + piece.shape[1:])
+
+
+def scatter_rows(full):
+    rows = full.shape[0]
+    zh_size = lax.axis_size("zh")
+    y_size = lax.axis_size("y")
+    split = full.reshape((zh_size, y_size, rows // (zh_size * y_size)) + full.shape[1:])
+    part = lax.psum_scatter(split, "y", scatter_dimension=1, tiled=False)
+    return lax.psum_scatter(part, "zh", scatter_dimension=0, tiled=False)
+
+
+def prompt_for_requests(prompt_keys, prompt_values, prompt_group):
+    every_group = lax.all_gather(prompt_group, "dp", axis=0, tiled=True)
+    dp_size = lax.axis_size("dp")
+    wanted = every_group.reshape(dp_size, -1)
+    both = jnp.stack([prompt_keys, prompt_values], axis=1)
+    outgoing = jnp.take(both, wanted, axis=0)
+    incoming = lax.all_to_all(outgoing, "dp", 0, 0, tiled=False)
+    local_reqs = wanted.shape[1]
+    rows = prompt_keys.shape[1]
+    incoming = incoming.transpose(1, 2, 0, 3, 4)
+    incoming = incoming.reshape(local_reqs, 2, dp_size * rows, prompt_keys.shape[2])
+    return incoming[:, 0], incoming[:, 1]
 
 
 def body(
@@ -118,7 +144,7 @@
     score_scale = 1.0 / math.sqrt(HEAD_SIZE)
     source = norm_rows(tokens, attn_gain)
     offset = 0
-    row_piece = lax.all_gather(source, "tensor", axis=0, tiled=True)
+    row_piece = gather_rows(source)
     row_count = row_piece.shape[0]
     normed = row_piece
     flattened_rows = normed.reshape(row_count * local_reqs, MODEL_WIDTH)
@@ -184,10 +210,7 @@
     horizon = PROMPT_TOKENS + cached_len[:, None] + row_ids[None, :] - WINDOW_SPAN
     soft_state = shared_block(
         soft_state,
-        (
-            lax.all_gather(prompt_keys, "dp", axis=1, tiled=True),
-            lax.all_gather(prompt_values, "dp", axis=1, tiled=True),
-        ),
+        prompt_for_requests(prompt_keys, prompt_values, prompt_group),
         queries,
         prompt_group,
         horizon,
@@ -197,20 +220,17 @@
     attended = (accumulated / row_sum[..., None]).astype(jnp.bfloat16)
     attended = attended.transpose(3, 0, 1, 2, 4).reshape(FRESH_TOKENS, local_reqs, query_cols)
     picked = attended
-    attn_part = lax.psum_scatter(
+    attn_part = scatter_rows(
         jnp.dot(
-            picked.reshape(lax.axis_size("tensor") * local_rows * local_reqs, query_cols),
+            picked.reshape(FRESH_TOKENS * local_reqs, query_cols),
             w_out,
             preferred_element_type=jnp.float32,
         )
-        .reshape(lax.axis_size("tensor") * local_rows, local_reqs, MODEL_WIDTH)
-        .astype(jnp.bfloat16),
-        "tensor",
-        scatter_dimension=0,
-        tiled=True,
+        .reshape(FRESH_TOKENS, local_reqs, MODEL_WIDTH)
+        .astype(jnp.bfloat16)
     ).astype(jnp.float32)
     residual = (tokens.astype(jnp.float32) + attn_part).astype(jnp.bfloat16)
-    row_piece = lax.all_gather(norm_rows(residual, mlp_gain), "tensor", axis=0, tiled=True)
+    row_piece = gather_rows(norm_rows(residual, mlp_gain))
     row_count = row_piece.shape[0]
     flattened_rows = row_piece.reshape(row_count * local_reqs, MODEL_WIDTH)
     gate_part = jnp.dot(flattened_rows, w_gate, preferred_element_type=jnp.float32)
@@ -221,39 +241,43 @@
         .reshape(row_count, local_reqs, hidden_cols)
     )
     picked = hidden
-    mlp_part = lax.psum_scatter(
+    mlp_part = scatter_rows(
         jnp.dot(
-            picked.reshape(lax.axis_size("tensor") * local_rows * local_reqs, hidden_cols),
+            picked.reshape(FRESH_TOKENS * local_reqs, hidden_cols),
             w_down,
             preferred_element_type=jnp.float32,
         )
-        .reshape(lax.axis_size("tensor") * local_rows, local_reqs, MODEL_WIDTH)
-        .astype(jnp.bfloat16),
-        "tensor",
-        scatter_dimension=0,
-        tiled=True,
+        .reshape(FRESH_TOKENS, local_reqs, MODEL_WIDTH)
+        .astype(jnp.bfloat16)
     ).astype(jnp.float32)
     return (residual.astype(jnp.float32) + mlp_part).astype(jnp.bfloat16)
 
 
 def solution(mesh):
+    zh_size = 2
+    split_mesh = jax.sharding.Mesh(
+        mesh.devices.reshape(mesh.devices.shape[0], zh_size, -1), ("dp", "zh", "y")
+    )
+    rows = ("zh", "y")
     in_specs = (
-        P("tensor", "dp", None),
+        P(rows, "dp", None),
         P("dp"),
         P("dp"),
         P(),
-        P(None, "tensor"),
-        P(None, "tensor"),
-        P(None, "tensor"),
-        P("tensor", None),
-        P("dp", None, "tensor"),
-        P("dp", None, "tensor"),
-        P(None, "dp", "tensor"),
-        P(None, "dp", "tensor"),
+        P(None, rows),
+        P(None, rows),
+        P(None, rows),
+        P(rows, None),
+        P("dp", None, rows),
+        P("dp", None, rows),
+        P(None, "dp", rows),
+        P(None, "dp", rows),
         P(),
-        P(None, "tensor"),
-        P(None, "tensor"),
-        P("tensor", None),
-    )
-    out_specs = P("tensor", "dp", None)
-    return jax.shard_map(body, mesh=mesh, in_specs=in_specs, out_specs=out_specs, check_vma=False)
+        P(None, rows),
+        P(None, rows),
+        P(rows, None),
+    )
+    out_specs = P(rows, "dp", None)
+    return jax.shard_map(
+        body, mesh=split_mesh, in_specs=in_specs, out_specs=out_specs, check_vma=False
+    )

time: 690 us -> 546 us (0.79)
  the two profiles are of different devices: /device:TPU:65 before, /device:TPU:1 now
where the time goes in v1:
time: 546 us; the launch traced here: 536 us
  waiting for transfers between devices  212 us (39%)
  matrix products  104 us (19%)
  local copies, waits for them, and re-layouts  83.3 us (15%)
  blocking collectives  56.2 us (10%)
  other arithmetic  44.5 us (8%)
  between operations  14.7 us (3%)
  loops' own time  11.4 us (2%)
  starting transfers between devices  9.8 us (2%)
    reduce_scatter x2, waiting for transfers between devices, scatter_rows(): part = lax.psum_scatter(split, 'y', scatter_dimension=1, tiled=False)  82.4 us
    reduce_scatter x2, waiting for transfers between devices, scatter_rows(): return lax.psum_scatter(part, 'zh', scatter_dimension=0, tiled=False)  74.8 us
    dot_general x17, matrix products, absorb(): jnp.einsum('rhgik,rkhd->rhgid', weights.astype(jnp.bfloat16), value_block...  57.5 us
    all_gather x2, waiting for transfers between devices, gather_rows(): both = lax.all_gather(across, 'y', axis=0, tiled=False)  54.9 us
    all_gather x2, blocking collectives, gather_rows(): across = lax.all_gather(piece, 'zh', axis=0, tiled=False)  36.8 us
    dot_general x17, matrix products, absorb(): jnp.einsum('irhgd,rkhd->rhgik', queries, key_block, preferred_element_typ...  26.2 us
    unnamed x1, blocking collectives  19.4 us
    reduce_sum x17, other arithmetic, absorb(): jnp.sum(weights, axis=-1)  18.8 us
  transfers between devices with their start and end apart: 7, of which 6 were waited for; matrix products, arithmetic and copies ran while one was open for 19% of the time, Pallas kernels for 0%

profile of v1, /device:TPU:1, one launch (start us, length us, event | category | flops | bytes accessed | tf_op | source)
XLA Modules:
  0.0 536.2 jit_solution(1385479520854756767)
XLA Ops:
  9.1 17.8 %all-gather = bf16[128,2,1536]{2,0,1:T(8,128)(2,1)} all-gather(bf16[64,2,1536]{2,0,1:T(8,128)(2,1)S(1)} %fusion.67), channel_id=2, replica_groups=mesh['dp'=32,'zh'=2,'y'=4] {'zh'}, dimensions={0}, use_global_device_ids=true | all-gather | bytes 1179648 | tf_op jit(solution)/shard_map/all_gather | solution.py:90
  28.4 19.4 %all-reduce = s32[64]{0:T(128)S(1)} all-reduce(s32[64]{0:T(128)S(1)} %dynamic-update-slice), channel_id=1, replica_groups=mesh['dp'=32,'zh'=2,'y'=4] {'dp'}, use_global_device_ids=true, to_apply=%add | all-reduce | flops 64 | bytes 512
  55.2 9.6 %all-to-all-start = ((bf16[32,2,2,128,96]{3,4,1,2,0:T(8,128)(2,1)}), bf16[32,2,2,128,96]{3,4,1,2,0:T(8,128)(2,1)}, u32[]{:S(2)}, u32[]{:S(2)}) async-start(bf16[32,2,2,128,96]{3,4,1,2,0:T(8,128)(2,1)} %copy.75), calls=%async_computation | async-start | bytes 6291456 | tf_op jit(solution)/shard_map/all_to_all | solution.py:111
  66.3 12.4 %all-gather.7.cloned.1.call-done = bf16[8,64,2,1536]{3,1,0,2:T(8,128)(2,1)} async-done(((bf16[2,64,2,1536]{3,1,0,2:T(8,128)(2,1)}), bf16[8,64,2,1536]{3,1,0,2:T(8,128)(2,1)}) %all-gather.7.cloned.1.call-update) | async-done | bytes 3145744 | tf_op jit(solution)/shard_map/all_gather | solution.py:91
  81.6 5.0 copy.71
  92.6 8.0 %reshape_reshape.8 = bf16[1024,1536]{1,0:T(8,128)(2,1)} reshape(bf16[2,4,64,2,1536]{4,3,2,1,0:T(2,128)(2,1)} %copy.71) | data formatting | bytes 6291456 | tf_op jit(solution)/shard_map/reshape;reshape | solution.py:150
  109.5 66.7 %while.32 = (s32[]{:T(128)}, f32[2,1,2,512]{3,2,0,1:T(2,128)S(1)}, f32[2,1,2,512]{3,2,0,1:T(2,128)S(1)}, f32[2,1,2,512,96]{3,4,2,0,1:T(8,128)}, s32[8]{0:T(128)S...) while((s32[]{:T(128)}, f32[2,1,2,512]{3,2,0,1:T(2,128)S(1)}, ...), condition=%wide.region_6.7_spmd.clone.clone, body=%wide.region_3.6_spmd.clone.clone.sunk | while | flops 415374848 | bytes 17703132 | solution.py:207
  176.2 5.6 %copy.76 = bf16[2,2,32,128,96]{3,2,4,1,0:T(8,128)(2,1)} copy(bf16[2,2,32,128,96]{3,4,0,1,2:T(8,128)(2,1)} %bitcast.36) | data formatting | bytes 6291456 | tf_op jit(solution)/shard_map/transpose | solution.py:114
  181.8 5.8 %reshape.416 = bf16[2,2,4096,96]{2,3,1,0:T(8,128)(2,1)} reshape(bf16[2,2,32,128,96]{3,2,4,1,0:T(8,128)(2,1)} %copy.76) | data formatting | bytes 6291456 | tf_op jit(solution)/shard_map/reshape | solution.py:115
  191.4 68.6 %while.31 = (s32[]{:T(128)}, f32[2,1,2,512]{3,2,0,1:T(2,128)S(1)}, f32[2,1,2,512]{3,2,0,1:T(2,128)S(1)}, f32[2,1,2,512,96]{3,4,2,0,1:T(8,128)}, s32[8]{0:T(128)}...) while((s32[]{:T(128)}, f32[2,1,2,512]{3,2,0,1:T(2,128)S(1)}, ...), condition=%wide.region_10.11_spmd.clone, body=%wide.region_7.10_spmd.clone.sunk | while | flops 415639040 | bytes 17183952 | solution.py:86
  204.2 3.5 fusion.127
  255.5 3.5 fusion.127
  265.3 41.2 %reduce-scatter.5.cloned.1.call-done = bf16[2,1,64,2,1536]{4,2,3,0,1:T(8,128)(2,1)} async-done(((bf16[2,4,64,2,1536]{4,2,3,0,1:T(8,128)(2,1)}), bf16[2,1,64,2,1536]{4,2,3,0,1:T(8,128)(2,1)}) %reduce-scatter.5.cloned.1.call-update) | async-done | bytes 786448 | tf_op jit(solution)/shard_map/reduce_scatter | solution.py:101
  306.6 37.4 %reduce-scatter.7.cloned.1.call-done = bf16[1,64,2,1536]{3,1,2,0:T(8,128)(2,1)} async-done(((bf16[2,64,2,1536]{3,1,2,0:T(8,128)(2,1)}), bf16[1,64,2,1536]{3,1,2,0:T(8,128)(2,1)}) %reduce-scatter.7.cloned.1.call-update) | async-done | bytes 393232 | tf_op jit(solution)/shard_map/reduce_scatter | solution.py:102
  346.3 19.0 %all-gather.2 = bf16[128,2,1536]{2,0,1:T(8,128)(2,1)S(1)} all-gather(bf16[64,2,1536]{2,0,1:T(8,128)(2,1)S(1)} %fusion.71), channel_id=4, replica_groups=mesh['dp'=32,'zh'=2,'y'=4] {'zh'}, dimensions={0}, use_global_device_ids=true | all-gather | bytes 1179648 | tf_op jit(solution)/shard_map/all_gather | solution.py:90
  366.3 42.5 %all-gather.9.cloned.1.call-done = bf16[8,64,2,1536]{3,1,2,0:T(8,128)(2,1)} async-done(((bf16[2,64,2,1536]{3,1,2,0:T(8,128)(2,1)}), bf16[8,64,2,1536]{3,1,2,0:T(8,128)(2,1)}) %all-gather.9.cloned.1.call-update) | async-done | bytes 3145744 | tf_op jit(solution)/shard_map/all_gather | solution.py:91
  408.8 6.8 %copy.79 = bf16[2,4,64,2,1536]{4,3,2,1,0:T(2,128)(2,1)} copy(bf16[2,4,64,2,1536]{4,2,3,0,1:T(8,128)(2,1)} %bitcast.297) | data formatting | bytes 6291456 | tf_op jit(solution)/shard_map/transpose | solution.py:92
  415.6 7.8 %reshape_reshape.9 = bf16[1024,1536]{1,0:T(8,128)(2,1)} reshape(bf16[2,4,64,2,1536]{4,3,2,1,0:T(2,128)(2,1)} %copy.79) | data formatting | bytes 6291456 | tf_op jit(solution)/shard_map/reshape;reshape | solution.py:235
  423.5 5.0 fusion.98
  428.5 8.2 %convolution_convert_fusion.1 = bf16[1024,1536]{1,0:T(8,128)(2,1)} fusion(bf16[512,1536]{1,0:T(8,128)(2,1)S(1)} %copy-done, f32[1024,512]{1,0:T(8,128)} %fusion.98, bf16[1024,1536]{1,0:T(8,128)(2,1)} %reshape_reshape.9, bf16[1536,512]{1,0:T(8,128)(2,1)} %param.34), kind=kOutput, calls=%fused_computation.63 | convolution fusion | flops 3225944064 | bytes 11534336 | tf_op jit(solution)/shard_map/dot_general | solution.py:245
  436.7 7.2 %convert_element_type.95 = bf16[2,4,64,2,1536]{4,3,2,1,0:T(2,128)(2,1)} reshape(bf16[1024,1536]{1,0:T(8,128)(2,1)} %convolution_convert_fusion.1) | data formatting | bytes 6291456 | tf_op jit(solution)/shard_map/convert_element_type | solution.py:251
  443.9 4.2 copy.80
  448.2 41.2 %reduce-scatter.9.cloned.1.call-done = bf16[2,1,64,2,1536]{4,2,3,0,1:T(8,128)(2,1)} async-done(((bf16[2,4,64,2,1536]{4,2,3,0,1:T(8,128)(2,1)}), bf16[2,1,64,2,1536]{4,2,3,0,1:T(8,128)(2,1)}) %reduce-scatter.9.cloned.1.call-update) | async-done | bytes 786448 | tf_op jit(solution)/shard_map/reduce_scatter | solution.py:101
  489.4 37.4 %reduce-scatter.11.cloned.1.call-done = bf16[1,64,2,1536]{3,1,2,0:T(8,128)(2,1)} async-done(((bf16[2,64,2,1536]{3,1,2,0:T(8,128)(2,1)}), bf16[1,64,2,1536]{3,1,2,0:T(8,128)(2,1)}) %reduce-scatter.11.cloned.1.call-update) | async-done | bytes 393232 | tf_op jit(solution)/shard_map/reduce_scatter | solution.py:102
  (273 shorter events, 161.8 us)
Async XLA Ops:
  6.5 421.9 %copy-start = (bf16[512,1536]{1,0:T(8,128)(2,1)S(1)}, bf16[512,1536]{1,0:T(8,128)(2,1)}, u32[]{:S(2)}) copy-start(bf16[512,1536]{1,0:T(8,128)(2,1)} %param.35) | copy-start | bytes 4718596
  6.5 20.4 %copy-start.15 = (u32[256]{0:T(256)S(1)}, u32[256]{0:T(256)}, u32[]{:S(2)}) copy-start(u32[256]{0:T(256)} %constant.93) | copy-start | bytes 3076
  6.5 21.6 %copy-start.13 = (s32[2]{0:T(128)S(1)}, s32[2]{0:T(128)}, u32[]{:S(2)}) copy-start(s32[2]{0:T(128)} %param.22) | copy-start | bytes 28
  6.5 41.6 %copy-start.8 = (bf16[8,128,96]{1,2,0:T(8,128)(2,1)S(1)}, bf16[8,128,96]{1,2,0:T(8,128)(2,1)}, u32[]{:S(2)}) copy-start(bf16[8,128,96]{1,2,0:T(8,128)(2,1)} %param.30) | copy-start | bytes 589828
  6.5 41.6 %copy-start.7 = (bf16[8,128,96]{1,2,0:T(8,128)(2,1)S(1)}, bf16[8,128,96]{1,2,0:T(8,128)(2,1)}, u32[]{:S(2)}) copy-start(bf16[8,128,96]{1,2,0:T(8,128)(2,1)} %param.31) | copy-start | bytes 589828
  6.5 72.2 %all-gather.7.cloned.1.call-start = ((), (), s32[]{:S(2)}) async-start(), calls=%async_computation.9 | async-start | bytes 3932160 | tf_op jit(solution)/shard_map/all_gather | solution.py:91
  55.2 9.7 %copy-start.14 = (s32[2]{0:T(128)S(1)}, s32[2]{0:T(128)}, u32[]{:S(2)}) copy-start(s32[2]{0:T(128)} %param.21) | copy-start | bytes 28
  55.2 121.0 %all-to-all-start = ((bf16[32,2,2,128,96]{3,4,1,2,0:T(8,128)(2,1)}), bf16[32,2,2,128,96]{3,4,1,2,0:T(8,128)(2,1)}, u32[]{:S(2)}, u32[]{:S(2)}) async-start(bf16[32,2,2,128,96]{3,4,1,2,0:T(8,128)(2,1)} %copy.75), calls=%async_computation | async-start | bytes 6291456 | tf_op jit(solution)/shard_map/all_to_all | solution.py:111
  64.8 241.7 %reduce-scatter.5.cloned.1.call-start = ((), (), s32[]{:S(2)}) async-start(), calls=%async_computation.5 | async-start | bytes 3932160 | tf_op jit(solution)/shard_map/reduce_scatter | solution.py:101
  64.9 0.5 copy-start.9
  78.7 2.8 copy-start.1
  81.5 5.0 copy-start.5
  86.5 1.9 copy-start.12
  92.6 8.0 %copy-start.6 = (bf16[1536,96]{0,1:T(8,128)(2,1)S(1)}, bf16[1536,96]{0,1:T(8,128)(2,1)}, u32[]{:S(2)}) copy-start(bf16[1536,96]{0,1:T(8,128)(2,1)} %param.26) | copy-start | bytes 884740
  103.8 3.5 copy-start.3
  265.2 78.7 %copy-start.2 = (bf16[64,2,1536]{2,1,0:T(2,128)(2,1)S(1)}, bf16[64,2,1536]{2,1,0:T(2,128)(2,1)}, u32[]{:S(2)}) copy-start(bf16[64,2,1536]{2,1,0:T(2,128)(2,1)} %param.20) | copy-start | bytes 1179652
  265.2 79.9 %copy-start.10 = (f32[1536]{0:T(1024)S(1)}, f32[1536]{0:T(1024)}, u32[]{:S(2)}) copy-start(f32[1536]{0:T(1024)} %param.32) | copy-start | bytes 18436
  265.3 78.7 %reduce-scatter.7.cloned.1.call-start = ((), (), s32[]{:S(2)}) async-start(), calls=%async_computation.6 | async-start | bytes 1179648 | tf_op jit(solution)/shard_map/reduce_scatter | solution.py:102
  306.5 102.3 %all-gather.9.cloned.1.call-start = ((), (), s32[]{:S(2)}) async-start(), calls=%async_computation.10 | async-start | bytes 3932160 | tf_op jit(solution)/shard_map/all_gather | solution.py:91
  366.3 123.1 %reduce-scatter.9.cloned.1.call-start = ((), (), s32[]{:S(2)}) async-start(), calls=%async_computation.7 | async-start | bytes 3932160 | tf_op jit(solution)/shard_map/reduce_scatter | solution.py:101
  415.6 7.8 %copy-start.11 = (bf16[1536,512]{1,0:T(8,128)(2,1)S(1)}, bf16[1536,512]{1,0:T(8,128)(2,1)}, u32[]{:S(2)}) copy-start(bf16[1536,512]{1,0:T(8,128)(2,1)} %param.33) | copy-start | bytes 4718596
  448.1 78.7 %copy-start.4 = (bf16[1,64,2,1536]{3,1,2,0:T(8,128)(2,1)S(1)}, bf16[1,64,2,1536]{3,1,2,0:T(8,128)(2,1)}, u32[]{:S(2)}) copy-start(bf16[1,64,2,1536]{3,1,2,0:T(8,128)(2,1)} %reduce-scatter.7.cloned.1.call-done) | copy-start | bytes 1179652
  448.2 78.7 %reduce-scatter.11.cloned.1.call-start = ((), (), s32[]{:S(2)}) async-start(), calls=%async_computation.8 | async-start | bytes 1179648 | tf_op jit(solution)/shard_map/reduce_scatter | solution.py:102
Sparse Core Ops, SparseCore 0:
  27.0 51.6 all-gather.6
  265.4 41.0 reduce-scatter.4
  309.0 34.8 reduce-scatter.6
  366.4 42.3 all-gather.8
  448.3 41.0 reduce-scatter.8
  491.9 34.9 reduce-scatter.10

commit v2 on v1

--- a/solution.py
+++ b/solution.py
@@ -4,6 +4,8 @@
 import jax.numpy as jnp
 from jax import lax
 from jax.sharding import PartitionSpec as P
+from jax.experimental import pallas as pl
+from jax.experimental.pallas import tpu as pltpu
 
 MODEL_WIDTH = 1536
 HEAD_SIZE = 96
@@ -41,49 +43,117 @@
     )
 
 
-def absorb(soft_state, queries, key_block, value_block, visible, score_scale):
-    row_peak, row_sum, accumulated = soft_state
-    scores = (
-        jnp.einsum("irhgd,rkhd->rhgik", queries, key_block, preferred_element_type=jnp.float32)
-        * score_scale
-    )
-    scores = jnp.where(visible[:, None, None], scores, -jnp.inf)
-    new_peak = jnp.maximum(row_peak, jnp.max(scores, axis=-1))
-    factor = jnp.exp(row_peak - new_peak)
-    weights = jnp.exp(scores - new_peak[..., None])
-    blended = jnp.einsum(
-        "rhgik,rkhd->rhgid",
-        weights.astype(jnp.bfloat16),
-        value_block,
-        preferred_element_type=jnp.float32,
-    )
-    return (
-        new_peak,
-        row_sum * factor + jnp.sum(weights, axis=-1),
-        accumulated * factor[..., None] + blended,
-    )
-
-
-def shared_block(soft_state, pieces, queries, selector, horizon, score_scale):
-    key_piece, value_piece = pieces
-    row_count = key_piece.shape[1]
-    key_heads = key_piece.shape[2] // HEAD_SIZE
-    local_reqs = queries.shape[1]
-    picked_keys = key_piece.reshape(local_reqs, row_count, key_heads, HEAD_SIZE)
-    picked_values = value_piece.reshape(local_reqs, row_count, key_heads, HEAD_SIZE)
-    block_len = math.gcd(row_count, FRESH_TOKENS)
-
-    def block_step(running, block_index):
-        block_start = block_index * block_len
-        key_block = lax.dynamic_slice_in_dim(picked_keys, block_start, block_len, 1)
-        value_block = lax.dynamic_slice_in_dim(picked_values, block_start, block_len, 1)
-        prompt_pos = block_start + jnp.arange(block_len, dtype=jnp.int32)
-        visible = (prompt_pos[None, None, :] < SINKS) | (
-            prompt_pos[None, None, :] > horizon[:, :, None]
+KEY_BLOCK = 512
+
+
+def attention_kernel(
+    length_ref, q_ref, pk_ref, pv_ref, wk_ref, wv_ref, nk_ref, nv_ref, o_ref, peak, total, acc
+):
+    request = pl.program_id(0)
+    block = pl.program_id(1)
+    length = length_ref[request]
+    prompt_blocks = PROMPT_TOKENS // KEY_BLOCK
+    window_blocks = WINDOW_SPAN // KEY_BLOCK
+    row_count = q_ref.shape[1]
+    score_scale = 1.0 / math.sqrt(HEAD_SIZE)
+
+    @pl.when(block == 0)
+    def _():
+        peak[...] = jnp.full(peak.shape, far_below, jnp.float32)
+        total[...] = jnp.zeros(total.shape, jnp.float32)
+        acc[...] = jnp.zeros(acc.shape, jnp.float32)
+
+    rows = lax.rem(lax.broadcasted_iota(jnp.int32, (row_count, KEY_BLOCK), 0), FRESH_TOKENS)
+    cols = lax.broadcasted_iota(jnp.int32, (row_count, KEY_BLOCK), 1)
+
+    def absorb(k_ref, v_ref, visible):
+        scores = (
+            lax.dot_general(
+                q_ref[0],
+                k_ref[0],
+                (((1,), (1,)), ((), ())),
+                preferred_element_type=jnp.float32,
+            )
+            * score_scale
         )
-        return (absorb(running, queries, key_block, value_block, visible, score_scale), None)
-
-    return lax.scan(block_step, soft_state, jnp.arange(row_count // block_len, dtype=jnp.int32))[0]
+        scores = jnp.where(visible, scores, -jnp.inf)
+        old_peak = peak[...]
+        new_peak = jnp.maximum(old_peak, jnp.max(scores, axis=-1, keepdims=True))
+        factor = jnp.exp(old_peak - new_peak)
+        weights = jnp.exp(scores - new_peak)
+        total[...] = total[...] * factor + jnp.sum(weights, axis=-1, keepdims=True)
+        acc[...] = acc[...] * factor + jnp.dot(
+            weights.astype(jnp.bfloat16), v_ref[0], preferred_element_type=jnp.float32
+        )
+        peak[...] = new_peak
+
+    prompt_start = block * KEY_BLOCK
+
+    @pl.when(
+        (block < prompt_blocks)
+        & ((block == 0) | (prompt_start + KEY_BLOCK - 1 > length))
+    )
+    def _():
+        spot = prompt_start + cols
+        absorb(pk_ref, pv_ref, (spot < SINKS) | (spot > length + rows))
+
+    window_start = (block - prompt_blocks) * KEY_BLOCK
+
+    @pl.when(
+        (block >= prompt_blocks)
+        & (block < prompt_blocks + window_blocks)
+        & (window_start + KEY_BLOCK - 1 >= WINDOW_SPAN - length)
+    )
+    def _():
+        slot = window_start + cols
+        absorb(wk_ref, wv_ref, (slot >= WINDOW_SPAN - length) & (slot > rows))
+
+    @pl.when(block == prompt_blocks + window_blocks)
+    def _():
+        absorb(nk_ref, nv_ref, cols <= rows)
+        o_ref[0] = (acc[...] / total[...]).astype(o_ref.dtype)
+
+
+def attention(lengths, queries, prompt_k, prompt_v, window_k, window_v, new_k, new_v):
+    local_reqs, row_count, width = queries.shape
+    prompt_blocks = PROMPT_TOKENS // KEY_BLOCK
+    window_blocks = WINDOW_SPAN // KEY_BLOCK
+    steps = prompt_blocks + window_blocks + 1
+    key_spec = lambda pick: pl.BlockSpec((1, KEY_BLOCK, width), pick)
+    prompt_pick = lambda r, b, lens: (r, jnp.minimum(b, prompt_blocks - 1), 0)
+    window_pick = lambda r, b, lens: (r, jnp.clip(b - prompt_blocks, 0, window_blocks - 1), 0)
+    fixed_pick = lambda r, b, lens: (r, 0, 0)
+    grid_spec = pltpu.PrefetchScalarGridSpec(
+        num_scalar_prefetch=1,
+        grid=(local_reqs, steps),
+        in_specs=[
+            pl.BlockSpec((1, row_count, width), fixed_pick),
+            key_spec(prompt_pick),
+            key_spec(prompt_pick),
+            key_spec(window_pick),
+            key_spec(window_pick),
+            key_spec(fixed_pick),
+            key_spec(fixed_pick),
+        ],
+        out_specs=pl.BlockSpec((1, row_count, width), fixed_pick),
+        scratch_shapes=[
+            pltpu.VMEM((row_count, 1), jnp.float32),
+            pltpu.VMEM((row_count, 1), jnp.float32),
+            pltpu.VMEM((row_count, width), jnp.float32),
+        ],
+    )
+    keys_total = PROMPT_TOKENS + WINDOW_SPAN + FRESH_TOKENS
+    flops = 4 * local_reqs * row_count * keys_total * width
+    return pl.pallas_call(
+        attention_kernel,
+        grid_spec=grid_spec,
+        out_shape=jax.ShapeDtypeStruct(queries.shape, jnp.bfloat16),
+        cost_estimate=pl.CostEstimate(
+            flops=flops,
+            transcendentals=local_reqs * row_count * keys_total,
+            bytes_accessed=4 * local_reqs * keys_total * width * 2,
+        ),
+    )(lengths, queries, prompt_k, prompt_v, window_k, window_v, new_k, new_v)
 
 
 def gather_rows(piece):
@@ -103,9 +173,10 @@
 
 
 def prompt_for_requests(prompt_keys, prompt_values, prompt_group):
-    every_group = lax.all_gather(prompt_group, "dp", axis=0, tiled=True)
     dp_size = lax.axis_size("dp")
-    wanted = every_group.reshape(dp_size, -1)
+    wanted = lax.all_to_all(
+        jnp.broadcast_to(prompt_group[None], (dp_size,) + prompt_group.shape), "dp", 0, 0, tiled=False
+    )
     both = jnp.stack([prompt_keys, prompt_values], axis=1)
     outgoing = jnp.take(both, wanted, axis=0)
     incoming = lax.all_to_all(outgoing, "dp", 0, 0, tiled=False)
@@ -170,55 +241,23 @@
     fresh_keys = (
         rotate(fresh_keys, positions).astype(jnp.bfloat16).reshape(row_count, local_reqs, key_cols)
     )
-    gathered = jnp.concatenate([project_queries, fresh_keys, fresh_values], axis=2)
-    queries = gathered[:, :, offset : offset + query_cols].reshape(
-        FRESH_TOKENS, local_reqs, key_heads, query_group_width, HEAD_SIZE
-    )
-    own_keys = jnp.swapaxes(
-        gathered[:, :, offset + query_cols : offset + query_cols + key_cols], 0, 1
-    ).reshape(local_reqs, FRESH_TOKENS, key_heads, HEAD_SIZE)
-    own_values = jnp.swapaxes(
-        gathered[:, :, offset + query_cols + key_cols : offset + query_cols + 2 * key_cols], 0, 1
-    ).reshape(local_reqs, FRESH_TOKENS, key_heads, HEAD_SIZE)
-    state_shape = (local_reqs, key_heads, query_group_width, FRESH_TOKENS)
-    soft_state = (
-        jnp.full(state_shape, far_below, jnp.float32),
-        jnp.zeros(state_shape, jnp.float32),
-        jnp.zeros(state_shape + (HEAD_SIZE,), jnp.float32),
-    )
-    row_ids = jnp.arange(FRESH_TOKENS, dtype=jnp.int32)
-    causal = jnp.broadcast_to(
-        row_ids[None, None, :] <= row_ids[None, :, None], (local_reqs, FRESH_TOKENS, FRESH_TOKENS)
-    )
-    soft_state = absorb(soft_state, queries, own_keys, own_values, causal, score_scale)
-    past_keys = window_cache_keys.reshape(local_reqs, WINDOW_SPAN, key_heads, HEAD_SIZE)
-    past_values = window_cache_values.reshape(local_reqs, WINDOW_SPAN, key_heads, HEAD_SIZE)
-
-    def window_step(running, block_index):
-        block_start = block_index * FRESH_TOKENS
-        key_block = lax.dynamic_slice_in_dim(past_keys, block_start, FRESH_TOKENS, 1)
-        value_block = lax.dynamic_slice_in_dim(past_values, block_start, FRESH_TOKENS, 1)
-        slot_ids = block_start + row_ids
-        visible = (slot_ids[None, None, :] >= WINDOW_SPAN - cached_len[:, None, None]) & (
-            slot_ids[None, None, :] > row_ids[None, :, None]
-        )
-        return (absorb(running, queries, key_block, value_block, visible, score_scale), None)
-
-    soft_state = lax.scan(
-        window_step, soft_state, jnp.arange(WINDOW_SPAN // FRESH_TOKENS, dtype=jnp.int32)
-    )[0]
-    horizon = PROMPT_TOKENS + cached_len[:, None] + row_ids[None, :] - WINDOW_SPAN
-    soft_state = shared_block(
-        soft_state,
-        prompt_for_requests(prompt_keys, prompt_values, prompt_group),
-        queries,
-        prompt_group,
-        horizon,
-        score_scale,
-    )
-    row_peak, row_sum, accumulated = soft_state
-    attended = (accumulated / row_sum[..., None]).astype(jnp.bfloat16)
-    attended = attended.transpose(3, 0, 1, 2, 4).reshape(FRESH_TOKENS, local_reqs, query_cols)
+    query_heads = query_cols // HEAD_SIZE
+    queries = (
+        project_queries.reshape(row_count, local_reqs, query_heads, HEAD_SIZE)
+        .transpose(1, 2, 0, 3)
+        .reshape(local_reqs, query_heads * row_count, HEAD_SIZE)
+    )
+    own_keys = jnp.swapaxes(fresh_keys, 0, 1)
+    own_values = jnp.swapaxes(fresh_values, 0, 1)
+    prompt_k, prompt_v = prompt_for_requests(prompt_keys, prompt_values, prompt_group)
+    attended = attention(
+        cached_len, queries, prompt_k, prompt_v, window_cache_keys, window_cache_values, own_keys, own_values
+    )
+    attended = (
+        attended.reshape(local_reqs, query_heads, row_count, HEAD_SIZE)
+        .transpose(2, 0, 1, 3)
+        .reshape(row_count, local_reqs, query_cols)
+    )
     picked = attended
     attn_part = scatter_rows(
         jnp.dot(

time: 546 us -> 496 us (0.908)
  the two profiles are of different devices: /device:TPU:1 before, /device:TPU:65 now
where the time goes in v2:
time: 496 us; the launch traced here: 491 us
  waiting for transfers between devices  241 us (49%)
  Pallas kernels  70.8 us (14%)
  local copies, waits for them, and re-layouts  68 us (14%)
  blocking collectives  46.5 us (9%)
  matrix products  21.3 us (4%)
  starting transfers between devices  15.3 us (3%)
  other arithmetic  14.4 us (3%)
  between operations  13.7 us (3%)
    reduce_scatter x2, waiting for transfers between devices, scatter_rows(): part = lax.psum_scatter(split, 'y', scatter_dimension=1, tiled=False)  90.5 us
    pallas_call x1, Pallas kernels, attention(): pl.pallas_call(attention_kernel, grid_spec=grid_spec, out_shape=jax.Shape...  70.8 us
    reduce_scatter x2, waiting for transfers between devices, scatter_rows(): return lax.psum_scatter(part, 'zh', scatter_dimension=0, tiled=False)  70.3 us
    all_gather x2, waiting for transfers between devices, gather_rows(): both = lax.all_gather(across, 'y', axis=0, tiled=False)  50.1 us
    all_gather x2, blocking collectives, gather_rows(): across = lax.all_gather(piece, 'zh', axis=0, tiled=False)  46.5 us
    all_to_all x1, waiting for transfers between devices, prompt_for_requests(): incoming = lax.all_to_all(outgoing, 'dp', 0, 0, tiled=False)  24.9 us
    transpose x3, local copies, waits for them, and re-layouts, gather_rows(): both = jnp.swapaxes(both, 0, 1)  14 us
    convert_element_type x2, local copies, waits for them, and re-layouts, body(): mlp_part = scatter_rows(jnp.dot(picked.reshape(FRESH_TOKENS * local_reqs,...  11.4 us
  transfers between devices with their start and end apart: 8, of which 8 were waited for; matrix products, arithmetic and copies ran while one was open for 8% of the time, Pallas kernels for 0%

profile of v2, /device:TPU:65, one launch (start us, length us, event | category | flops | bytes accessed | tf_op | source)
XLA Modules:
  0.0 491.0 jit_solution(9620060066050498481)
XLA Ops:
  9.1 23.5 %all-gather = bf16[128,2,1536]{2,0,1:T(8,128)(2,1)} all-gather(bf16[64,2,1536]{2,0,1:T(8,128)(2,1)S(1)} %fusion.2), channel_id=2, replica_groups=mesh['dp'=32,'zh'=2,'y'=4] {'zh'}, dimensions={0}, use_global_device_ids=true | all-gather | bytes 1179648 | tf_op jit(solution)/shard_map/all_gather | solution.py:160
  33.2 7.7 %all-to-all-start = ((s32[32,1,2]{2,1,0:T(1,128)}), s32[32,1,2]{2,1,0:T(1,128)S(1)}, u32[]{:S(2)}, u32[]{:S(2)}) async-start(s32[32,1,2]{2,1,0:T(1,128)} %broadcast_in_dim.9), calls=%async_computation | async-start | bytes 32768 | tf_op jit(solution)/shard_map/all_to_all | solution.py:177
  41.0 5.1 %all-to-all-done = s32[32,1,2]{2,1,0:T(1,128)S(1)} async-done(((s32[32,1,2]{2,1,0:T(1,128)}), s32[32,1,2]{2,1,0:T(1,128)S(1)}, u32[]{:S(2)}, u32[]{:S(2)}) %all-to-all-start) | async-done | bytes 288 | tf_op jit(solution)/shard_map/all_to_all | solution.py:177
  49.1 4.1 broadcast_select_fusion
  53.2 7.2 %all-to-all-start.1 = ((bf16[32,2,2,128,96]{3,4,2,1,0:T(8,128)(2,1)}), bf16[32,2,2,128,96]{3,4,2,1,0:T(8,128)(2,1)}, u32[]{:S(2)}, u32[]{:S(2)}) async-start(bf16[32,2,2,128,96]{3,4,2,1,0:T(8,128)(2,1)} %broadcast_select_fusion), calls=%async_computation.1 | async-start | bytes 6291456 | tf_op jit(solution)/shard_map/all_to_all | solution.py:182
  67.8 9.3 %all-gather.7.cloned.1.call-done = bf16[8,64,2,1536]{3,1,0,2:T(8,128)(2,1)} async-done(((bf16[2,64,2,1536]{3,1,0,2:T(8,128)(2,1)}), bf16[8,64,2,1536]{3,1,0,2:T(8,128)(2,1)}) %all-gather.7.cloned.1.call-update) | async-done | bytes 3145744 | tf_op jit(solution)/shard_map/all_gather | solution.py:161
  80.0 4.9 copy.67
  87.2 7.5 %reshape_reshape.7 = bf16[1024,1536]{1,0:T(8,128)(2,1)} reshape(bf16[2,4,64,2,1536]{4,3,2,1,0:T(2,128)(2,1)} %copy.67) | data formatting | bytes 6291456 | tf_op jit(solution)/shard_map/reshape;reshape | solution.py:221
  104.1 24.9 %all-to-all-done.1 = bf16[32,2,2,128,96]{3,4,2,1,0:T(8,128)(2,1)} async-done(((bf16[32,2,2,128,96]{3,4,2,1,0:T(8,128)(2,1)}), bf16[32,2,2,128,96]{3,4,2,1,0:T(8,128)(2,1)}, u32[]{:S(2)}, u32[]{:S(2)}) %all-to-all-start.1) | async-done | bytes 3145760 | tf_op jit(solution)/shard_map/all_to_all | solution.py:182
  129.0 6.1 %copy.65 = bf16[2,2,32,128,96]{4,3,2,0,1:T(8,128)(2,1)} copy(bf16[2,2,32,128,96]{3,4,1,0,2:T(8,128)(2,1)} %bitcast.17) | data formatting | bytes 6291456 | tf_op jit(solution)/shard_map/transpose | solution.py:185
  135.1 4.5 slice_bitcast_fusion
  139.6 70.8 %shard_map.154 = bf16[2,1024,96]{2,1,0:T(8,128)(2,1)} custom-call(s32[2]{0:T(128)} %length_ref.1, bf16[2,1024,96]{2,1,0:T(8,128)(2,1)} %bitcast.99, bf16[2,4096,96]{2,1,0:T(8,128)(2,1)} %get-tuple-element.6.pk_ref, bf16[2,4096,96]{2,1,0:T(8,128)(2,1)} %get-tuple-element.5.pv_ref, bf16[2,4096,96]{2,1,0:T(8,128)(2,1)} %copy.70.wk_ref, ...), custom_call_target="tpu_custom_call" | custom-call | flops 6845104128 | bytes 13369344 | tf_op jit(solution)/shard_map/pallas_call | solution.py:147
  214.7 49.4 %reduce-scatter.5.cloned.1.call-done = bf16[2,1,64,2,1536]{4,2,3,0,1:T(8,128)(2,1)} async-done(((bf16[2,4,64,2,1536]{4,2,3,0,1:T(8,128)(2,1)}), bf16[2,1,64,2,1536]{4,2,3,0,1:T(8,128)(2,1)}) %reduce-scatter.5.cloned.1.call-update) | async-done | bytes 786448 | tf_op jit(solution)/shard_map/reduce_scatter | solution.py:171
  264.1 35.1 %reduce-scatter.7.cloned.1.call-done = bf16[1,64,2,1536]{3,1,2,0:T(8,128)(2,1)} async-done(((bf16[2,64,2,1536]{3,1,2,0:T(8,128)(2,1)}), bf16[1,64,2,1536]{3,1,2,0:T(8,128)(2,1)}) %reduce-scatter.7.cloned.1.call-update) | async-done | bytes 393232 | tf_op jit(solution)/shard_map/reduce_scatter | solution.py:172
  301.5 22.9 %all-gather.2 = bf16[128,2,1536]{2,0,1:T(8,128)(2,1)S(1)} all-gather(bf16[64,2,1536]{2,0,1:T(8,128)(2,1)S(1)} %fusion.6), channel_id=4, replica_groups=mesh['dp'=32,'zh'=2,'y'=4] {'zh'}, dimensions={0}, use_global_device_ids=true | all-gather | bytes 1179648 | tf_op jit(solution)/shard_map/all_gather | solution.py:160
  325.5 40.8 %all-gather.9.cloned.1.call-done = bf16[8,64,2,1536]{3,1,2,0:T(8,128)(2,1)} async-done(((bf16[2,64,2,1536]{3,1,2,0:T(8,128)(2,1)}), bf16[8,64,2,1536]{3,1,2,0:T(8,128)(2,1)}) %all-gather.9.cloned.1.call-update) | async-done | bytes 3145744 | tf_op jit(solution)/shard_map/all_gather | solution.py:161
  366.3 6.8 %copy.75 = bf16[2,4,64,2,1536]{4,3,2,1,0:T(2,128)(2,1)} copy(bf16[2,4,64,2,1536]{4,2,3,0,1:T(8,128)(2,1)} %bitcast.93) | data formatting | bytes 6291456 | tf_op jit(solution)/shard_map/transpose | solution.py:162
  373.1 7.6 %reshape_reshape.8 = bf16[1024,1536]{1,0:T(8,128)(2,1)} reshape(bf16[2,4,64,2,1536]{4,3,2,1,0:T(2,128)(2,1)} %copy.75) | data formatting | bytes 6291456 | tf_op jit(solution)/shard_map/reshape;reshape | solution.py:274
  380.7 5.1 %fusion.22 = f32[1024,512]{1,0:T(8,128)} fusion(bf16[1024,1536]{1,0:T(8,128)(2,1)} %reshape_reshape.8, bf16[1536,512]{1,0:T(8,128)(2,1)S(1)} %copy-done.13), kind=kOutput, calls=%fused_computation.56 | convolution fusion | flops 1610612736 | bytes 6815744 | tf_op jit(solution)/shard_map/dot_general | solution.py:275
  385.8 8.2 %convolution_convert_fusion.1 = bf16[1024,1536]{1,0:T(8,128)(2,1)} fusion(bf16[512,1536]{1,0:T(8,128)(2,1)S(1)} %copy-done, f32[1024,512]{1,0:T(8,128)} %fusion.22, bf16[1024,1536]{1,0:T(8,128)(2,1)} %reshape_reshape.8, bf16[1536,512]{1,0:T(8,128)(2,1)} %param.30), kind=kOutput, calls=%fused_computation.2 | convolution fusion | flops 3225944064 | bytes 11534336 | tf_op jit(solution)/shard_map/dot_general | solution.py:284
  394.0 7.2 %convert_element_type.73 = bf16[2,4,64,2,1536]{4,3,2,1,0:T(2,128)(2,1)} reshape(bf16[1024,1536]{1,0:T(8,128)(2,1)} %convolution_convert_fusion.1) | data formatting | bytes 6291456 | tf_op jit(solution)/shard_map/convert_element_type | solution.py:290
  401.2 4.2 copy.76
  405.5 41.2 %reduce-scatter.9.cloned.1.call-done = bf16[2,1,64,2,1536]{4,2,3,0,1:T(8,128)(2,1)} async-done(((bf16[2,4,64,2,1536]{4,2,3,0,1:T(8,128)(2,1)}), bf16[2,1,64,2,1536]{4,2,3,0,1:T(8,128)(2,1)}) %reduce-scatter.9.cloned.1.call-update) | async-done | bytes 786448 | tf_op jit(solution)/shard_map/reduce_scatter | solution.py:171
  446.7 35.2 %reduce-scatter.11.cloned.1.call-done = bf16[1,64,2,1536]{3,1,2,0:T(8,128)(2,1)} async-done(((bf16[2,64,2,1536]{3,1,2,0:T(8,128)(2,1)}), bf16[1,64,2,1536]{3,1,2,0:T(8,128)(2,1)}) %reduce-scatter.11.cloned.1.call-update) | async-done | bytes 393232 | tf_op jit(solution)/shard_map/reduce_scatter | solution.py:172
  (82 shorter events, 38.0 us)
Async XLA Ops:
  6.5 379.3 %copy-start = (bf16[512,1536]{1,0:T(8,128)(2,1)S(1)}, bf16[512,1536]{1,0:T(8,128)(2,1)}, u32[]{:S(2)}) copy-start(bf16[512,1536]{1,0:T(8,128)(2,1)} %param.31) | copy-start | bytes 4718596
  6.5 26.1 %copy-start.12 = (s32[2]{0:T(128)S(1)}, s32[2]{0:T(128)}, u32[]{:S(2)}) copy-start(s32[2]{0:T(128)} %param.18) | copy-start | bytes 28
  6.5 34.4 %copy-start.10 = (bf16[8,128,96]{1,2,0:T(8,128)(2,1)S(1)}, bf16[8,128,96]{1,2,0:T(8,128)(2,1)}, u32[]{:S(2)}) copy-start(bf16[8,128,96]{1,2,0:T(8,128)(2,1)} %param.26) | copy-start | bytes 589828
  6.5 34.5 %copy-start.9 = (bf16[8,128,96]{1,2,0:T(8,128)(2,1)S(1)}, bf16[8,128,96]{1,2,0:T(8,128)(2,1)}, u32[]{:S(2)}) copy-start(bf16[8,128,96]{1,2,0:T(8,128)(2,1)} %param.27) | copy-start | bytes 589828
  6.5 70.6 %all-gather.7.cloned.1.call-start = ((), (), s32[]{:S(2)}) async-start(), calls=%async_computation.10 | async-start | bytes 3932160 | tf_op jit(solution)/shard_map/all_gather | solution.py:161
  33.2 12.9 %all-to-all-start = ((s32[32,1,2]{2,1,0:T(1,128)}), s32[32,1,2]{2,1,0:T(1,128)S(1)}, u32[]{:S(2)}, u32[]{:S(2)}) async-start(s32[32,1,2]{2,1,0:T(1,128)} %broadcast_in_dim.9), calls=%async_computation | async-start | bytes 32768 | tf_op jit(solution)/shard_map/all_to_all | solution.py:177
  53.2 7.4 %copy-start.5 = (bf16[2,4096,96]{1,2,0:T(8,128)(2,1)S(1)}, bf16[2,4096,96]{1,2,0:T(8,128)(2,1)}, u32[]{:S(2)}) copy-start(bf16[2,4096,96]{1,2,0:T(8,128)(2,1)} %param.24) | copy-start | bytes 4718596
  53.2 75.8 %all-to-all-start.1 = ((bf16[32,2,2,128,96]{3,4,2,1,0:T(8,128)(2,1)}), bf16[32,2,2,128,96]{3,4,2,1,0:T(8,128)(2,1)}, u32[]{:S(2)}, u32[]{:S(2)}) async-start(bf16[32,2,2,128,96]{3,4,2,1,0:T(8,128)(2,1)} %broadcast_select_fusion), calls=%async_computation.1 | async-start | bytes 6291456 | tf_op jit(solution)/shard_map/all_to_all | solution.py:182
  60.4 6.6 %copy-start.15 = (s32[2]{0:T(128)S(1)}, s32[2]{0:T(128)}, u32[]{:S(2)}) copy-start(s32[2]{0:T(128)} %length_ref.1) | copy-start | bytes 28
  60.4 203.6 %reduce-scatter.5.cloned.1.call-start = ((), (), s32[]{:S(2)}) async-start(), calls=%async_computation.6 | async-start | bytes 3932160 | tf_op jit(solution)/shard_map/reduce_scatter | solution.py:171
  77.1 2.8 copy-start.1
  80.0 4.9 copy-start.2
  80.0 4.9 copy-start.14
  87.2 7.5 %copy-start.7 = (bf16[1536,96]{0,1:T(8,128)(2,1)S(1)}, bf16[1536,96]{0,1:T(8,128)(2,1)}, u32[]{:S(2)}) copy-start(bf16[1536,96]{0,1:T(8,128)(2,1)} %param.22) | copy-start | bytes 884740
  94.8 3.2 copy-start.8
  139.6 72.0 %copy-start.6 = (bf16[192,1536]{1,0:T(8,128)(2,1)S(1)}, bf16[192,1536]{1,0:T(8,128)(2,1)}, u32[]{:S(2)}) copy-start(bf16[192,1536]{1,0:T(8,128)(2,1)} %param.23) | copy-start | bytes 1769476
  214.6 84.6 %copy-start.3 = (bf16[64,2,1536]{2,1,0:T(2,128)(2,1)S(1)}, bf16[64,2,1536]{2,1,0:T(2,128)(2,1)}, u32[]{:S(2)}) copy-start(bf16[64,2,1536]{2,1,0:T(2,128)(2,1)} %param.16) | copy-start | bytes 1179652
  214.6 85.8 %copy-start.11 = (f32[1536]{0:T(1024)S(1)}, f32[1536]{0:T(1024)}, u32[]{:S(2)}) copy-start(f32[1536]{0:T(1024)} %param.28) | copy-start | bytes 18436
  214.6 84.6 %reduce-scatter.7.cloned.1.call-start = ((), (), s32[]{:S(2)}) async-start(), calls=%async_computation.7 | async-start | bytes 1179648 | tf_op jit(solution)/shard_map/reduce_scatter | solution.py:172
  264.0 102.3 %all-gather.9.cloned.1.call-start = ((), (), s32[]{:S(2)}) async-start(), calls=%async_computation.11 | async-start | bytes 3932160 | tf_op jit(solution)/shard_map/all_gather | solution.py:161
  325.4 121.2 %reduce-scatter.9.cloned.1.call-start = ((), (), s32[]{:S(2)}) async-start(), calls=%async_computation.8 | async-start | bytes 3932160 | tf_op jit(solution)/shard_map/reduce_scatter | solution.py:171
  373.1 7.6 %copy-start.13 = (bf16[1536,512]{1,0:T(8,128)(2,1)S(1)}, bf16[1536,512]{1,0:T(8,128)(2,1)}, u32[]{:S(2)}) copy-start(bf16[1536,512]{1,0:T(8,128)(2,1)} %param.29) | copy-start | bytes 4718596
  405.4 76.5 %copy-start.4 = (bf16[1,64,2,1536]{3,1,2,0:T(8,128)(2,1)S(1)}, bf16[1,64,2,1536]{3,1,2,0:T(8,128)(2,1)}, u32[]{:S(2)}) copy-start(bf16[1,64,2,1536]{3,1,2,0:T(8,128)(2,1)} %reduce-scatter.7.cloned.1.call-done) | copy-start | bytes 1179652
  405.4 76.4 %reduce-scatter.11.cloned.1.call-start = ((), (), s32[]{:S(2)}) async-start(), calls=%async_computation.9 | async-start | bytes 1179648 | tf_op jit(solution)/shard_map/reduce_scatter | solution.py:172
Sparse Core Ops, SparseCore 0:
  32.7 44.3 all-gather.6
  214.7 49.2 reduce-scatter.4
  266.5 32.6 reduce-scatter.6
  325.6 40.7 all-gather.8
  405.6 41.0 reduce-scatter.8
  449.2 32.6 reduce-scatter.10

commit v3 on v2

--- a/solution.py
+++ b/solution.py
@@ -156,20 +156,57 @@
     )(lengths, queries, prompt_k, prompt_v, window_k, window_v, new_k, new_v)
 
 
-def gather_rows(piece):
-    across = lax.all_gather(piece, "zh", axis=0, tiled=False)
-    both = lax.all_gather(across, "y", axis=0, tiled=False)
-    both = jnp.swapaxes(both, 0, 1)
+def exchange_kernel(piece_ref, other_ref, send_sem, recv_sem):
+    partner = (
+        lax.axis_index("dp"),
+        1 - lax.axis_index("zh"),
+        lax.axis_index("y"),
+    )
+    barrier = pltpu.get_barrier_semaphore()
+    pl.semaphore_signal(
+        barrier, 1, device_id=partner, device_id_type=pl.DeviceIdType.MESH
+    )
+    pl.semaphore_wait(barrier, 1)
+    copy = pltpu.make_async_remote_copy(
+        src_ref=piece_ref,
+        dst_ref=other_ref,
+        send_sem=send_sem,
+        recv_sem=recv_sem,
+        device_id=partner,
+        device_id_type=pl.DeviceIdType.MESH,
+    )
+    copy.start()
+    copy.wait()
+
+
+def exchange(piece, call_id):
+    return pl.pallas_call(
+        exchange_kernel,
+        out_shape=jax.ShapeDtypeStruct(piece.shape, piece.dtype),
+        in_specs=[pl.BlockSpec(memory_space=pl.ANY)],
+        out_specs=pl.BlockSpec(memory_space=pl.ANY),
+        scratch_shapes=[pltpu.SemaphoreType.DMA, pltpu.SemaphoreType.DMA],
+        compiler_params=pltpu.CompilerParams(collective_id=call_id, has_side_effects=True),
+    )(piece)
+
+
+def gather_rows(piece, call_id):
+    upper = lax.axis_index("zh") == 1
+    other = exchange(piece, call_id)
+    pair = jnp.stack([jnp.where(upper, other, piece), jnp.where(upper, piece, other)])
+    both = lax.all_gather(pair, "y", axis=0, tiled=False)
     return both.reshape((-1,) + piece.shape[1:])
 
 
-def scatter_rows(full):
-    rows = full.shape[0]
+def scatter_rows(full, call_id):
+    y_size = lax.axis_size("y")
     zh_size = lax.axis_size("zh")
-    y_size = lax.axis_size("y")
-    split = full.reshape((zh_size, y_size, rows // (zh_size * y_size)) + full.shape[1:])
-    part = lax.psum_scatter(split, "y", scatter_dimension=1, tiled=False)
-    return lax.psum_scatter(part, "zh", scatter_dimension=0, tiled=False)
+    split = full.reshape((y_size, zh_size, full.shape[0] // (y_size * zh_size)) + full.shape[1:])
+    part = lax.psum_scatter(split, "y", scatter_dimension=0, tiled=False)
+    me = lax.axis_index("zh")
+    mine = lax.dynamic_index_in_dim(part, me, 0, keepdims=False)
+    outgoing = lax.dynamic_index_in_dim(part, 1 - me, 0, keepdims=False)
+    return mine.astype(jnp.float32) + exchange(outgoing, call_id).astype(jnp.float32)
 
 
 def prompt_for_requests(prompt_keys, prompt_values, prompt_group):
@@ -215,13 +252,19 @@
     score_scale = 1.0 / math.sqrt(HEAD_SIZE)
     source = norm_rows(tokens, attn_gain)
     offset = 0
-    row_piece = gather_rows(source)
+    row_piece = gather_rows(source, 0)
     row_count = row_piece.shape[0]
     normed = row_piece
     flattened_rows = normed.reshape(row_count * local_reqs, MODEL_WIDTH)
-    positions = (
-        PROMPT_TOKENS + cached_len[None, :] + jnp.arange(row_count, dtype=jnp.int32)[:, None]
-    )
+    y_size = lax.axis_size("y")
+    zh_size = lax.axis_size("zh")
+    gathered_row = jnp.arange(row_count, dtype=jnp.int32)
+    token_of_row = (
+        (gathered_row // (zh_size * local_rows) + y_size * ((gathered_row // local_rows) % zh_size))
+        * local_rows
+        + gathered_row % local_rows
+    )
+    positions = PROMPT_TOKENS + cached_len[None, :] + token_of_row[:, None]
     project_queries = jnp.dot(flattened_rows, w_query, preferred_element_type=jnp.float32).reshape(
         row_count, local_reqs, query_cols // HEAD_SIZE, HEAD_SIZE
     )
@@ -242,20 +285,29 @@
         rotate(fresh_keys, positions).astype(jnp.bfloat16).reshape(row_count, local_reqs, key_cols)
     )
     query_heads = query_cols // HEAD_SIZE
+    grid_rows = (y_size, zh_size, local_rows, local_reqs)
     queries = (
-        project_queries.reshape(row_count, local_reqs, query_heads, HEAD_SIZE)
-        .transpose(1, 2, 0, 3)
+        project_queries.reshape(grid_rows + (query_heads, HEAD_SIZE))
+        .transpose(3, 4, 1, 0, 2, 5)
         .reshape(local_reqs, query_heads * row_count, HEAD_SIZE)
     )
-    own_keys = jnp.swapaxes(fresh_keys, 0, 1)
-    own_values = jnp.swapaxes(fresh_values, 0, 1)
+    own_keys = (
+        fresh_keys.reshape(grid_rows + (HEAD_SIZE,))
+        .transpose(3, 1, 0, 2, 4)
+        .reshape(local_reqs, row_count, HEAD_SIZE)
+    )
+    own_values = (
+        fresh_values.reshape(grid_rows + (HEAD_SIZE,))
+        .transpose(3, 1, 0, 2, 4)
+        .reshape(local_reqs, row_count, HEAD_SIZE)
+    )
     prompt_k, prompt_v = prompt_for_requests(prompt_keys, prompt_values, prompt_group)
     attended = attention(
         cached_len, queries, prompt_k, prompt_v, window_cache_keys, window_cache_values, own_keys, own_values
     )
     attended = (
-        attended.reshape(local_reqs, query_heads, row_count, HEAD_SIZE)
-        .transpose(2, 0, 1, 3)
+        attended.reshape(local_reqs, query_heads, zh_size, y_size, local_rows, HEAD_SIZE)
+        .transpose(3, 2, 4, 0, 1, 5)
         .reshape(row_count, local_reqs, query_cols)
     )
     picked = attended
@@ -266,10 +318,11 @@
             preferred_element_type=jnp.float32,
         )
         .reshape(FRESH_TOKENS, local_reqs, MODEL_WIDTH)
-        .astype(jnp.bfloat16)
-    ).astype(jnp.float32)
+        .astype(jnp.bfloat16),
+        1,
+    )
     residual = (tokens.astype(jnp.float32) + attn_part).astype(jnp.bfloat16)
-    row_piece = gather_rows(norm_rows(residual, mlp_gain))
+    row_piece = gather_rows(norm_rows(residual, mlp_gain), 2)
     row_count = row_piece.shape[0]
     flattened_rows = row_piece.reshape(row_count * local_reqs, MODEL_WIDTH)
     gate_part = jnp.dot(flattened_rows, w_gate, preferred_element_type=jnp.float32)
@@ -287,8 +340,9 @@
             preferred_element_type=jnp.float32,
         )
         .reshape(FRESH_TOKENS, local_reqs, MODEL_WIDTH)
-        .astype(jnp.bfloat16)
-    ).astype(jnp.float32)
+        .astype(jnp.bfloat16),
+        3,
+    )
     return (residual.astype(jnp.float32) + mlp_part).astype(jnp.bfloat16)
 
 

time: 496 us -> 485 us (0.978)
  Pallas kernels: 70.8 us -> 161 us
  waiting for transfers between devices: 241 us -> 165 us
  blocking collectives: 46.5 us -> 0 us
  local copies, waits for them, and re-layouts: 68 us -> 77.9 us
  other arithmetic: 14.4 us -> 23.7 us
    pallas_call x0 -> x4, Pallas kernels: none -> 89 us  [exchange(): pl.pallas_call(exchange_kernel, out_shape=jax.ShapeDtypeStruct(piece.shap...]
    reduce_scatter x4 -> x2, waiting for transfers between devices: 161 us -> 86.6 us  [scatter_rows(): part = lax.psum_scatter(split, 'y', scatter_dimension=0, tiled=False)]
    all_gather x2 -> x0, blocking collectives: 46.5 us -> none  [gather_rows(): across = lax.all_gather(piece, 'zh', axis=0, tiled=False)]
    all_gather x1 -> x3, local copies, waits for them, and re-layouts: 0.94 us -> 15.7 us  [gather_rows(): both = lax.all_gather(pair, 'y', axis=0, tiled=False)]
    transpose x5 -> x1, local copies, waits for them, and re-layouts: 16.2 us -> 1.69 us  [body(): own_values = fresh_values.reshape(grid_rows + (HEAD_SIZE,)).transpose(3,...]
    another operation x1 -> x6, other arithmetic: 0.15 us -> 7.22 us  [the longest x4 6.26 us: gather_rows(): jnp.stack([jnp.where(upper, other, piece), jnp.where(upper, piece, other)])]
  transfers between devices with their start and end apart: 8 -> 6, of which waited for: 8 -> 6; matrix products, arithmetic and copies ran while one was open for 8% -> 10% of each run, Pallas kernels for 0% -> 0%
where the time goes in v3:
time: 485 us; the launch traced here: 479 us
  waiting for transfers between devices  165 us (34%)
  Pallas kernels  161 us (33%)
  local copies, waits for them, and re-layouts  77.9 us (16%)
  other arithmetic  23.7 us (5%)
  matrix products  21.8 us (4%)
  starting transfers between devices  15.7 us (3%)
  between operations  13.7 us (3%)
    pallas_call x4, Pallas kernels, exchange(): pl.pallas_call(exchange_kernel, out_shape=jax.ShapeDtypeStruct(piece.shap...  89 us
    reduce_scatter x2, waiting for transfers between devices, scatter_rows(): part = lax.psum_scatter(split, 'y', scatter_dimension=0, tiled=False)  86.6 us
    pallas_call x1, Pallas kernels, attention(): pl.pallas_call(attention_kernel, grid_spec=grid_spec, out_shape=jax.Shape...  72.1 us
    all_gather x2, waiting for transfers between devices, gather_rows(): both = lax.all_gather(pair, 'y', axis=0, tiled=False)  52.7 us
    all_to_all x1, waiting for transfers between devices, prompt_for_requests(): incoming = lax.all_to_all(outgoing, 'dp', 0, 0, tiled=False)  20.4 us
    all_gather x3, local copies, waits for them, and re-layouts, gather_rows(): both = lax.all_gather(pair, 'y', axis=0, tiled=False)  15.7 us
    convert_element_type x2, local copies, waits for them, and re-layouts, body(): mlp_part = scatter_rows(jnp.dot(picked.reshape(FRESH_TOKENS * local_reqs,...  11.4 us
  transfers between devices with their start and end apart: 6, of which 6 were waited for; matrix products, arithmetic and copies ran while one was open for 10% of the time, Pallas kernels for 0%

profile of v3, /device:TPU:65, one launch (start us, length us, event | category | flops | bytes accessed | tf_op | source)
XLA Modules:
  0.0 478.8 jit_solution(13621612201176276210)
XLA Ops:
  10.4 23.0 %shard_map.154 = bf16[64,2,1536]{2,1,0:T(2,128)(2,1)} custom-call(bf16[64,2,1536]{2,1,0:T(2,128)(2,1)} %fusion.2.piece_ref), custom_call_target="tpu_custom_call" | custom-call | tf_op jit(solution)/shard_map/pallas_call | solution.py:183
  38.3 7.8 %all-to-all-start = ((s32[32,1,2]{2,1,0:T(1,128)}), s32[32,1,2]{2,1,0:T(1,128)S(1)}, u32[]{:S(2)}, u32[]{:S(2)}) async-start(s32[32,1,2]{2,1,0:T(1,128)} %broadcast_in_dim.9), calls=%async_computation | async-start | bytes 32768 | tf_op jit(solution)/shard_map/all_to_all | solution.py:214
  46.1 5.1 %all-to-all-done = s32[32,1,2]{2,1,0:T(1,128)S(1)} async-done(((s32[32,1,2]{2,1,0:T(1,128)}), s32[32,1,2]{2,1,0:T(1,128)S(1)}, u32[]{:S(2)}, u32[]{:S(2)}) %all-to-all-start) | async-done | bytes 288 | tf_op jit(solution)/shard_map/all_to_all | solution.py:214
  54.2 4.1 broadcast_select_fusion
  58.3 7.2 %all-to-all-start.1 = ((bf16[32,2,2,128,96]{3,4,2,1,0:T(8,128)(2,1)}), bf16[32,2,2,128,96]{3,4,2,1,0:T(8,128)(2,1)}, u32[]{:S(2)}, u32[]{:S(2)}) async-start(bf16[32,2,2,128,96]{3,4,2,1,0:T(8,128)(2,1)} %broadcast_select_fusion), calls=%async_computation.1 | async-start | bytes 6291456 | tf_op jit(solution)/shard_map/all_to_all | solution.py:219
  73.2 9.0 %all-gather.5.cloned.1.call-done = bf16[8,64,2,1536]{3,1,2,0:T(8,128)(2,1)} async-done(((bf16[2,64,2,1536]{3,1,2,0:T(8,128)(2,1)}), bf16[8,64,2,1536]{3,1,2,0:T(8,128)(2,1)}) %all-gather.5.cloned.1.call-update) | async-done | bytes 3145744 | tf_op jit(solution)/shard_map/all_gather | solution.py:197
  91.9 6.8 %copy.136 = bf16[8,64,2,1536]{3,2,1,0:T(2,128)(2,1)} copy(bf16[8,64,2,1536]{3,1,2,0:T(8,128)(2,1)} %all-gather.5.cloned.1.call-done) | data formatting | bytes 6291456 | tf_op jit(solution)/shard_map/all_gather | solution.py:197
  98.6 7.5 %reshape_reshape.12 = bf16[1024,1536]{1,0:T(8,128)(2,1)} reshape(bf16[8,64,2,1536]{3,2,1,0:T(2,128)(2,1)} %copy.136) | data formatting | bytes 6291456 | tf_op jit(solution)/shard_map/reshape;reshape | solution.py:258
  113.6 20.4 %all-to-all-done.1 = bf16[32,2,2,128,96]{3,4,2,1,0:T(8,128)(2,1)} async-done(((bf16[32,2,2,128,96]{3,4,2,1,0:T(8,128)(2,1)}), bf16[32,2,2,128,96]{3,4,2,1,0:T(8,128)(2,1)}, u32[]{:S(2)}, u32[]{:S(2)}) %all-to-all-start.1) | async-done | bytes 3145760 | tf_op jit(solution)/shard_map/all_to_all | solution.py:219
  134.1 6.1 %copy.133 = bf16[2,2,32,128,96]{4,3,2,0,1:T(8,128)(2,1)} copy(bf16[2,2,32,128,96]{3,4,1,0,2:T(8,128)(2,1)} %bitcast.15) | data formatting | bytes 6291456 | tf_op jit(solution)/shard_map/transpose | solution.py:222
  140.2 4.5 slice_bitcast_fusion
  144.7 72.1 %shard_map.155 = bf16[2,1024,96]{2,1,0:T(8,128)(2,1)} custom-call(s32[2]{0:T(128)} %length_ref.1, bf16[2,1024,96]{2,1,0:T(8,128)(2,1)} %bitcast.111, bf16[2,4096,96]{2,1,0:T(8,128)(2,1)} %get-tuple-element.8.pk_ref, bf16[2,4096,96]{2,1,0:T(8,128)(2,1)} %get-tuple-element.7.pv_ref, bf16[2,4096,96]{2,1,0:T(8,128)(2,1)} %copy.139.wk_ref, ...), custom_call_target="tpu_custom_call" | custom-call | flops 6845104128 | bytes 13369344 | tf_op jit(solution)/shard_map/pallas_call | solution.py:147
  221.6 45.3 %reduce-scatter.3.cloned.1.call-done = bf16[1,2,64,2,1536]{4,2,3,1,0:T(8,128)(2,1)} async-done(((bf16[4,2,64,2,1536]{4,2,3,1,0:T(8,128)(2,1)}), bf16[1,2,64,2,1536]{4,2,3,1,0:T(8,128)(2,1)}) %reduce-scatter.3.cloned.1.call-update) | async-done | bytes 786448 | tf_op jit(solution)/shard_map/reduce_scatter | solution.py:205
  269.3 23.6 %shard_map.156 = bf16[64,2,1536]{2,1,0:T(2,128)(2,1)} custom-call(bf16[64,2,1536]{2,1,0:T(2,128)(2,1)} %bitcast.108), custom_call_target="tpu_custom_call" | custom-call | tf_op jit(solution)/shard_map/pallas_call | solution.py:183
  296.3 18.7 %shard_map.157 = bf16[64,2,1536]{2,1,0:T(2,128)(2,1)} custom-call(bf16[64,2,1536]{2,1,0:T(2,128)(2,1)} %fusion.6.piece_ref), custom_call_target="tpu_custom_call" | custom-call | tf_op jit(solution)/shard_map/pallas_call | solution.py:183
  319.4 43.7 %all-gather.7.cloned.1.call-done = bf16[8,64,2,1536]{3,1,2,0:T(8,128)(2,1)} async-done(((bf16[2,64,2,1536]{3,1,2,0:T(8,128)(2,1)}), bf16[8,64,2,1536]{3,1,2,0:T(8,128)(2,1)}) %all-gather.7.cloned.1.call-update) | async-done | bytes 3145744 | tf_op jit(solution)/shard_map/all_gather | solution.py:197
  363.0 6.8 %copy.149 = bf16[8,64,2,1536]{3,2,1,0:T(2,128)(2,1)} copy(bf16[8,64,2,1536]{3,1,2,0:T(8,128)(2,1)} %all-gather.7.cloned.1.call-done) | data formatting | bytes 6291456 | tf_op jit(solution)/shard_map/all_gather | solution.py:197
  369.8 7.5 %reshape_reshape.14 = bf16[1024,1536]{1,0:T(8,128)(2,1)} reshape(bf16[8,64,2,1536]{3,2,1,0:T(2,128)(2,1)} %copy.149) | data formatting | bytes 6291456 | tf_op jit(solution)/shard_map/reshape;reshape | solution.py:327
  377.3 5.5 %fusion.38 = f32[1024,512]{1,0:T(8,128)} fusion(bf16[1024,1536]{1,0:T(8,128)(2,1)} %reshape_reshape.14, bf16[1536,512]{1,0:T(8,128)(2,1)} %param.29), kind=kOutput, calls=%fused_computation.97 | convolution fusion | flops 1610612736 | bytes 6815744 | tf_op jit(solution)/shard_map/dot_general | solution.py:328
  382.8 8.2 %convolution_convert_fusion.1 = bf16[1024,1536]{1,0:T(8,128)(2,1)} fusion(bf16[512,1536]{1,0:T(8,128)(2,1)S(1)} %copy-done, f32[1024,512]{1,0:T(8,128)} %fusion.38, bf16[1024,1536]{1,0:T(8,128)(2,1)} %reshape_reshape.14, bf16[1536,512]{1,0:T(8,128)(2,1)} %param.30), kind=kOutput, calls=%fused_computation.2 | convolution fusion | flops 3225944064 | bytes 11534336 | tf_op jit(solution)/shard_map/dot_general | solution.py:337
  391.0 7.2 %convert_element_type.81 = bf16[4,2,64,2,1536]{4,3,2,1,0:T(2,128)(2,1)} reshape(bf16[1024,1536]{1,0:T(8,128)(2,1)} %convolution_convert_fusion.1) | data formatting | bytes 6291456 | tf_op jit(solution)/shard_map/convert_element_type | solution.py:343
  398.2 4.2 copy.150
  402.5 41.2 %reduce-scatter.5.cloned.1.call-done = bf16[1,2,64,2,1536]{4,2,3,1,0:T(8,128)(2,1)} async-done(((bf16[4,2,64,2,1536]{4,2,3,1,0:T(8,128)(2,1)}), bf16[1,2,64,2,1536]{4,2,3,1,0:T(8,128)(2,1)}) %reduce-scatter.5.cloned.1.call-update) | async-done | bytes 786448 | tf_op jit(solution)/shard_map/reduce_scatter | solution.py:205
  446.0 23.6 %shard_map.158 = bf16[64,2,1536]{2,1,0:T(2,128)(2,1)} custom-call(bf16[64,2,1536]{2,1,0:T(2,128)(2,1)} %bitcast.109), custom_call_target="tpu_custom_call" | custom-call | tf_op jit(solution)/shard_map/pallas_call | solution.py:183
  (88 shorter events, 55.9 us)
Async XLA Ops:
  6.5 376.3 %copy-start = (bf16[512,1536]{1,0:T(8,128)(2,1)S(1)}, bf16[512,1536]{1,0:T(8,128)(2,1)}, u32[]{:S(2)}) copy-start(bf16[512,1536]{1,0:T(8,128)(2,1)} %param.31) | copy-start | bytes 4718596
  6.5 75.7 %all-gather.5.cloned.1.call-start = ((), (), s32[]{:S(2)}) async-start(), calls=%async_computation.6 | async-start | bytes 3932160 | tf_op jit(solution)/shard_map/all_gather | solution.py:197
  10.4 27.3 %copy-start.9 = (s32[2]{0:T(128)S(1)}, s32[2]{0:T(128)}, u32[]{:S(2)}) copy-start(s32[2]{0:T(128)} %param.18) | copy-start | bytes 28
  10.4 35.7 %copy-start.6 = (bf16[8,128,96]{1,2,0:T(8,128)(2,1)S(1)}, bf16[8,128,96]{1,2,0:T(8,128)(2,1)}, u32[]{:S(2)}) copy-start(bf16[8,128,96]{1,2,0:T(8,128)(2,1)} %param.27) | copy-start | bytes 589828
  10.4 35.7 %copy-start.7 = (bf16[8,128,96]{1,2,0:T(8,128)(2,1)S(1)}, bf16[8,128,96]{1,2,0:T(8,128)(2,1)}, u32[]{:S(2)}) copy-start(bf16[8,128,96]{1,2,0:T(8,128)(2,1)} %param.26) | copy-start | bytes 589828
  38.3 12.9 %all-to-all-start = ((s32[32,1,2]{2,1,0:T(1,128)}), s32[32,1,2]{2,1,0:T(1,128)S(1)}, u32[]{:S(2)}, u32[]{:S(2)}) async-start(s32[32,1,2]{2,1,0:T(1,128)} %broadcast_in_dim.9), calls=%async_computation | async-start | bytes 32768 | tf_op jit(solution)/shard_map/all_to_all | solution.py:214
  58.3 7.7 %copy-start.3 = (bf16[2,4096,96]{1,2,0:T(8,128)(2,1)S(1)}, bf16[2,4096,96]{1,2,0:T(8,128)(2,1)}, u32[]{:S(2)}) copy-start(bf16[2,4096,96]{1,2,0:T(8,128)(2,1)} %param.24) | copy-start | bytes 4718596
  58.3 75.8 %all-to-all-start.1 = ((bf16[32,2,2,128,96]{3,4,2,1,0:T(8,128)(2,1)}), bf16[32,2,2,128,96]{3,4,2,1,0:T(8,128)(2,1)}, u32[]{:S(2)}, u32[]{:S(2)}) async-start(bf16[32,2,2,128,96]{3,4,2,1,0:T(8,128)(2,1)} %broadcast_select_fusion), calls=%async_computation.1 | async-start | bytes 6291456 | tf_op jit(solution)/shard_map/all_to_all | solution.py:219
  65.5 6.9 %copy-start.11 = (s32[2]{0:T(128)S(1)}, s32[2]{0:T(128)}, u32[]{:S(2)}) copy-start(s32[2]{0:T(128)} %length_ref.1) | copy-start | bytes 28
  65.5 201.5 %reduce-scatter.3.cloned.1.call-start = ((), (), s32[]{:S(2)}) async-start(), calls=%async_computation.4 | async-start | bytes 3932160 | tf_op jit(solution)/shard_map/reduce_scatter | solution.py:205
  73.2 11.2 %copy-start.10 = (bf16[1536,192]{0,1:T(8,128)(2,1)S(1)}, bf16[1536,192]{0,1:T(8,128)(2,1)}, u32[]{:S(2)}) copy-start(bf16[1536,192]{0,1:T(8,128)(2,1)} %param.20) | copy-start | bytes 1769476
  84.4 1.6 copy-start.1
  85.6 1.8 copy-start.5
  144.7 74.0 %copy-start.4 = (bf16[192,1536]{1,0:T(8,128)(2,1)S(1)}, bf16[192,1536]{1,0:T(8,128)(2,1)}, u32[]{:S(2)}) copy-start(bf16[192,1536]{1,0:T(8,128)(2,1)} %param.23) | copy-start | bytes 1769476
  221.6 71.4 %copy-start.2 = (bf16[64,2,1536]{2,1,0:T(2,128)(2,1)S(1)}, bf16[64,2,1536]{2,1,0:T(2,128)(2,1)}, u32[]{:S(2)}) copy-start(bf16[64,2,1536]{2,1,0:T(2,128)(2,1)} %param.16) | copy-start | bytes 1179652
  221.6 73.4 %copy-start.8 = (f32[1536]{0:T(1024)S(1)}, f32[1536]{0:T(1024)}, u32[]{:S(2)}) copy-start(f32[1536]{0:T(1024)} %param.28) | copy-start | bytes 18436
  221.6 141.4 %all-gather.7.cloned.1.call-start = ((), (), s32[]{:S(2)}) async-start(), calls=%async_computation.7 | async-start | bytes 3932160 | tf_op jit(solution)/shard_map/all_gather | solution.py:197
  319.1 124.6 %reduce-scatter.5.cloned.1.call-start = ((), (), s32[]{:S(2)}) async-start(), calls=%async_computation.5 | async-start | bytes 3932160 | tf_op jit(solution)/shard_map/reduce_scatter | solution.py:205
Sparse Core Ops, SparseCore 0:
  37.8 44.3 all-gather.4
  221.7 45.2 reduce-scatter.2
  319.2 43.7 all-gather.6
  402.6 41.0 reduce-scatter.4

commit v4 on v3

--- a/solution.py
+++ b/solution.py
@@ -66,11 +66,11 @@
     rows = lax.rem(lax.broadcasted_iota(jnp.int32, (row_count, KEY_BLOCK), 0), FRESH_TOKENS)
     cols = lax.broadcasted_iota(jnp.int32, (row_count, KEY_BLOCK), 1)
 
-    def absorb(k_ref, v_ref, visible):
+    def absorb(keys, values, visible):
         scores = (
             lax.dot_general(
                 q_ref[0],
-                k_ref[0],
+                keys,
                 (((1,), (1,)), ((), ())),
                 preferred_element_type=jnp.float32,
             )
@@ -83,7 +83,7 @@
         weights = jnp.exp(scores - new_peak)
         total[...] = total[...] * factor + jnp.sum(weights, axis=-1, keepdims=True)
         acc[...] = acc[...] * factor + jnp.dot(
-            weights.astype(jnp.bfloat16), v_ref[0], preferred_element_type=jnp.float32
+            weights.astype(jnp.bfloat16), values, preferred_element_type=jnp.float32
         )
         peak[...] = new_peak
 
@@ -95,7 +95,11 @@
     )
     def _():
         spot = prompt_start + cols
-        absorb(pk_ref, pv_ref, (spot < SINKS) | (spot > length + rows))
+        absorb(
+            pk_ref[:, 0, 0].reshape(KEY_BLOCK, HEAD_SIZE),
+            pv_ref[:, 0, 0].reshape(KEY_BLOCK, HEAD_SIZE),
+            (spot < SINKS) | (spot > length + rows),
+        )
 
     window_start = (block - prompt_blocks) * KEY_BLOCK
 
@@ -106,21 +110,38 @@
     )
     def _():
         slot = window_start + cols
-        absorb(wk_ref, wv_ref, (slot >= WINDOW_SPAN - length) & (slot > rows))
+        absorb(wk_ref[0], wv_ref[0], (slot >= WINDOW_SPAN - length) & (slot > rows))
 
     @pl.when(block == prompt_blocks + window_blocks)
     def _():
-        absorb(nk_ref, nv_ref, cols <= rows)
+        absorb(nk_ref[0], nv_ref[0], cols <= rows)
         o_ref[0] = (acc[...] / total[...]).astype(o_ref.dtype)
 
 
-def attention(lengths, queries, prompt_k, prompt_v, window_k, window_v, new_k, new_v):
+def attention(lengths, queries, prompt_kv, window_k, window_v, new_k, new_v):
     local_reqs, row_count, width = queries.shape
     prompt_blocks = PROMPT_TOKENS // KEY_BLOCK
     window_blocks = WINDOW_SPAN // KEY_BLOCK
     steps = prompt_blocks + window_blocks + 1
     key_spec = lambda pick: pl.BlockSpec((1, KEY_BLOCK, width), pick)
-    prompt_pick = lambda r, b, lens: (r, jnp.minimum(b, prompt_blocks - 1), 0)
+    source_rows = prompt_kv.shape[3]
+    if source_rows <= KEY_BLOCK:
+        prompt_spec = lambda half: pl.BlockSpec(
+            (KEY_BLOCK // source_rows, 1, 1, source_rows, width),
+            lambda r, b, lens: (jnp.minimum(b, prompt_blocks - 1), r, half, 0, 0),
+        )
+    else:
+        per_source = source_rows // KEY_BLOCK
+        prompt_spec = lambda half: pl.BlockSpec(
+            (1, 1, 1, KEY_BLOCK, width),
+            lambda r, b, lens: (
+                jnp.minimum(b, prompt_blocks - 1) // per_source,
+                r,
+                half,
+                jnp.minimum(b, prompt_blocks - 1) % per_source,
+                0,
+            ),
+        )
     window_pick = lambda r, b, lens: (r, jnp.clip(b - prompt_blocks, 0, window_blocks - 1), 0)
     fixed_pick = lambda r, b, lens: (r, 0, 0)
     grid_spec = pltpu.PrefetchScalarGridSpec(
@@ -128,8 +149,8 @@
         grid=(local_reqs, steps),
         in_specs=[
             pl.BlockSpec((1, row_count, width), fixed_pick),
-            key_spec(prompt_pick),
-            key_spec(prompt_pick),
+            prompt_spec(0),
+            prompt_spec(1),
             key_spec(window_pick),
             key_spec(window_pick),
             key_spec(fixed_pick),
@@ -153,7 +174,7 @@
             transcendentals=local_reqs * row_count * keys_total,
             bytes_accessed=4 * local_reqs * keys_total * width * 2,
         ),
-    )(lengths, queries, prompt_k, prompt_v, window_k, window_v, new_k, new_v)
+    )(lengths, queries, prompt_kv, prompt_kv, window_k, window_v, new_k, new_v)
 
 
 def exchange_kernel(piece_ref, other_ref, send_sem, recv_sem):
@@ -194,15 +215,14 @@
     upper = lax.axis_index("zh") == 1
     other = exchange(piece, call_id)
     pair = jnp.stack([jnp.where(upper, other, piece), jnp.where(upper, piece, other)])
-    both = lax.all_gather(pair, "y", axis=0, tiled=False)
-    return both.reshape((-1,) + piece.shape[1:])
+    return lax.all_gather(pair, "y", axis=0, tiled=True).reshape((-1,) + piece.shape[1:])
 
 
 def scatter_rows(full, call_id):
     y_size = lax.axis_size("y")
     zh_size = lax.axis_size("zh")
-    split = full.reshape((y_size, zh_size, full.shape[0] // (y_size * zh_size)) + full.shape[1:])
-    part = lax.psum_scatter(split, "y", scatter_dimension=0, tiled=False)
+    split = full.reshape((y_size * zh_size, full.shape[0] // (y_size * zh_size)) + full.shape[1:])
+    part = lax.psum_scatter(split, "y", scatter_dimension=0, tiled=True)
     me = lax.axis_index("zh")
     mine = lax.dynamic_index_in_dim(part, me, 0, keepdims=False)
     outgoing = lax.dynamic_index_in_dim(part, 1 - me, 0, keepdims=False)
@@ -216,12 +236,7 @@
     )
     both = jnp.stack([prompt_keys, prompt_values], axis=1)
     outgoing = jnp.take(both, wanted, axis=0)
-    incoming = lax.all_to_all(outgoing, "dp", 0, 0, tiled=False)
-    local_reqs = wanted.shape[1]
-    rows = prompt_keys.shape[1]
-    incoming = incoming.transpose(1, 2, 0, 3, 4)
-    incoming = incoming.reshape(local_reqs, 2, dp_size * rows, prompt_keys.shape[2])
-    return incoming[:, 0], incoming[:, 1]
+    return lax.all_to_all(outgoing, "dp", 0, 0, tiled=False)
 
 
 def body(
@@ -250,12 +265,10 @@
     key_heads = key_cols // HEAD_SIZE
     query_group_width = query_cols // key_cols
     score_scale = 1.0 / math.sqrt(HEAD_SIZE)
-    source = norm_rows(tokens, attn_gain)
+    source = norm_rows(tokens, attn_gain).reshape(local_rows * local_reqs, MODEL_WIDTH)
     offset = 0
-    row_piece = gather_rows(source, 0)
-    row_count = row_piece.shape[0]
-    normed = row_piece
-    flattened_rows = normed.reshape(row_count * local_reqs, MODEL_WIDTH)
+    flattened_rows = gather_rows(source, 0)
+    row_count = flattened_rows.shape[0] // local_reqs
     y_size = lax.axis_size("y")
     zh_size = lax.axis_size("zh")
     gathered_row = jnp.arange(row_count, dtype=jnp.int32)
@@ -301,9 +314,9 @@
         .transpose(3, 1, 0, 2, 4)
         .reshape(local_reqs, row_count, HEAD_SIZE)
     )
-    prompt_k, prompt_v = prompt_for_requests(prompt_keys, prompt_values, prompt_group)
+    prompt_kv = prompt_for_requests(prompt_keys, prompt_values, prompt_group)
     attended = attention(
-        cached_len, queries, prompt_k, prompt_v, window_cache_keys, window_cache_values, own_keys, own_values
+        cached_len, queries, prompt_kv, window_cache_keys, window_cache_values, own_keys, own_values
     )
     attended = (
         attended.reshape(local_reqs, query_heads, zh_size, y_size, local_rows, HEAD_SIZE)
@@ -316,33 +329,20 @@
             picked.reshape(FRESH_TOKENS * local_reqs, query_cols),
             w_out,
             preferred_element_type=jnp.float32,
-        )
-        .reshape(FRESH_TOKENS, local_reqs, MODEL_WIDTH)
-        .astype(jnp.bfloat16),
+        ).astype(jnp.bfloat16),
         1,
-    )
+    ).reshape(tokens.shape)
     residual = (tokens.astype(jnp.float32) + attn_part).astype(jnp.bfloat16)
-    row_piece = gather_rows(norm_rows(residual, mlp_gain), 2)
-    row_count = row_piece.shape[0]
-    flattened_rows = row_piece.reshape(row_count * local_reqs, MODEL_WIDTH)
+    flattened_rows = gather_rows(
+        norm_rows(residual, mlp_gain).reshape(local_rows * local_reqs, MODEL_WIDTH), 2
+    )
     gate_part = jnp.dot(flattened_rows, w_gate, preferred_element_type=jnp.float32)
     up_part = jnp.dot(flattened_rows, w_up, preferred_element_type=jnp.float32)
-    hidden = (
-        (jax.nn.silu(gate_part) * up_part)
-        .astype(jnp.bfloat16)
-        .reshape(row_count, local_reqs, hidden_cols)
-    )
-    picked = hidden
+    hidden = (jax.nn.silu(gate_part) * up_part).astype(jnp.bfloat16)
     mlp_part = scatter_rows(
-        jnp.dot(
-            picked.reshape(FRESH_TOKENS * local_reqs, hidden_cols),
-            w_down,
-            preferred_element_type=jnp.float32,
-        )
-        .reshape(FRESH_TOKENS, local_reqs, MODEL_WIDTH)
-        .astype(jnp.bfloat16),
+        jnp.dot(hidden, w_down, preferred_element_type=jnp.float32).astype(jnp.bfloat16),
         3,
-    )
+    ).reshape(tokens.shape)
     return (residual.astype(jnp.float32) + mlp_part).astype(jnp.bfloat16)
 
 

time: 485 us -> 448 us (0.924); the launches traced: 479 us -> 447 us
  local copies, waits for them, and re-layouts: 77.9 us -> 37.3 us
  waiting for transfers between devices: 165 us -> 179 us
  Pallas kernels: 161 us -> 156 us
    another operation x4 -> x1, local copies, waits for them, and re-layouts: 17 us -> 0.32 us  [body(): picked.reshape(FRESH_TOKENS * local_reqs, query_cols)]
    all_gather x3 -> x0, local copies, waits for them, and re-layouts: 15.7 us -> none  [gather_rows(): both = lax.all_gather(pair, 'y', axis=0, tiled=False)]
    convert_element_type x2 -> x0, local copies, waits for them, and re-layouts: 11.4 us -> none  [body(): mlp_part = scatter_rows(jnp.dot(picked.reshape(FRESH_TOKENS * local_reqs,...]
    all_to_all x1, waiting for transfers between devices: 20.4 us -> 28 us  [prompt_for_requests(): return lax.all_to_all(outgoing, 'dp', 0, 0, tiled=False)]
    dot_general x1, local copies, waits for them, and re-layouts: 0.32 us -> 7.2 us  [body(): jnp.dot(flattened_rows, w_query, preferred_element_type=jnp.float32)]
    reduce_scatter x2, waiting for transfers between devices: 86.6 us -> 92.9 us  [scatter_rows(): part = lax.psum_scatter(split, 'y', scatter_dimension=0, tiled=True)]
    all_to_all x0 -> x1, local copies, waits for them, and re-layouts: none -> 6.17 us  [prompt_for_requests(): return lax.all_to_all(outgoing, 'dp', 0, 0, tiled=False)]
    transpose x1 -> x0, local copies, waits for them, and re-layouts: 6.08 us -> none  [prompt_for_requests(): incoming = incoming.transpose(1, 2, 0, 3, 4)]
  transfers between devices with their start and end apart: 6 -> 6, of which waited for: 6 -> 6; matrix products, arithmetic and copies ran while one was open for 10% -> 9% of each run, Pallas kernels for 0% -> 0%
where the time goes in v4:
time: 448 us; the launch traced here: 447 us
  waiting for transfers between devices  179 us (40%)
  Pallas kernels  156 us (35%)
  local copies, waits for them, and re-layouts  37.3 us (8%)
  matrix products  24.9 us (6%)
  other arithmetic  21 us (5%)
  starting transfers between devices  15.5 us (3%)
  between operations  13.5 us (3%)
    reduce_scatter x2, waiting for transfers between devices, scatter_rows(): part = lax.psum_scatter(split, 'y', scatter_dimension=0, tiled=True)  92.9 us
    pallas_call x4, Pallas kernels, exchange(): pl.pallas_call(exchange_kernel, out_shape=jax.ShapeDtypeStruct(piece.shap...  89 us
    pallas_call x1, Pallas kernels, attention(): pl.pallas_call(attention_kernel, grid_spec=grid_spec, out_shape=jax.Shape...  66.6 us
    all_gather x2, waiting for transfers between devices, gather_rows(): lax.all_gather(pair, 'y', axis=0, tiled=True)  52.9 us
    all_to_all x1, waiting for transfers between devices, prompt_for_requests(): return lax.all_to_all(outgoing, 'dp', 0, 0, tiled=False)  28 us
  transfers between devices with their start and end apart: 6, of which 6 were waited for; matrix products, arithmetic and copies ran while one was open for 9% of the time, Pallas kernels for 0%

profile of v4, /device:TPU:65, one launch (start us, length us, event | category | flops | bytes accessed | tf_op | source)
XLA Modules:
  0.0 446.8 jit_solution(1899816074397913184)
XLA Ops:
  10.6 23.1 %shard_map.154 = bf16[128,1536]{1,0:T(8,128)(2,1)} custom-call(bf16[128,1536]{1,0:T(8,128)(2,1)} %reshape.218.piece_ref), custom_call_target="tpu_custom_call" | custom-call | tf_op jit(solution)/shard_map/pallas_call | solution.py:204
  36.5 7.8 %all-to-all-start = ((s32[32,1,2]{2,1,0:T(1,128)}), s32[32,1,2]{2,1,0:T(1,128)S(1)}, u32[]{:S(2)}, u32[]{:S(2)}) async-start(s32[32,1,2]{2,1,0:T(1,128)} %broadcast_in_dim.9), calls=%async_computation | async-start | bytes 32768 | tf_op jit(solution)/shard_map/all_to_all | solution.py:234
  44.3 5.1 %all-to-all-done = s32[32,1,2]{2,1,0:T(1,128)S(1)} async-done(((s32[32,1,2]{2,1,0:T(1,128)}), s32[32,1,2]{2,1,0:T(1,128)S(1)}, u32[]{:S(2)}, u32[]{:S(2)}) %all-to-all-start) | async-done | bytes 288 | tf_op jit(solution)/shard_map/all_to_all | solution.py:234
  49.8 2.6 gather_fusion
  52.4 4.1 broadcast_select_fusion
  56.5 7.2 %all-to-all-start.1 = ((bf16[32,2,2,128,96]{3,4,2,1,0:T(8,128)(2,1)}), bf16[32,2,2,128,96]{3,4,2,1,0:T(8,128)(2,1)}, u32[]{:S(2)}, u32[]{:S(2)}) async-start(bf16[32,2,2,128,96]{3,4,2,1,0:T(8,128)(2,1)} %broadcast_select_fusion), calls=%async_computation.1 | async-start | bytes 6291456 | tf_op jit(solution)/shard_map/all_to_all | solution.py:239
  66.4 3.9 copy.111.wv_ref
  71.2 9.2 %all-gather.3.cloned.1.call-done = bf16[8,128,1536]{2,1,0:T(8,128)(2,1)} async-done(((bf16[2,128,1536]{2,1,0:T(8,128)(2,1)}), bf16[8,128,1536]{2,1,0:T(8,128)(2,1)}) %all-gather.3.cloned.1.call-update) | async-done | bytes 3145744 | tf_op jit(solution)/shard_map/all_gather | solution.py:218
  80.4 7.2 %dot_general.29 = bf16[512,2,1536]{2,1,0:T(2,128)(2,1)} reshape(bf16[8,128,1536]{2,1,0:T(8,128)(2,1)} %all-gather.3.cloned.1.call-done) | data formatting | bytes 6291456 | tf_op jit(solution)/shard_map/dot_general | solution.py:281
  87.6 3.1 fusion
  92.2 3.0 fusion.4
  96.7 3.0 convolution_convert_fusion.2
  104.3 28.0 %all-to-all-done.1 = bf16[32,2,2,128,96]{3,4,2,1,0:T(8,128)(2,1)} async-done(((bf16[32,2,2,128,96]{3,4,2,1,0:T(8,128)(2,1)}), bf16[32,2,2,128,96]{3,4,2,1,0:T(8,128)(2,1)}, u32[]{:S(2)}, u32[]{:S(2)}) %all-to-all-start.1) | async-done | bytes 3145760 | tf_op jit(solution)/shard_map/all_to_all | solution.py:239
  132.3 6.2 %copy.108.pk_ref.pv_ref = bf16[32,2,2,128,96]{4,3,2,1,0:T(8,128)(2,1)} copy(bf16[32,2,2,128,96]{3,4,2,1,0:T(8,128)(2,1)} %all-to-all-done.1) | data formatting | bytes 6291456 | tf_op jit(solution)/shard_map/all_to_all | solution.py:239
  138.4 66.6 %shard_map.155 = bf16[2,1024,96]{2,1,0:T(8,128)(2,1)} custom-call(s32[2]{0:T(128)} %length_ref.1, bf16[2,1024,96]{2,1,0:T(8,128)(2,1)} %bitcast.89, bf16[32,2,2,128,96]{4,3,2,1,0:T(8,128)(2,1)} %copy.108.pk_ref.pv_ref, bf16[32,2,2,128,96]{4,3,2,1,0:T(8,128)(2,1)} %copy.108.pk_ref.pv_ref, bf16[2,4096,96]{2,1,0:T(8,128)(2,1)} %copy.110.wk_ref, ...), custom_call_target="tpu_custom_call" | custom-call | flops 6845104128 | bytes 13369344 | tf_op jit(solution)/shard_map/pallas_call | solution.py:168
  207.0 2.6 convolution_convert_fusion
  209.7 51.7 %reduce-scatter.3.cloned.1.call-done = bf16[2,128,1536]{2,1,0:T(8,128)(2,1)} async-done(((bf16[8,128,1536]{2,1,0:T(8,128)(2,1)}), bf16[2,128,1536]{2,1,0:T(8,128)(2,1)}) %reduce-scatter.3.cloned.1.call-update) | async-done | bytes 786448 | tf_op jit(solution)/shard_map/reduce_scatter | solution.py:225
  263.1 23.6 %shard_map.156 = bf16[128,1536]{1,0:T(8,128)(2,1)} custom-call(bf16[128,1536]{1,0:T(8,128)(2,1)} %dynamic-slice_bitcast_fusion.1.piece_ref), custom_call_target="tpu_custom_call" | custom-call | tf_op jit(solution)/shard_map/pallas_call | solution.py:204
  292.6 18.7 %shard_map.157 = bf16[128,1536]{1,0:T(8,128)(2,1)} custom-call(bf16[128,1536]{1,0:T(8,128)(2,1)} %reshape.226.piece_ref), custom_call_target="tpu_custom_call" | custom-call | tf_op jit(solution)/shard_map/pallas_call | solution.py:204
  313.8 43.7 %all-gather.5.cloned.1.call-done = bf16[8,128,1536]{2,1,0:T(8,128)(2,1)} async-done(((bf16[2,128,1536]{2,1,0:T(8,128)(2,1)}), bf16[8,128,1536]{2,1,0:T(8,128)(2,1)}) %all-gather.5.cloned.1.call-update) | async-done | bytes 3145744 | tf_op jit(solution)/shard_map/all_gather | solution.py:218
  357.5 5.0 %fusion.39 = f32[1024,512]{1,0:T(8,128)} fusion(bf16[1024,1536]{1,0:T(8,128)(2,1)} %bitcast.95, bf16[1536,512]{1,0:T(8,128)(2,1)S(1)} %copy-done.8), kind=kOutput, calls=%fused_computation.87 | convolution fusion | flops 1610612736 | bytes 6815744 | tf_op jit(solution)/shard_map/dot_general | solution.py:339
  362.6 8.2 %convolution_convert_fusion.1 = bf16[1024,1536]{1,0:T(8,128)(2,1)} fusion(bf16[512,1536]{1,0:T(8,128)(2,1)S(1)} %copy-done, f32[1024,512]{1,0:T(8,128)} %fusion.39, bf16[1024,1536]{1,0:T(8,128)(2,1)} %bitcast.96, bf16[1536,512]{1,0:T(8,128)(2,1)} %param.30), kind=kOutput, calls=%fused_computation.2 | convolution fusion | flops 3225944064 | bytes 11534336 | tf_op jit(solution)/shard_map/dot_general | solution.py:343
  370.8 41.2 %reduce-scatter.5.cloned.1.call-done = bf16[2,128,1536]{2,1,0:T(8,128)(2,1)} async-done(((bf16[8,128,1536]{2,1,0:T(8,128)(2,1)}), bf16[2,128,1536]{2,1,0:T(8,128)(2,1)}) %reduce-scatter.5.cloned.1.call-update) | async-done | bytes 786448 | tf_op jit(solution)/shard_map/reduce_scatter | solution.py:225
  413.8 23.6 %shard_map.158 = bf16[128,1536]{1,0:T(8,128)(2,1)} custom-call(bf16[128,1536]{1,0:T(8,128)(2,1)} %dynamic-slice_bitcast_fusion.piece_ref), custom_call_target="tpu_custom_call" | custom-call | tf_op jit(solution)/shard_map/pallas_call | solution.py:204
  (82 shorter events, 35.0 us)
Async XLA Ops:
  6.5 356.0 %copy-start = (bf16[512,1536]{1,0:T(8,128)(2,1)S(1)}, bf16[512,1536]{1,0:T(8,128)(2,1)}, u32[]{:S(2)}) copy-start(bf16[512,1536]{1,0:T(8,128)(2,1)} %param.31) | copy-start | bytes 4718596
  6.5 73.8 %all-gather.3.cloned.1.call-start = ((), (), s32[]{:S(2)}) async-start(), calls=%async_computation.4 | async-start | bytes 3932160 | tf_op jit(solution)/shard_map/all_gather | solution.py:218
  8.2 27.7 %copy-start.7 = (s32[2]{0:T(128)S(1)}, s32[2]{0:T(128)}, u32[]{:S(2)}) copy-start(s32[2]{0:T(128)} %param.18) | copy-start | bytes 28
  8.2 36.1 %copy-start.4 = (bf16[8,128,96]{1,2,0:T(8,128)(2,1)S(1)}, bf16[8,128,96]{1,2,0:T(8,128)(2,1)}, u32[]{:S(2)}) copy-start(bf16[8,128,96]{1,2,0:T(8,128)(2,1)} %param.27) | copy-start | bytes 589828
  8.2 36.1 %copy-start.5 = (bf16[8,128,96]{1,2,0:T(8,128)(2,1)S(1)}, bf16[8,128,96]{1,2,0:T(8,128)(2,1)}, u32[]{:S(2)}) copy-start(bf16[8,128,96]{1,2,0:T(8,128)(2,1)} %param.26) | copy-start | bytes 589828
  36.5 12.9 %all-to-all-start = ((s32[32,1,2]{2,1,0:T(1,128)}), s32[32,1,2]{2,1,0:T(1,128)S(1)}, u32[]{:S(2)}, u32[]{:S(2)}) async-start(s32[32,1,2]{2,1,0:T(1,128)} %broadcast_in_dim.9), calls=%async_computation | async-start | bytes 32768 | tf_op jit(solution)/shard_map/all_to_all | solution.py:234
  56.5 7.4 %copy-start.2 = (bf16[2,4096,96]{1,2,0:T(8,128)(2,1)S(1)}, bf16[2,4096,96]{1,2,0:T(8,128)(2,1)}, u32[]{:S(2)}) copy-start(bf16[2,4096,96]{1,2,0:T(8,128)(2,1)} %param.24) | copy-start | bytes 4718596
  56.5 75.8 %all-to-all-start.1 = ((bf16[32,2,2,128,96]{3,4,2,1,0:T(8,128)(2,1)}), bf16[32,2,2,128,96]{3,4,2,1,0:T(8,128)(2,1)}, u32[]{:S(2)}, u32[]{:S(2)}) async-start(bf16[32,2,2,128,96]{3,4,2,1,0:T(8,128)(2,1)} %broadcast_select_fusion), calls=%async_computation.1 | async-start | bytes 6291456 | tf_op jit(solution)/shard_map/all_to_all | solution.py:239
  63.7 6.7 %copy-start.11 = (s32[2]{0:T(128)S(1)}, s32[2]{0:T(128)}, u32[]{:S(2)}) copy-start(s32[2]{0:T(128)} %length_ref.1) | copy-start | bytes 28
  63.7 197.7 %reduce-scatter.3.cloned.1.call-start = ((), (), s32[]{:S(2)}) async-start(), calls=%async_computation.5 | async-start | bytes 3932160 | tf_op jit(solution)/shard_map/reduce_scatter | solution.py:225
  71.2 16.4 %copy-start.9 = (bf16[1536,192]{0,1:T(8,128)(2,1)S(1)}, bf16[1536,192]{0,1:T(8,128)(2,1)}, u32[]{:S(2)}) copy-start(bf16[1536,192]{0,1:T(8,128)(2,1)} %param.20) | copy-start | bytes 1769476
  90.7 1.6 copy-start.10
  138.4 68.5 %copy-start.3 = (bf16[192,1536]{1,0:T(8,128)(2,1)S(1)}, bf16[192,1536]{1,0:T(8,128)(2,1)}, u32[]{:S(2)}) copy-start(bf16[192,1536]{1,0:T(8,128)(2,1)} %param.23) | copy-start | bytes 1769476
  209.6 80.9 %copy-start.1 = (bf16[64,2,1536]{2,1,0:T(2,128)(2,1)S(1)}, bf16[64,2,1536]{2,1,0:T(2,128)(2,1)}, u32[]{:S(2)}) copy-start(bf16[64,2,1536]{2,1,0:T(2,128)(2,1)} %param.16) | copy-start | bytes 1179652
  209.6 147.9 %all-gather.5.cloned.1.call-start = ((), (), s32[]{:S(2)}) async-start(), calls=%async_computation.6 | async-start | bytes 3932160 | tf_op jit(solution)/shard_map/all_gather | solution.py:218
  209.6 81.6 %copy-start.6 = (f32[1536]{0:T(1024)S(1)}, f32[1536]{0:T(1024)}, u32[]{:S(2)}) copy-start(f32[1536]{0:T(1024)} %param.28) | copy-start | bytes 18436
  292.6 64.9 %copy-start.8 = (bf16[1536,512]{1,0:T(8,128)(2,1)S(1)}, bf16[1536,512]{1,0:T(8,128)(2,1)}, u32[]{:S(2)}) copy-start(bf16[1536,512]{1,0:T(8,128)(2,1)} %param.29) | copy-start | bytes 4718596
  313.5 98.5 %reduce-scatter.5.cloned.1.call-start = ((), (), s32[]{:S(2)}) async-start(), calls=%async_computation.7 | async-start | bytes 3932160 | tf_op jit(solution)/shard_map/reduce_scatter | solution.py:225
Sparse Core Ops, SparseCore 0:
  36.0 44.3 all-gather.2
  209.7 51.6 reduce-scatter.2
  313.6 43.8 all-gather.4
  370.9 41.0 reduce-scatter.4

commit v5 on v4

--- a/solution.py
+++ b/solution.py
@@ -46,25 +46,8 @@
 KEY_BLOCK = 512
 
 
-def attention_kernel(
-    length_ref, q_ref, pk_ref, pv_ref, wk_ref, wv_ref, nk_ref, nv_ref, o_ref, peak, total, acc
-):
-    request = pl.program_id(0)
-    block = pl.program_id(1)
-    length = length_ref[request]
-    prompt_blocks = PROMPT_TOKENS // KEY_BLOCK
-    window_blocks = WINDOW_SPAN // KEY_BLOCK
-    row_count = q_ref.shape[1]
+def absorber(q_ref, peak, total, acc):
     score_scale = 1.0 / math.sqrt(HEAD_SIZE)
-
-    @pl.when(block == 0)
-    def _():
-        peak[...] = jnp.full(peak.shape, far_below, jnp.float32)
-        total[...] = jnp.zeros(total.shape, jnp.float32)
-        acc[...] = jnp.zeros(acc.shape, jnp.float32)
-
-    rows = lax.rem(lax.broadcasted_iota(jnp.int32, (row_count, KEY_BLOCK), 0), FRESH_TOKENS)
-    cols = lax.broadcasted_iota(jnp.int32, (row_count, KEY_BLOCK), 1)
 
     def absorb(keys, values, visible):
         scores = (
@@ -77,22 +60,70 @@
             * score_scale
         )
         scores = jnp.where(visible, scores, -jnp.inf)
-        old_peak = peak[...]
+        old_peak = peak[0]
         new_peak = jnp.maximum(old_peak, jnp.max(scores, axis=-1, keepdims=True))
         factor = jnp.exp(old_peak - new_peak)
         weights = jnp.exp(scores - new_peak)
-        total[...] = total[...] * factor + jnp.sum(weights, axis=-1, keepdims=True)
-        acc[...] = acc[...] * factor + jnp.dot(
+        total[0] = total[0] * factor + jnp.sum(weights, axis=-1, keepdims=True)
+        acc[0] = acc[0] * factor + jnp.dot(
             weights.astype(jnp.bfloat16), values, preferred_element_type=jnp.float32
         )
-        peak[...] = new_peak
-
+        peak[0] = new_peak
+
+    return absorb
+
+
+def recent_kernel(length_ref, q_ref, wk_ref, wv_ref, nk_ref, nv_ref, acc, peak, total):
+    request = pl.program_id(0)
+    block = pl.program_id(1)
+    length = length_ref[request]
+    window_blocks = WINDOW_SPAN // KEY_BLOCK
+    row_count = q_ref.shape[1]
+    absorb = absorber(q_ref, peak, total, acc)
+
+    @pl.when(block == 0)
+    def _():
+        peak[...] = jnp.full(peak.shape, far_below, jnp.float32)
+        total[...] = jnp.zeros(total.shape, jnp.float32)
+        acc[...] = jnp.zeros(acc.shape, jnp.float32)
+
+    rows = lax.rem(lax.broadcasted_iota(jnp.int32, (row_count, KEY_BLOCK), 0), FRESH_TOKENS)
+    cols = lax.broadcasted_iota(jnp.int32, (row_count, KEY_BLOCK), 1)
+    window_start = block * KEY_BLOCK
+
+    @pl.when(
+        (block < window_blocks) & (window_start + KEY_BLOCK - 1 >= WINDOW_SPAN - length)
+    )
+    def _():
+        slot = window_start + cols
+        absorb(wk_ref[0], wv_ref[0], (slot >= WINDOW_SPAN - length) & (slot > rows))
+
+    @pl.when(block == window_blocks)
+    def _():
+        absorb(nk_ref[0], nv_ref[0], cols <= rows)
+
+
+def prompt_kernel(
+    length_ref, q_ref, pk_ref, pv_ref, acc_in, peak_in, total_in, o_ref, acc, peak, total
+):
+    request = pl.program_id(0)
+    block = pl.program_id(1)
+    length = length_ref[request]
+    prompt_blocks = PROMPT_TOKENS // KEY_BLOCK
+    row_count = q_ref.shape[1]
+    absorb = absorber(q_ref, peak, total, acc)
+
+    @pl.when(block == 0)
+    def _():
+        peak[...] = peak_in[...]
+        total[...] = total_in[...]
+        acc[...] = acc_in[...]
+
+    rows = lax.rem(lax.broadcasted_iota(jnp.int32, (row_count, KEY_BLOCK), 0), FRESH_TOKENS)
+    cols = lax.broadcasted_iota(jnp.int32, (row_count, KEY_BLOCK), 1)
     prompt_start = block * KEY_BLOCK
 
-    @pl.when(
-        (block < prompt_blocks)
-        & ((block == 0) | (prompt_start + KEY_BLOCK - 1 > length))
-    )
+    @pl.when((block == 0) | (prompt_start + KEY_BLOCK - 1 > length))
     def _():
         spot = prompt_start + cols
         absorb(
@@ -101,80 +132,88 @@
             (spot < SINKS) | (spot > length + rows),
         )
 
-    window_start = (block - prompt_blocks) * KEY_BLOCK
-
-    @pl.when(
-        (block >= prompt_blocks)
-        & (block < prompt_blocks + window_blocks)
-        & (window_start + KEY_BLOCK - 1 >= WINDOW_SPAN - length)
-    )
-    def _():
-        slot = window_start + cols
-        absorb(wk_ref[0], wv_ref[0], (slot >= WINDOW_SPAN - length) & (slot > rows))
-
-    @pl.when(block == prompt_blocks + window_blocks)
-    def _():
-        absorb(nk_ref[0], nv_ref[0], cols <= rows)
-        o_ref[0] = (acc[...] / total[...]).astype(o_ref.dtype)
+    @pl.when(block == prompt_blocks - 1)
+    def _():
+        o_ref[0] = (acc[0] / total[0]).astype(o_ref.dtype)
 
 
 def attention(lengths, queries, prompt_kv, window_k, window_v, new_k, new_v):
     local_reqs, row_count, width = queries.shape
     prompt_blocks = PROMPT_TOKENS // KEY_BLOCK
     window_blocks = WINDOW_SPAN // KEY_BLOCK
-    steps = prompt_blocks + window_blocks + 1
     key_spec = lambda pick: pl.BlockSpec((1, KEY_BLOCK, width), pick)
+    window_pick = lambda r, b, lens: (r, jnp.minimum(b, window_blocks - 1), 0)
+    fixed_pick = lambda r, b, lens: (r, 0, 0)
+    state_specs = [
+        pl.BlockSpec((1, row_count, width), fixed_pick),
+        pl.BlockSpec((1, row_count, 1), fixed_pick),
+        pl.BlockSpec((1, row_count, 1), fixed_pick),
+    ]
+    state_shapes = [
+        jax.ShapeDtypeStruct((local_reqs, row_count, width), jnp.float32),
+        jax.ShapeDtypeStruct((local_reqs, row_count, 1), jnp.float32),
+        jax.ShapeDtypeStruct((local_reqs, row_count, 1), jnp.float32),
+    ]
+    recent_keys = WINDOW_SPAN + FRESH_TOKENS
+    state = pl.pallas_call(
+        recent_kernel,
+        grid_spec=pltpu.PrefetchScalarGridSpec(
+            num_scalar_prefetch=1,
+            grid=(local_reqs, window_blocks + 1),
+            in_specs=[
+                pl.BlockSpec((1, row_count, width), fixed_pick),
+                key_spec(window_pick),
+                key_spec(window_pick),
+                key_spec(fixed_pick),
+                key_spec(fixed_pick),
+            ],
+            out_specs=state_specs,
+        ),
+        out_shape=state_shapes,
+        cost_estimate=pl.CostEstimate(
+            flops=4 * local_reqs * row_count * recent_keys * width,
+            transcendentals=local_reqs * row_count * recent_keys,
+            bytes_accessed=4 * local_reqs * recent_keys * width,
+        ),
+    )(lengths, queries, window_k, window_v, new_k, new_v)
+
     source_rows = prompt_kv.shape[3]
     if source_rows <= KEY_BLOCK:
         prompt_spec = lambda half: pl.BlockSpec(
             (KEY_BLOCK // source_rows, 1, 1, source_rows, width),
-            lambda r, b, lens: (jnp.minimum(b, prompt_blocks - 1), r, half, 0, 0),
+            lambda r, b, lens: (b, r, half, 0, 0),
         )
     else:
         per_source = source_rows // KEY_BLOCK
         prompt_spec = lambda half: pl.BlockSpec(
             (1, 1, 1, KEY_BLOCK, width),
-            lambda r, b, lens: (
-                jnp.minimum(b, prompt_blocks - 1) // per_source,
-                r,
-                half,
-                jnp.minimum(b, prompt_blocks - 1) % per_source,
-                0,
-            ),
+            lambda r, b, lens: (b // per_source, r, half, b % per_source, 0),
         )
-    window_pick = lambda r, b, lens: (r, jnp.clip(b - prompt_blocks, 0, window_blocks - 1), 0)
-    fixed_pick = lambda r, b, lens: (r, 0, 0)
-    grid_spec = pltpu.PrefetchScalarGridSpec(
-        num_scalar_prefetch=1,
-        grid=(local_reqs, steps),
-        in_specs=[
-            pl.BlockSpec((1, row_count, width), fixed_pick),
-            prompt_spec(0),
-            prompt_spec(1),
-            key_spec(window_pick),
-            key_spec(window_pick),
-            key_spec(fixed_pick),
-            key_spec(fixed_pick),
-        ],
-        out_specs=pl.BlockSpec((1, row_count, width), fixed_pick),
-        scratch_shapes=[
-            pltpu.VMEM((row_count, 1), jnp.float32),
-            pltpu.VMEM((row_count, 1), jnp.float32),
-            pltpu.VMEM((row_count, width), jnp.float32),
-        ],
-    )
-    keys_total = PROMPT_TOKENS + WINDOW_SPAN + FRESH_TOKENS
-    flops = 4 * local_reqs * row_count * keys_total * width
     return pl.pallas_call(
-        attention_kernel,
-        grid_spec=grid_spec,
+        prompt_kernel,
+        grid_spec=pltpu.PrefetchScalarGridSpec(
+            num_scalar_prefetch=1,
+            grid=(local_reqs, prompt_blocks),
+            in_specs=[
+                pl.BlockSpec((1, row_count, width), fixed_pick),
+                prompt_spec(0),
+                prompt_spec(1),
+            ]
+            + state_specs,
+            out_specs=pl.BlockSpec((1, row_count, width), fixed_pick),
+            scratch_shapes=[
+                pltpu.VMEM((1, row_count, width), jnp.float32),
+                pltpu.VMEM((1, row_count, 1), jnp.float32),
+                pltpu.VMEM((1, row_count, 1), jnp.float32),
+            ],
+        ),
         out_shape=jax.ShapeDtypeStruct(queries.shape, jnp.bfloat16),
         cost_estimate=pl.CostEstimate(
-            flops=flops,
-            transcendentals=local_reqs * row_count * keys_total,
-            bytes_accessed=4 * local_reqs * keys_total * width * 2,
+            flops=4 * local_reqs * row_count * PROMPT_TOKENS * width,
+            transcendentals=local_reqs * row_count * PROMPT_TOKENS,
+            bytes_accessed=4 * local_reqs * PROMPT_TOKENS * width,
         ),
-    )(lengths, queries, prompt_kv, prompt_kv, window_k, window_v, new_k, new_v)
+    )(lengths, queries, prompt_kv, prompt_kv, *state)
 
 
 def exchange_kernel(piece_ref, other_ref, send_sem, recv_sem):

time: 448 us -> 425 us (0.949)
  waiting for transfers between devices: 179 us -> 143 us
  Pallas kernels: 156 us -> 169 us
    all_to_all x1, waiting for transfers between devices: 28 us -> 0.01 us  [prompt_for_requests(): return lax.all_to_all(outgoing, 'dp', 0, 0, tiled=False)]
    pallas_call x1 -> x2, Pallas kernels: 66.6 us -> 80.1 us  [the longest x1 47 us: attention(): pl.pallas_call(prompt_kernel, grid_spec=pltpu.PrefetchScalarGridSpec(num_...]
    reduce_scatter x2, waiting for transfers between devices: 92.9 us -> 84.3 us  [scatter_rows(): part = lax.psum_scatter(split, 'y', scatter_dimension=0, tiled=True)]
  transfers between devices with their start and end apart: 6 -> 6, of which waited for: 6 -> 5; matrix products, arithmetic and copies ran while one was open for 9% -> 9% of each run, Pallas kernels for 0% -> 8%
where the time goes in v5:
time: 425 us; the launch traced here: 424 us
  Pallas kernels  169 us (40%)
  waiting for transfers between devices  143 us (34%)
  local copies, waits for them, and re-layouts  37.2 us (9%)
  matrix products  24.9 us (6%)
  other arithmetic  20.9 us (5%)
  starting transfers between devices  15.3 us (4%)
  between operations  13.5 us (3%)
    pallas_call x4, Pallas kernels, exchange(): pl.pallas_call(exchange_kernel, out_shape=jax.ShapeDtypeStruct(piece.shap...  89.1 us
    reduce_scatter x2, waiting for transfers between devices, scatter_rows(): part = lax.psum_scatter(split, 'y', scatter_dimension=0, tiled=True)  84.3 us
    all_gather x2, waiting for transfers between devices, gather_rows(): lax.all_gather(pair, 'y', axis=0, tiled=True)  53.2 us
    pallas_call x1, Pallas kernels, attention(): pl.pallas_call(prompt_kernel, grid_spec=pltpu.PrefetchScalarGridSpec(num_...  47 us
    pallas_call x1, Pallas kernels, attention(): pl.pallas_call(recent_kernel, grid_spec=pltpu.PrefetchScalarGridSpec(num_...  33.1 us
  transfers between devices with their start and end apart: 6, of which 5 were waited for; matrix products, arithmetic and copies ran while one was open for 9% of the time, Pallas kernels for 8%

profile of v5, /device:TPU:65, one launch (start us, length us, event | category | flops | bytes accessed | tf_op | source)
XLA Modules:
  0.0 423.7 jit_solution(7359777069269011324)
XLA Ops:
  10.6 23.1 %shard_map.154 = bf16[128,1536]{1,0:T(8,128)(2,1)} custom-call(bf16[128,1536]{1,0:T(8,128)(2,1)} %reshape.218.piece_ref), custom_call_target="tpu_custom_call" | custom-call | tf_op jit(solution)/shard_map/pallas_call | solution.py:243
  36.5 7.8 %all-to-all-start = ((s32[32,1,2]{2,1,0:T(1,128)}), s32[32,1,2]{2,1,0:T(1,128)S(1)}, u32[]{:S(2)}, u32[]{:S(2)}) async-start(s32[32,1,2]{2,1,0:T(1,128)} %broadcast_in_dim.9), calls=%async_computation | async-start | bytes 32768 | tf_op jit(solution)/shard_map/all_to_all | solution.py:273
  44.3 5.1 %all-to-all-done = s32[32,1,2]{2,1,0:T(1,128)S(1)} async-done(((s32[32,1,2]{2,1,0:T(1,128)}), s32[32,1,2]{2,1,0:T(1,128)S(1)}, u32[]{:S(2)}, u32[]{:S(2)}) %all-to-all-start) | async-done | bytes 288 | tf_op jit(solution)/shard_map/all_to_all | solution.py:273
  49.8 2.6 gather_fusion
  52.4 4.0 broadcast_select_fusion
  56.4 7.2 %all-to-all-start.1 = ((bf16[32,2,2,128,96]{3,4,2,1,0:T(8,128)(2,1)}), bf16[32,2,2,128,96]{3,4,2,1,0:T(8,128)(2,1)}, u32[]{:S(2)}, u32[]{:S(2)}) async-start(bf16[32,2,2,128,96]{3,4,2,1,0:T(8,128)(2,1)} %broadcast_select_fusion), calls=%async_computation.1 | async-start | bytes 6291456 | tf_op jit(solution)/shard_map/all_to_all | solution.py:278
  66.1 3.9 copy.109.wv_ref
  70.9 9.5 %all-gather.3.cloned.1.call-done = bf16[8,128,1536]{2,1,0:T(8,128)(2,1)} async-done(((bf16[2,128,1536]{2,1,0:T(8,128)(2,1)}), bf16[8,128,1536]{2,1,0:T(8,128)(2,1)}) %all-gather.3.cloned.1.call-update) | async-done | bytes 3145744 | tf_op jit(solution)/shard_map/all_gather | solution.py:257
  80.4 7.2 %dot_general.29 = bf16[512,2,1536]{2,1,0:T(2,128)(2,1)} reshape(bf16[8,128,1536]{2,1,0:T(8,128)(2,1)} %all-gather.3.cloned.1.call-done) | data formatting | bytes 6291456 | tf_op jit(solution)/shard_map/dot_general | solution.py:320
  87.6 3.1 fusion
  92.3 3.0 fusion.4
  96.8 3.0 convolution_convert_fusion.2
  104.3 33.1 %shard_map.155 = (f32[2,1024,96]{2,1,0:T(8,128)}, f32[2,1024,1]{2,1,0:T(8,128)}, f32[2,1024,1]{2,1,0:T(8,128)}) custom-call(s32[2]{0:T(128)} %length_ref.3, bf16[2,1024,96]{2,1,0:T(8,128)(2,1)} %bitcast.89, bf16[2,4096,96]{2,1,0:T(8,128)(2,1)} %copy.108.wk_ref, bf16[2,4096,96]{2,1,0:T(8,128)(2,1)} %copy.109.wv_ref, bf16[2,512,96]{2,1,0:T(8,128)(2,1)} %bitcast.92, ...), custom_call_target="tpu_custom_call" | custom-call | flops 3623878656 | bytes 3538944 | tf_op jit(solution)/shard_map/pallas_call | solution.py:158
  137.4 6.2 %copy.110.pk_ref.pv_ref = bf16[32,2,2,128,96]{4,3,2,1,0:T(8,128)(2,1)} copy(bf16[32,2,2,128,96]{3,4,2,1,0:T(8,128)(2,1)} %all-to-all-done.1) | data formatting | bytes 6291456 | tf_op jit(solution)/shard_map/all_to_all | solution.py:278
  143.6 47.0 %shard_map.156 = bf16[2,1024,96]{2,1,0:T(8,128)(2,1)} custom-call(s32[2]{0:T(128)} %length_ref.3, bf16[2,1024,96]{2,1,0:T(8,128)(2,1)} %bitcast.90, bf16[32,2,2,128,96]{4,3,2,1,0:T(8,128)(2,1)} %copy.110.pk_ref.pv_ref, bf16[32,2,2,128,96]{4,3,2,1,0:T(8,128)(2,1)} %copy.110.pk_ref.pv_ref, f32[2,1024,96]{2,1,0:T(8,128)} %get-tuple-element.8.acc_in, ...), custom_call_target="tpu_custom_call" | custom-call | flops 3221225472 | bytes 3145728 | tf_op jit(solution)/shard_map/pallas_call | solution.py:192
  192.5 2.6 convolution_convert_fusion
  195.2 43.1 %reduce-scatter.3.cloned.1.call-done = bf16[2,128,1536]{2,1,0:T(8,128)(2,1)} async-done(((bf16[8,128,1536]{2,1,0:T(8,128)(2,1)}), bf16[2,128,1536]{2,1,0:T(8,128)(2,1)}) %reduce-scatter.3.cloned.1.call-update) | async-done | bytes 786448 | tf_op jit(solution)/shard_map/reduce_scatter | solution.py:264
  240.1 23.6 %shard_map.157 = bf16[128,1536]{1,0:T(8,128)(2,1)} custom-call(bf16[128,1536]{1,0:T(8,128)(2,1)} %dynamic-slice_bitcast_fusion.1.piece_ref), custom_call_target="tpu_custom_call" | custom-call | tf_op jit(solution)/shard_map/pallas_call | solution.py:243
  269.6 18.7 %shard_map.158 = bf16[128,1536]{1,0:T(8,128)(2,1)} custom-call(bf16[128,1536]{1,0:T(8,128)(2,1)} %reshape.226.piece_ref), custom_call_target="tpu_custom_call" | custom-call | tf_op jit(solution)/shard_map/pallas_call | solution.py:243
  290.7 43.7 %all-gather.5.cloned.1.call-done = bf16[8,128,1536]{2,1,0:T(8,128)(2,1)} async-done(((bf16[2,128,1536]{2,1,0:T(8,128)(2,1)}), bf16[8,128,1536]{2,1,0:T(8,128)(2,1)}) %all-gather.5.cloned.1.call-update) | async-done | bytes 3145744 | tf_op jit(solution)/shard_map/all_gather | solution.py:257
  334.4 5.0 %fusion.39 = f32[1024,512]{1,0:T(8,128)} fusion(bf16[1024,1536]{1,0:T(8,128)(2,1)} %bitcast.96, bf16[1536,512]{1,0:T(8,128)(2,1)S(1)} %copy-done.8), kind=kOutput, calls=%fused_computation.87 | convolution fusion | flops 1610612736 | bytes 6815744 | tf_op jit(solution)/shard_map/dot_general | solution.py:378
  339.5 8.2 %convolution_convert_fusion.1 = bf16[1024,1536]{1,0:T(8,128)(2,1)} fusion(bf16[512,1536]{1,0:T(8,128)(2,1)S(1)} %copy-done, f32[1024,512]{1,0:T(8,128)} %fusion.39, bf16[1024,1536]{1,0:T(8,128)(2,1)} %bitcast.97, bf16[1536,512]{1,0:T(8,128)(2,1)} %param.30), kind=kOutput, calls=%fused_computation.2 | convolution fusion | flops 3225944064 | bytes 11534336 | tf_op jit(solution)/shard_map/dot_general | solution.py:382
  347.7 41.2 %reduce-scatter.5.cloned.1.call-done = bf16[2,128,1536]{2,1,0:T(8,128)(2,1)} async-done(((bf16[8,128,1536]{2,1,0:T(8,128)(2,1)}), bf16[2,128,1536]{2,1,0:T(8,128)(2,1)}) %reduce-scatter.5.cloned.1.call-update) | async-done | bytes 786448 | tf_op jit(solution)/shard_map/reduce_scatter | solution.py:264
  390.7 23.6 %shard_map.159 = bf16[128,1536]{1,0:T(8,128)(2,1)} custom-call(bf16[128,1536]{1,0:T(8,128)(2,1)} %dynamic-slice_bitcast_fusion.piece_ref), custom_call_target="tpu_custom_call" | custom-call | tf_op jit(solution)/shard_map/pallas_call | solution.py:243
  (83 shorter events, 34.7 us)
Async XLA Ops:
  6.5 333.0 %copy-start = (bf16[512,1536]{1,0:T(8,128)(2,1)S(1)}, bf16[512,1536]{1,0:T(8,128)(2,1)}, u32[]{:S(2)}) copy-start(bf16[512,1536]{1,0:T(8,128)(2,1)} %param.31) | copy-start | bytes 4718596
  6.5 73.9 %all-gather.3.cloned.1.call-start = ((), (), s32[]{:S(2)}) async-start(), calls=%async_computation.4 | async-start | bytes 3932160 | tf_op jit(solution)/shard_map/all_gather | solution.py:257
  8.2 27.7 %copy-start.7 = (s32[2]{0:T(128)S(1)}, s32[2]{0:T(128)}, u32[]{:S(2)}) copy-start(s32[2]{0:T(128)} %param.18) | copy-start | bytes 28
  8.2 36.1 %copy-start.4 = (bf16[8,128,96]{1,2,0:T(8,128)(2,1)S(1)}, bf16[8,128,96]{1,2,0:T(8,128)(2,1)}, u32[]{:S(2)}) copy-start(bf16[8,128,96]{1,2,0:T(8,128)(2,1)} %param.27) | copy-start | bytes 589828
  8.2 36.1 %copy-start.5 = (bf16[8,128,96]{1,2,0:T(8,128)(2,1)S(1)}, bf16[8,128,96]{1,2,0:T(8,128)(2,1)}, u32[]{:S(2)}) copy-start(bf16[8,128,96]{1,2,0:T(8,128)(2,1)} %param.26) | copy-start | bytes 589828
  36.5 12.9 %all-to-all-start = ((s32[32,1,2]{2,1,0:T(1,128)}), s32[32,1,2]{2,1,0:T(1,128)S(1)}, u32[]{:S(2)}, u32[]{:S(2)}) async-start(s32[32,1,2]{2,1,0:T(1,128)} %broadcast_in_dim.9), calls=%async_computation | async-start | bytes 32768 | tf_op jit(solution)/shard_map/all_to_all | solution.py:273
  56.4 7.2 %copy-start.2 = (bf16[2,4096,96]{1,2,0:T(8,128)(2,1)S(1)}, bf16[2,4096,96]{1,2,0:T(8,128)(2,1)}, u32[]{:S(2)}) copy-start(bf16[2,4096,96]{1,2,0:T(8,128)(2,1)} %param.24) | copy-start | bytes 4718596
  56.4 81.0 %all-to-all-start.1 = ((bf16[32,2,2,128,96]{3,4,2,1,0:T(8,128)(2,1)}), bf16[32,2,2,128,96]{3,4,2,1,0:T(8,128)(2,1)}, u32[]{:S(2)}, u32[]{:S(2)}) async-start(bf16[32,2,2,128,96]{3,4,2,1,0:T(8,128)(2,1)} %broadcast_select_fusion), calls=%async_computation.1 | async-start | bytes 6291456 | tf_op jit(solution)/shard_map/all_to_all | solution.py:278
  63.6 6.5 %copy-start.11 = (s32[2]{0:T(128)S(1)}, s32[2]{0:T(128)}, u32[]{:S(2)}) copy-start(s32[2]{0:T(128)} %length_ref.3) | copy-start | bytes 28
  63.6 174.7 %reduce-scatter.3.cloned.1.call-start = ((), (), s32[]{:S(2)}) async-start(), calls=%async_computation.5 | async-start | bytes 3932160 | tf_op jit(solution)/shard_map/reduce_scatter | solution.py:264
  70.9 16.7 %copy-start.9 = (bf16[1536,192]{0,1:T(8,128)(2,1)S(1)}, bf16[1536,192]{0,1:T(8,128)(2,1)}, u32[]{:S(2)}) copy-start(bf16[1536,192]{0,1:T(8,128)(2,1)} %param.20) | copy-start | bytes 1769476
  90.7 1.6 copy-start.10
  143.6 48.9 %copy-start.3 = (bf16[192,1536]{1,0:T(8,128)(2,1)S(1)}, bf16[192,1536]{1,0:T(8,128)(2,1)}, u32[]{:S(2)}) copy-start(bf16[192,1536]{1,0:T(8,128)(2,1)} %param.23) | copy-start | bytes 1769476
  195.1 72.3 %copy-start.1 = (bf16[64,2,1536]{2,1,0:T(2,128)(2,1)S(1)}, bf16[64,2,1536]{2,1,0:T(2,128)(2,1)}, u32[]{:S(2)}) copy-start(bf16[64,2,1536]{2,1,0:T(2,128)(2,1)} %param.16) | copy-start | bytes 1179652
  195.1 139.3 %all-gather.5.cloned.1.call-start = ((), (), s32[]{:S(2)}) async-start(), calls=%async_computation.6 | async-start | bytes 3932160 | tf_op jit(solution)/shard_map/all_gather | solution.py:257
  195.2 73.0 %copy-start.6 = (f32[1536]{0:T(1024)S(1)}, f32[1536]{0:T(1024)}, u32[]{:S(2)}) copy-start(f32[1536]{0:T(1024)} %param.28) | copy-start | bytes 18436
  269.6 64.9 %copy-start.8 = (bf16[1536,512]{1,0:T(8,128)(2,1)S(1)}, bf16[1536,512]{1,0:T(8,128)(2,1)}, u32[]{:S(2)}) copy-start(bf16[1536,512]{1,0:T(8,128)(2,1)} %param.29) | copy-start | bytes 4718596
  290.5 98.5 %reduce-scatter.5.cloned.1.call-start = ((), (), s32[]{:S(2)}) async-start(), calls=%async_computation.7 | async-start | bytes 3932160 | tf_op jit(solution)/shard_map/reduce_scatter | solution.py:264
Sparse Core Ops, SparseCore 0:
  36.0 44.3 all-gather.2
  195.2 43.0 reduce-scatter.2
  290.6 43.8 all-gather.4
  347.8 41.0 reduce-scatter.4

commit v6 on v5

--- a/solution.py
+++ b/solution.py
@@ -59,7 +59,8 @@
             )
             * score_scale
         )
-        scores = jnp.where(visible, scores, -jnp.inf)
+        if visible is not None:
+            scores = jnp.where(visible, scores, -jnp.inf)
         old_peak = peak[0]
         new_peak = jnp.maximum(old_peak, jnp.max(scores, axis=-1, keepdims=True))
         factor = jnp.exp(old_peak - new_peak)
@@ -91,12 +92,20 @@
     cols = lax.broadcasted_iota(jnp.int32, (row_count, KEY_BLOCK), 1)
     window_start = block * KEY_BLOCK
 
+    whole = (window_start >= WINDOW_SPAN - length) & (window_start >= FRESH_TOKENS)
+
     @pl.when(
-        (block < window_blocks) & (window_start + KEY_BLOCK - 1 >= WINDOW_SPAN - length)
+        (block < window_blocks)
+        & (window_start + KEY_BLOCK - 1 >= WINDOW_SPAN - length)
+        & jnp.logical_not(whole)
     )
     def _():
         slot = window_start + cols
         absorb(wk_ref[0], wv_ref[0], (slot >= WINDOW_SPAN - length) & (slot > rows))
+
+    @pl.when((block < window_blocks) & whole)
+    def _():
+        absorb(wk_ref[0], wv_ref[0], None)
 
     @pl.when(block == window_blocks)
     def _():
@@ -123,13 +132,23 @@
     cols = lax.broadcasted_iota(jnp.int32, (row_count, KEY_BLOCK), 1)
     prompt_start = block * KEY_BLOCK
 
-    @pl.when((block == 0) | (prompt_start + KEY_BLOCK - 1 > length))
+    whole = prompt_start > length + FRESH_TOKENS - 1
+
+    @pl.when(((block == 0) | (prompt_start + KEY_BLOCK - 1 > length)) & jnp.logical_not(whole))
     def _():
         spot = prompt_start + cols
         absorb(
             pk_ref[:, 0, 0].reshape(KEY_BLOCK, HEAD_SIZE),
             pv_ref[:, 0, 0].reshape(KEY_BLOCK, HEAD_SIZE),
             (spot < SINKS) | (spot > length + rows),
+        )
+
+    @pl.when(whole)
+    def _():
+        absorb(
+            pk_ref[:, 0, 0].reshape(KEY_BLOCK, HEAD_SIZE),
+            pv_ref[:, 0, 0].reshape(KEY_BLOCK, HEAD_SIZE),
+            None,
         )
 
     @pl.when(block == prompt_blocks - 1)

time: 425 us -> 425 us (level)
  transfers between devices with their start and end apart: 6 -> 6, of which waited for: 5 -> 5; matrix products, arithmetic and copies ran while one was open for 9% -> 9% of each run, Pallas kernels for 8% -> 7%
where the time goes in v6:
time: 425 us; the launch traced here: 423 us
  Pallas kernels  166 us (39%)
  waiting for transfers between devices  146 us (34%)
  local copies, waits for them, and re-layouts  37.2 us (9%)
  matrix products  24.9 us (6%)
  other arithmetic  20.9 us (5%)
  starting transfers between devices  15 us (4%)
  between operations  13.5 us (3%)
    pallas_call x4, Pallas kernels, exchange(): pl.pallas_call(exchange_kernel, out_shape=jax.ShapeDtypeStruct(piece.shap...  89 us
    reduce_scatter x2, waiting for transfers between devices, scatter_rows(): part = lax.psum_scatter(split, 'y', scatter_dimension=0, tiled=True)  87.2 us
    all_gather x2, waiting for transfers between devices, gather_rows(): lax.all_gather(pair, 'y', axis=0, tiled=True)  53.4 us
    pallas_call x1, Pallas kernels, attention(): pl.pallas_call(prompt_kernel, grid_spec=pltpu.PrefetchScalarGridSpec(num_...  46 us
    pallas_call x1, Pallas kernels, attention(): pl.pallas_call(recent_kernel, grid_spec=pltpu.PrefetchScalarGridSpec(num_...  30.9 us
  transfers between devices with their start and end apart: 6, of which 5 were waited for; matrix products, arithmetic and copies ran while one was open for 9% of the time, Pallas kernels for 7%

profile of v6, /device:TPU:65, one launch (start us, length us, event | category | flops | bytes accessed | tf_op | source)
XLA Modules:
  0.0 423.3 jit_solution(9984293636050897486)
XLA Ops:
  10.6 23.1 %shard_map.154 = bf16[128,1536]{1,0:T(8,128)(2,1)} custom-call(bf16[128,1536]{1,0:T(8,128)(2,1)} %reshape.218.piece_ref), custom_call_target="tpu_custom_call" | custom-call | tf_op jit(solution)/shard_map/pallas_call | solution.py:262
  36.5 7.8 %all-to-all-start = ((s32[32,1,2]{2,1,0:T(1,128)}), s32[32,1,2]{2,1,0:T(1,128)S(1)}, u32[]{:S(2)}, u32[]{:S(2)}) async-start(s32[32,1,2]{2,1,0:T(1,128)} %broadcast_in_dim.9), calls=%async_computation | async-start | bytes 32768 | tf_op jit(solution)/shard_map/all_to_all | solution.py:292
  44.3 5.1 %all-to-all-done = s32[32,1,2]{2,1,0:T(1,128)S(1)} async-done(((s32[32,1,2]{2,1,0:T(1,128)}), s32[32,1,2]{2,1,0:T(1,128)S(1)}, u32[]{:S(2)}, u32[]{:S(2)}) %all-to-all-start) | async-done | bytes 288 | tf_op jit(solution)/shard_map/all_to_all | solution.py:292
  49.8 2.6 gather_fusion
  52.4 4.0 broadcast_select_fusion
  56.4 7.2 %all-to-all-start.1 = ((bf16[32,2,2,128,96]{3,4,2,1,0:T(8,128)(2,1)}), bf16[32,2,2,128,96]{3,4,2,1,0:T(8,128)(2,1)}, u32[]{:S(2)}, u32[]{:S(2)}) async-start(bf16[32,2,2,128,96]{3,4,2,1,0:T(8,128)(2,1)} %broadcast_select_fusion), calls=%async_computation.1 | async-start | bytes 6291456 | tf_op jit(solution)/shard_map/all_to_all | solution.py:297
  66.1 3.9 copy.109.wv_ref
  70.9 9.5 %all-gather.3.cloned.1.call-done = bf16[8,128,1536]{2,1,0:T(8,128)(2,1)} async-done(((bf16[2,128,1536]{2,1,0:T(8,128)(2,1)}), bf16[8,128,1536]{2,1,0:T(8,128)(2,1)}) %all-gather.3.cloned.1.call-update) | async-done | bytes 3145744 | tf_op jit(solution)/shard_map/all_gather | solution.py:276
  80.4 7.2 %dot_general.29 = bf16[512,2,1536]{2,1,0:T(2,128)(2,1)} reshape(bf16[8,128,1536]{2,1,0:T(8,128)(2,1)} %all-gather.3.cloned.1.call-done) | data formatting | bytes 6291456 | tf_op jit(solution)/shard_map/dot_general | solution.py:339
  87.6 3.1 fusion
  92.3 3.0 fusion.4
  96.8 3.0 convolution_convert_fusion.2
  104.3 30.9 %shard_map.155 = (f32[2,1024,96]{2,1,0:T(8,128)}, f32[2,1024,1]{2,1,0:T(8,128)}, f32[2,1024,1]{2,1,0:T(8,128)}) custom-call(s32[2]{0:T(128)} %length_ref.3, bf16[2,1024,96]{2,1,0:T(8,128)(2,1)} %bitcast.89, bf16[2,4096,96]{2,1,0:T(8,128)(2,1)} %copy.108.wk_ref, bf16[2,4096,96]{2,1,0:T(8,128)(2,1)} %copy.109.wv_ref, bf16[2,512,96]{2,1,0:T(8,128)(2,1)} %bitcast.92, ...), custom_call_target="tpu_custom_call" | custom-call | flops 3623878656 | bytes 3538944 | tf_op jit(solution)/shard_map/pallas_call | solution.py:177
  135.2 6.2 %copy.110.pk_ref.pv_ref = bf16[32,2,2,128,96]{4,3,2,1,0:T(8,128)(2,1)} copy(bf16[32,2,2,128,96]{3,4,2,1,0:T(8,128)(2,1)} %all-to-all-done.1) | data formatting | bytes 6291456 | tf_op jit(solution)/shard_map/all_to_all | solution.py:297
  141.4 46.0 %shard_map.156 = bf16[2,1024,96]{2,1,0:T(8,128)(2,1)} custom-call(s32[2]{0:T(128)} %length_ref.3, bf16[2,1024,96]{2,1,0:T(8,128)(2,1)} %bitcast.90, bf16[32,2,2,128,96]{4,3,2,1,0:T(8,128)(2,1)} %copy.110.pk_ref.pv_ref, bf16[32,2,2,128,96]{4,3,2,1,0:T(8,128)(2,1)} %copy.110.pk_ref.pv_ref, f32[2,1024,96]{2,1,0:T(8,128)} %get-tuple-element.8.acc_in, ...), custom_call_target="tpu_custom_call" | custom-call | flops 3221225472 | bytes 3145728 | tf_op jit(solution)/shard_map/pallas_call | solution.py:211
  189.3 2.6 convolution_convert_fusion
  192.0 46.0 %reduce-scatter.3.cloned.1.call-done = bf16[2,128,1536]{2,1,0:T(8,128)(2,1)} async-done(((bf16[8,128,1536]{2,1,0:T(8,128)(2,1)}), bf16[2,128,1536]{2,1,0:T(8,128)(2,1)}) %reduce-scatter.3.cloned.1.call-update) | async-done | bytes 786448 | tf_op jit(solution)/shard_map/reduce_scatter | solution.py:283
  239.7 23.6 %shard_map.157 = bf16[128,1536]{1,0:T(8,128)(2,1)} custom-call(bf16[128,1536]{1,0:T(8,128)(2,1)} %dynamic-slice_bitcast_fusion.1.piece_ref), custom_call_target="tpu_custom_call" | custom-call | tf_op jit(solution)/shard_map/pallas_call | solution.py:262
  269.2 18.7 %shard_map.158 = bf16[128,1536]{1,0:T(8,128)(2,1)} custom-call(bf16[128,1536]{1,0:T(8,128)(2,1)} %reshape.226.piece_ref), custom_call_target="tpu_custom_call" | custom-call | tf_op jit(solution)/shard_map/pallas_call | solution.py:262
  290.1 43.9 %all-gather.5.cloned.1.call-done = bf16[8,128,1536]{2,1,0:T(8,128)(2,1)} async-done(((bf16[2,128,1536]{2,1,0:T(8,128)(2,1)}), bf16[8,128,1536]{2,1,0:T(8,128)(2,1)}) %all-gather.5.cloned.1.call-update) | async-done | bytes 3145744 | tf_op jit(solution)/shard_map/all_gather | solution.py:276
  334.1 5.1 %fusion.39 = f32[1024,512]{1,0:T(8,128)} fusion(bf16[1024,1536]{1,0:T(8,128)(2,1)} %bitcast.96, bf16[1536,512]{1,0:T(8,128)(2,1)S(1)} %copy-done.8), kind=kOutput, calls=%fused_computation.87 | convolution fusion | flops 1610612736 | bytes 6815744 | tf_op jit(solution)/shard_map/dot_general | solution.py:397
  339.1 8.2 %convolution_convert_fusion.1 = bf16[1024,1536]{1,0:T(8,128)(2,1)} fusion(bf16[512,1536]{1,0:T(8,128)(2,1)S(1)} %copy-done, f32[1024,512]{1,0:T(8,128)} %fusion.39, bf16[1024,1536]{1,0:T(8,128)(2,1)} %bitcast.97, bf16[1536,512]{1,0:T(8,128)(2,1)} %param.30), kind=kOutput, calls=%fused_computation.2 | convolution fusion | flops 3225944064 | bytes 11534336 | tf_op jit(solution)/shard_map/dot_general | solution.py:401
  347.3 41.2 %reduce-scatter.5.cloned.1.call-done = bf16[2,128,1536]{2,1,0:T(8,128)(2,1)} async-done(((bf16[8,128,1536]{2,1,0:T(8,128)(2,1)}), bf16[2,128,1536]{2,1,0:T(8,128)(2,1)}) %reduce-scatter.5.cloned.1.call-update) | async-done | bytes 786448 | tf_op jit(solution)/shard_map/reduce_scatter | solution.py:283
  390.3 23.6 %shard_map.159 = bf16[128,1536]{1,0:T(8,128)(2,1)} custom-call(bf16[128,1536]{1,0:T(8,128)(2,1)} %dynamic-slice_bitcast_fusion.piece_ref), custom_call_target="tpu_custom_call" | custom-call | tf_op jit(solution)/shard_map/pallas_call | solution.py:262
  (83 shorter events, 34.5 us)
Async XLA Ops:
  6.5 332.6 %copy-start = (bf16[512,1536]{1,0:T(8,128)(2,1)S(1)}, bf16[512,1536]{1,0:T(8,128)(2,1)}, u32[]{:S(2)}) copy-start(bf16[512,1536]{1,0:T(8,128)(2,1)} %param.31) | copy-start | bytes 4718596
  6.5 73.9 %all-gather.3.cloned.1.call-start = ((), (), s32[]{:S(2)}) async-start(), calls=%async_computation.4 | async-start | bytes 3932160 | tf_op jit(solution)/shard_map/all_gather | solution.py:276
  8.2 27.7 %copy-start.7 = (s32[2]{0:T(128)S(1)}, s32[2]{0:T(128)}, u32[]{:S(2)}) copy-start(s32[2]{0:T(128)} %param.18) | copy-start | bytes 28
  8.2 36.1 %copy-start.4 = (bf16[8,128,96]{1,2,0:T(8,128)(2,1)S(1)}, bf16[8,128,96]{1,2,0:T(8,128)(2,1)}, u32[]{:S(2)}) copy-start(bf16[8,128,96]{1,2,0:T(8,128)(2,1)} %param.27) | copy-start | bytes 589828
  8.2 36.1 %copy-start.5 = (bf16[8,128,96]{1,2,0:T(8,128)(2,1)S(1)}, bf16[8,128,96]{1,2,0:T(8,128)(2,1)}, u32[]{:S(2)}) copy-start(bf16[8,128,96]{1,2,0:T(8,128)(2,1)} %param.26) | copy-start | bytes 589828
  36.5 12.9 %all-to-all-start = ((s32[32,1,2]{2,1,0:T(1,128)}), s32[32,1,2]{2,1,0:T(1,128)S(1)}, u32[]{:S(2)}, u32[]{:S(2)}) async-start(s32[32,1,2]{2,1,0:T(1,128)} %broadcast_in_dim.9), calls=%async_computation | async-start | bytes 32768 | tf_op jit(solution)/shard_map/all_to_all | solution.py:292
  56.4 7.2 %copy-start.2 = (bf16[2,4096,96]{1,2,0:T(8,128)(2,1)S(1)}, bf16[2,4096,96]{1,2,0:T(8,128)(2,1)}, u32[]{:S(2)}) copy-start(bf16[2,4096,96]{1,2,0:T(8,128)(2,1)} %param.24) | copy-start | bytes 4718596
  56.4 78.8 %all-to-all-start.1 = ((bf16[32,2,2,128,96]{3,4,2,1,0:T(8,128)(2,1)}), bf16[32,2,2,128,96]{3,4,2,1,0:T(8,128)(2,1)}, u32[]{:S(2)}, u32[]{:S(2)}) async-start(bf16[32,2,2,128,96]{3,4,2,1,0:T(8,128)(2,1)} %broadcast_select_fusion), calls=%async_computation.1 | async-start | bytes 6291456 | tf_op jit(solution)/shard_map/all_to_all | solution.py:297
  63.6 6.5 %copy-start.11 = (s32[2]{0:T(128)S(1)}, s32[2]{0:T(128)}, u32[]{:S(2)}) copy-start(s32[2]{0:T(128)} %length_ref.3) | copy-start | bytes 28
  63.6 174.4 %reduce-scatter.3.cloned.1.call-start = ((), (), s32[]{:S(2)}) async-start(), calls=%async_computation.5 | async-start | bytes 3932160 | tf_op jit(solution)/shard_map/reduce_scatter | solution.py:283
  70.9 16.7 %copy-start.9 = (bf16[1536,192]{0,1:T(8,128)(2,1)S(1)}, bf16[1536,192]{0,1:T(8,128)(2,1)}, u32[]{:S(2)}) copy-start(bf16[1536,192]{0,1:T(8,128)(2,1)} %param.20) | copy-start | bytes 1769476
  90.7 1.6 copy-start.10
  141.4 47.9 %copy-start.3 = (bf16[192,1536]{1,0:T(8,128)(2,1)S(1)}, bf16[192,1536]{1,0:T(8,128)(2,1)}, u32[]{:S(2)}) copy-start(bf16[192,1536]{1,0:T(8,128)(2,1)} %param.23) | copy-start | bytes 1769476
  191.9 75.2 %copy-start.1 = (bf16[64,2,1536]{2,1,0:T(2,128)(2,1)S(1)}, bf16[64,2,1536]{2,1,0:T(2,128)(2,1)}, u32[]{:S(2)}) copy-start(bf16[64,2,1536]{2,1,0:T(2,128)(2,1)} %param.16) | copy-start | bytes 1179652
  191.9 142.1 %all-gather.5.cloned.1.call-start = ((), (), s32[]{:S(2)}) async-start(), calls=%async_computation.6 | async-start | bytes 3932160 | tf_op jit(solution)/shard_map/all_gather | solution.py:276
  192.0 75.8 %copy-start.6 = (f32[1536]{0:T(1024)S(1)}, f32[1536]{0:T(1024)}, u32[]{:S(2)}) copy-start(f32[1536]{0:T(1024)} %param.28) | copy-start | bytes 18436
  269.2 64.9 %copy-start.8 = (bf16[1536,512]{1,0:T(8,128)(2,1)S(1)}, bf16[1536,512]{1,0:T(8,128)(2,1)}, u32[]{:S(2)}) copy-start(bf16[1536,512]{1,0:T(8,128)(2,1)} %param.29) | copy-start | bytes 4718596
  290.1 98.5 %reduce-scatter.5.cloned.1.call-start = ((), (), s32[]{:S(2)}) async-start(), calls=%async_computation.7 | async-start | bytes 3932160 | tf_op jit(solution)/shard_map/reduce_scatter | solution.py:283
Sparse Core Ops, SparseCore 0:
  36.0 44.3 all-gather.2
  192.0 45.8 reduce-scatter.2
  290.2 43.8 all-gather.4
  347.4 41.0 reduce-scatter.4

commit v7 on v6

--- a/solution.py
+++ b/solution.py
@@ -269,11 +269,22 @@
     )(piece)
 
 
-def gather_rows(piece, call_id):
+def pair_rows(piece, call_id):
     upper = lax.axis_index("zh") == 1
     other = exchange(piece, call_id)
-    pair = jnp.stack([jnp.where(upper, other, piece), jnp.where(upper, piece, other)])
-    return lax.all_gather(pair, "y", axis=0, tiled=True).reshape((-1,) + piece.shape[1:])
+    return jnp.stack([jnp.where(upper, other, piece), jnp.where(upper, piece, other)])
+
+
+def gather_rows(pair):
+    return lax.all_gather(pair, "y", axis=0, tiled=True).reshape((-1,) + pair.shape[2:])
+
+
+def reduce_rows(full, call_id):
+    y_size = lax.axis_size("y")
+    zh_size = lax.axis_size("zh")
+    split = full.reshape((y_size * zh_size, full.shape[0] // (y_size * zh_size)) + full.shape[1:])
+    part = lax.psum_scatter(split, "y", scatter_dimension=0, tiled=True)
+    return part.astype(jnp.float32) + exchange(part, call_id).astype(jnp.float32)
 
 
 def scatter_rows(full, call_id):
@@ -323,9 +334,10 @@
     key_heads = key_cols // HEAD_SIZE
     query_group_width = query_cols // key_cols
     score_scale = 1.0 / math.sqrt(HEAD_SIZE)
-    source = norm_rows(tokens, attn_gain).reshape(local_rows * local_reqs, MODEL_WIDTH)
+    token_pair = pair_rows(tokens.reshape(local_rows * local_reqs, MODEL_WIDTH), 0)
+    source = norm_rows(token_pair, attn_gain)
     offset = 0
-    flattened_rows = gather_rows(source, 0)
+    flattened_rows = gather_rows(source)
     row_count = flattened_rows.shape[0] // local_reqs
     y_size = lax.axis_size("y")
     zh_size = lax.axis_size("zh")
@@ -382,18 +394,19 @@
         .reshape(row_count, local_reqs, query_cols)
     )
     picked = attended
-    attn_part = scatter_rows(
+    attn_pair = reduce_rows(
         jnp.dot(
             picked.reshape(FRESH_TOKENS * local_reqs, query_cols),
             w_out,
             preferred_element_type=jnp.float32,
         ).astype(jnp.bfloat16),
         1,
+    )
+    residual_pair = (token_pair.astype(jnp.float32) + attn_pair).astype(jnp.bfloat16)
+    residual = lax.dynamic_index_in_dim(
+        residual_pair, lax.axis_index("zh"), 0, keepdims=False
     ).reshape(tokens.shape)
-    residual = (tokens.astype(jnp.float32) + attn_part).astype(jnp.bfloat16)
-    flattened_rows = gather_rows(
-        norm_rows(residual, mlp_gain).reshape(local_rows * local_reqs, MODEL_WIDTH), 2
-    )
+    flattened_rows = gather_rows(norm_rows(residual_pair, mlp_gain))
     gate_part = jnp.dot(flattened_rows, w_gate, preferred_element_type=jnp.float32)
     up_part = jnp.dot(flattened_rows, w_up, preferred_element_type=jnp.float32)
     hidden = (jax.nn.silu(gate_part) * up_part).astype(jnp.bfloat16)

time: 425 us -> 422 us (level)
  waiting for transfers between devices: 146 us -> 136 us
  local copies, waits for them, and re-layouts: 37.2 us -> 45.9 us
    reduce_scatter x2 -> x1, waiting for transfers between devices: 87.2 us -> 40.7 us  [scatter_rows(): part = lax.psum_scatter(split, 'y', scatter_dimension=0, tiled=True)]
    reduce_scatter x0 -> x1, waiting for transfers between devices: none -> 39.7 us  [reduce_rows(): part = lax.psum_scatter(split, 'y', scatter_dimension=0, tiled=True)]
    concatenate x8, local copies, waits for them, and re-layouts: 2.04 us -> 10.1 us  [rotate(): jnp.concatenate([first_half * cosine - second_half * sine_part, second_ha...]
    pallas_call x4 -> x3, Pallas kernels: 89 us -> 87.1 us  [exchange(): pl.pallas_call(exchange_kernel, out_shape=jax.ShapeDtypeStruct(piece.shap...]
  transfers between devices with their start and end apart: 6 -> 6, of which waited for: 5 -> 5; matrix products, arithmetic and copies ran while one was open for 9% -> 13% of each run, Pallas kernels for 7% -> 8%
where the time goes in v7:
time: 422 us; the launch traced here: 420 us
  Pallas kernels  164 us (39%)
  waiting for transfers between devices  136 us (32%)
  local copies, waits for them, and re-layouts  45.9 us (11%)
  matrix products  27.1 us (6%)
  other arithmetic  19.4 us (5%)
  starting transfers between devices  14.9 us (4%)
  between operations  13.4 us (3%)
    pallas_call x3, Pallas kernels, exchange(): pl.pallas_call(exchange_kernel, out_shape=jax.ShapeDtypeStruct(piece.shap...  87.1 us
    all_gather x2, waiting for transfers between devices, gather_rows(): lax.all_gather(pair, 'y', axis=0, tiled=True)  50.3 us
    pallas_call x1, Pallas kernels, attention(): pl.pallas_call(prompt_kernel, grid_spec=pltpu.PrefetchScalarGridSpec(num_...  43.8 us
    reduce_scatter x1, waiting for transfers between devices, scatter_rows(): part = lax.psum_scatter(split, 'y', scatter_dimension=0, tiled=True)  40.7 us
    reduce_scatter x1, waiting for transfers between devices, reduce_rows(): part = lax.psum_scatter(split, 'y', scatter_dimension=0, tiled=True)  39.7 us
    pallas_call x1, Pallas kernels, attention(): pl.pallas_call(recent_kernel, grid_spec=pltpu.PrefetchScalarGridSpec(num_...  33 us
    concatenate x8, local copies, waits for them, and re-layouts, rotate(): jnp.concatenate([first_half * cosine - second_half * sine_part, second_ha...  10.1 us
  transfers between devices with their start and end apart: 6, of which 5 were waited for; matrix products, arithmetic and copies ran while one was open for 13% of the time, Pallas kernels for 8%

profile of v7, /device:TPU:65, one launch (start us, length us, event | category | flops | bytes accessed | tf_op | source)
XLA Modules:
  0.0 420.4 jit_solution(14201030225826599435)
XLA Ops:
  8.6 23.1 %shard_map.154 = bf16[128,1536]{1,0:T(8,128)(2,1)} custom-call(bf16[128,1536]{1,0:T(8,128)(2,1)} %reshape.214.piece_ref), custom_call_target="tpu_custom_call" | custom-call | tf_op jit(solution)/shard_map/pallas_call | solution.py:262
  34.9 7.8 %all-to-all-start = ((s32[32,1,2]{2,1,0:T(1,128)}), s32[32,1,2]{2,1,0:T(1,128)S(1)}, u32[]{:S(2)}, u32[]{:S(2)}) async-start(s32[32,1,2]{2,1,0:T(1,128)} %broadcast_in_dim.9), calls=%async_computation | async-start | bytes 32768 | tf_op jit(solution)/shard_map/all_to_all | solution.py:303
  42.8 5.1 %all-to-all-done = s32[32,1,2]{2,1,0:T(1,128)S(1)} async-done(((s32[32,1,2]{2,1,0:T(1,128)}), s32[32,1,2]{2,1,0:T(1,128)S(1)}, u32[]{:S(2)}, u32[]{:S(2)}) %all-to-all-start) | async-done | bytes 288 | tf_op jit(solution)/shard_map/all_to_all | solution.py:303
  48.3 2.6 gather_fusion
  50.9 4.0 broadcast_select_fusion
  54.9 7.0 %all-to-all-start.1 = ((bf16[32,2,2,128,96]{3,4,2,1,0:T(8,128)(2,1)}), bf16[32,2,2,128,96]{3,4,2,1,0:T(8,128)(2,1)}, u32[]{:S(2)}, u32[]{:S(2)}) async-start(bf16[32,2,2,128,96]{3,4,2,1,0:T(8,128)(2,1)} %broadcast_select_fusion), calls=%async_computation.1 | async-start | bytes 6291456 | tf_op jit(solution)/shard_map/all_to_all | solution.py:308
  62.0 3.9 copy.70.wk_ref
  65.9 3.9 copy.71.wv_ref
  70.6 8.2 %all-gather.3.cloned.1.call-done = bf16[8,128,1536]{2,1,0:T(8,128)(2,1)} async-done(((bf16[2,128,1536]{2,1,0:T(8,128)(2,1)}), bf16[8,128,1536]{2,1,0:T(8,128)(2,1)}) %all-gather.3.cloned.1.call-update) | async-done | bytes 3145744 | tf_op jit(solution)/shard_map/all_gather | solution.py:279
  78.9 7.2 %dot_general.29 = bf16[512,2,1536]{2,1,0:T(2,128)(2,1)} reshape(bf16[8,128,1536]{2,1,0:T(8,128)(2,1)} %all-gather.3.cloned.1.call-done) | data formatting | bytes 6291456 | tf_op jit(solution)/shard_map/dot_general | solution.py:351
  86.1 3.1 fusion
  94.0 3.0 fusion.11
  104.6 3.7 convolution_convert_fusion.2
  114.7 33.0 %shard_map.155 = (f32[2,1024,96]{2,1,0:T(8,128)}, f32[2,1024,1]{2,1,0:T(8,128)}, f32[2,1024,1]{2,1,0:T(8,128)}) custom-call(s32[2]{0:T(128)} %length_ref.3, bf16[2,1024,96]{2,1,0:T(8,128)(2,1)} %bitcast.80, bf16[2,4096,96]{2,1,0:T(8,128)(2,1)} %copy.70.wk_ref, bf16[2,4096,96]{2,1,0:T(8,128)(2,1)} %copy.71.wv_ref, bf16[2,512,96]{2,1,0:T(8,128)(2,1)} %bitcast.83, ...), custom_call_target="tpu_custom_call" | custom-call | flops 3623878656 | bytes 3538944 | tf_op jit(solution)/shard_map/pallas_call | solution.py:177
  147.7 6.2 %copy.72.pk_ref.pv_ref = bf16[32,2,2,128,96]{4,3,2,1,0:T(8,128)(2,1)} copy(bf16[32,2,2,128,96]{3,4,2,1,0:T(8,128)(2,1)} %all-to-all-done.1) | data formatting | bytes 6291456 | tf_op jit(solution)/shard_map/all_to_all | solution.py:308
  153.9 43.8 %shard_map.156 = bf16[2,1024,96]{2,1,0:T(8,128)(2,1)} custom-call(s32[2]{0:T(128)} %length_ref.3, bf16[2,1024,96]{2,1,0:T(8,128)(2,1)} %bitcast.81, bf16[32,2,2,128,96]{4,3,2,1,0:T(8,128)(2,1)} %copy.72.pk_ref.pv_ref, bf16[32,2,2,128,96]{4,3,2,1,0:T(8,128)(2,1)} %copy.72.pk_ref.pv_ref, f32[2,1024,96]{2,1,0:T(8,128)} %get-tuple-element.8.acc_in, ...), custom_call_target="tpu_custom_call" | custom-call | flops 3221225472 | bytes 3145728 | tf_op jit(solution)/shard_map/pallas_call | solution.py:211
  199.6 3.7 convolution_convert_fusion
  203.4 39.7 %reduce-scatter.3.cloned.1.call-done.piece_ref = bf16[2,128,1536]{2,1,0:T(8,128)(2,1)} async-done(((bf16[8,128,1536]{2,1,0:T(8,128)(2,1)}), bf16[2,128,1536]{2,1,0:T(8,128)(2,1)}) %reduce-scatter.3.cloned.1.call-update) | async-done | bytes 786448 | tf_op jit(solution)/shard_map/reduce_scatter | solution.py:286
  243.1 40.4 %shard_map.157 = bf16[2,128,1536]{2,1,0:T(8,128)(2,1)} custom-call(bf16[2,128,1536]{2,1,0:T(8,128)(2,1)} %reduce-scatter.3.cloned.1.call-done.piece_ref), custom_call_target="tpu_custom_call" | custom-call | tf_op jit(solution)/shard_map/pallas_call | solution.py:262
  286.6 42.0 %all-gather.5.cloned.1.call-done = bf16[8,128,1536]{2,1,0:T(8,128)(2,1)} async-done(((bf16[2,128,1536]{2,1,0:T(8,128)(2,1)}), bf16[8,128,1536]{2,1,0:T(8,128)(2,1)}) %all-gather.5.cloned.1.call-update) | async-done | bytes 3145744 | tf_op jit(solution)/shard_map/all_gather | solution.py:279
  328.6 5.5 %fusion.38 = f32[1024,512]{1,0:T(8,128)} fusion(bf16[1024,1536]{1,0:T(8,128)(2,1)} %bitcast.87, bf16[1536,512]{1,0:T(8,128)(2,1)} %param.29), kind=kOutput, calls=%fused_computation.82 | convolution fusion | flops 1610612736 | bytes 6815744 | tf_op jit(solution)/shard_map/dot_general | solution.py:410
  334.1 8.2 %convolution_convert_fusion.1 = bf16[1024,1536]{1,0:T(8,128)(2,1)} fusion(bf16[512,1536]{1,0:T(8,128)(2,1)S(1)} %copy-done, f32[1024,512]{1,0:T(8,128)} %fusion.38, bf16[1024,1536]{1,0:T(8,128)(2,1)} %bitcast.88, bf16[1536,512]{1,0:T(8,128)(2,1)} %param.30), kind=kOutput, calls=%fused_computation.2 | convolution fusion | flops 3225944064 | bytes 11534336 | tf_op jit(solution)/shard_map/dot_general | solution.py:414
  342.9 40.7 %reduce-scatter.5.cloned.1.call-done = bf16[2,128,1536]{2,1,0:T(8,128)(2,1)} async-done(((bf16[8,128,1536]{2,1,0:T(8,128)(2,1)}), bf16[2,128,1536]{2,1,0:T(8,128)(2,1)}) %reduce-scatter.5.cloned.1.call-update) | async-done | bytes 786448 | tf_op jit(solution)/shard_map/reduce_scatter | solution.py:294
  385.4 23.6 %shard_map.158 = bf16[128,1536]{1,0:T(8,128)(2,1)} custom-call(bf16[128,1536]{1,0:T(8,128)(2,1)} %dynamic-slice_bitcast_fusion.piece_ref), custom_call_target="tpu_custom_call" | custom-call | tf_op jit(solution)/shard_map/pallas_call | solution.py:262
  (69 shorter events, 37.7 us)
Async XLA Ops:
  6.5 327.6 %copy-start = (bf16[512,1536]{1,0:T(8,128)(2,1)S(1)}, bf16[512,1536]{1,0:T(8,128)(2,1)}, u32[]{:S(2)}) copy-start(bf16[512,1536]{1,0:T(8,128)(2,1)} %param.31) | copy-start | bytes 4718596
  6.5 26.6 %copy-start.3 = (f32[1536]{0:T(1024)S(1)}, f32[1536]{0:T(1024)}, u32[]{:S(2)}) copy-start(f32[1536]{0:T(1024)} %param.19) | copy-start | bytes 18436
  6.5 72.3 %all-gather.3.cloned.1.call-start = ((), (), s32[]{:S(2)}) async-start(), calls=%async_computation.4 | async-start | bytes 3932160 | tf_op jit(solution)/shard_map/all_gather | solution.py:279
  31.6 2.7 copy-start.5
  31.6 11.1 %copy-start.1 = (bf16[8,128,96]{1,2,0:T(8,128)(2,1)S(1)}, bf16[8,128,96]{1,2,0:T(8,128)(2,1)}, u32[]{:S(2)}) copy-start(bf16[8,128,96]{1,2,0:T(8,128)(2,1)} %param.27) | copy-start | bytes 589828
  31.6 11.1 %copy-start.2 = (bf16[8,128,96]{1,2,0:T(8,128)(2,1)S(1)}, bf16[8,128,96]{1,2,0:T(8,128)(2,1)}, u32[]{:S(2)}) copy-start(bf16[8,128,96]{1,2,0:T(8,128)(2,1)} %param.26) | copy-start | bytes 589828
  34.9 12.9 %all-to-all-start = ((s32[32,1,2]{2,1,0:T(1,128)}), s32[32,1,2]{2,1,0:T(1,128)S(1)}, u32[]{:S(2)}, u32[]{:S(2)}) async-start(s32[32,1,2]{2,1,0:T(1,128)} %broadcast_in_dim.9), calls=%async_computation | async-start | bytes 32768 | tf_op jit(solution)/shard_map/all_to_all | solution.py:303
  54.9 92.8 %all-to-all-start.1 = ((bf16[32,2,2,128,96]{3,4,2,1,0:T(8,128)(2,1)}), bf16[32,2,2,128,96]{3,4,2,1,0:T(8,128)(2,1)}, u32[]{:S(2)}, u32[]{:S(2)}) async-start(bf16[32,2,2,128,96]{3,4,2,1,0:T(8,128)(2,1)} %broadcast_select_fusion), calls=%async_computation.1 | async-start | bytes 6291456 | tf_op jit(solution)/shard_map/all_to_all | solution.py:308
  61.9 181.2 %reduce-scatter.3.cloned.1.call-start = ((), (), s32[]{:S(2)}) async-start(), calls=%async_computation.5 | async-start | bytes 3932160 | tf_op jit(solution)/shard_map/reduce_scatter | solution.py:286
  65.9 3.9 copy-start.7
  70.6 15.5 %copy-start.6 = (bf16[1536,192]{0,1:T(8,128)(2,1)S(1)}, bf16[1536,192]{0,1:T(8,128)(2,1)}, u32[]{:S(2)}) copy-start(bf16[1536,192]{0,1:T(8,128)(2,1)} %param.20) | copy-start | bytes 1769476
  203.3 82.1 %copy-start.4 = (f32[1536]{0:T(1024)S(1)}, f32[1536]{0:T(1024)}, u32[]{:S(2)}) copy-start(f32[1536]{0:T(1024)} %param.28) | copy-start | bytes 18436
  203.3 125.3 %all-gather.5.cloned.1.call-start = ((), (), s32[]{:S(2)}) async-start(), calls=%async_computation.6 | async-start | bytes 3932160 | tf_op jit(solution)/shard_map/all_gather | solution.py:279
  286.6 97.0 %reduce-scatter.5.cloned.1.call-start = ((), (), s32[]{:S(2)}) async-start(), calls=%async_computation.7 | async-start | bytes 3932160 | tf_op jit(solution)/shard_map/reduce_scatter | solution.py:294
Sparse Core Ops, SparseCore 0:
  34.4 44.3 all-gather.2
  203.4 39.6 reduce-scatter.2
  286.7 41.9 all-gather.4
  342.5 41.0 reduce-scatter.4

commit v8 on v7

--- a/solution.py
+++ b/solution.py
@@ -393,27 +393,38 @@
         .transpose(3, 2, 4, 0, 1, 5)
         .reshape(row_count, local_reqs, query_cols)
     )
-    picked = attended
-    attn_pair = reduce_rows(
-        jnp.dot(
-            picked.reshape(FRESH_TOKENS * local_reqs, query_cols),
-            w_out,
-            preferred_element_type=jnp.float32,
-        ).astype(jnp.bfloat16),
-        1,
-    )
-    residual_pair = (token_pair.astype(jnp.float32) + attn_pair).astype(jnp.bfloat16)
-    residual = lax.dynamic_index_in_dim(
-        residual_pair, lax.axis_index("zh"), 0, keepdims=False
-    ).reshape(tokens.shape)
-    flattened_rows = gather_rows(norm_rows(residual_pair, mlp_gain))
-    gate_part = jnp.dot(flattened_rows, w_gate, preferred_element_type=jnp.float32)
-    up_part = jnp.dot(flattened_rows, w_up, preferred_element_type=jnp.float32)
-    hidden = (jax.nn.silu(gate_part) * up_part).astype(jnp.bfloat16)
-    mlp_part = scatter_rows(
-        jnp.dot(hidden, w_down, preferred_element_type=jnp.float32).astype(jnp.bfloat16),
-        3,
-    ).reshape(tokens.shape)
+    blocks = lax.axis_size("y") * lax.axis_size("zh")
+    block_rows = local_rows * local_reqs
+    chunks = 2
+    chunk_rows = block_rows // chunks
+    rows_by_block = attended.reshape(blocks, block_rows, query_cols)
+    residual_parts = []
+    mlp_parts = []
+    for chunk in range(chunks):
+        picked = rows_by_block[:, chunk * chunk_rows : (chunk + 1) * chunk_rows].reshape(
+            blocks * chunk_rows, query_cols
+        )
+        attn_pair = reduce_rows(
+            jnp.dot(picked, w_out, preferred_element_type=jnp.float32).astype(jnp.bfloat16),
+            1 + chunk,
+        )
+        token_chunk = token_pair[:, chunk * chunk_rows : (chunk + 1) * chunk_rows]
+        residual_pair = (token_chunk.astype(jnp.float32) + attn_pair).astype(jnp.bfloat16)
+        residual_parts.append(
+            lax.dynamic_index_in_dim(residual_pair, lax.axis_index("zh"), 0, keepdims=False)
+        )
+        flattened_rows = gather_rows(norm_rows(residual_pair, mlp_gain))
+        gate_part = jnp.dot(flattened_rows, w_gate, preferred_element_type=jnp.float32)
+        up_part = jnp.dot(flattened_rows, w_up, preferred_element_type=jnp.float32)
+        hidden = (jax.nn.silu(gate_part) * up_part).astype(jnp.bfloat16)
+        mlp_parts.append(
+            scatter_rows(
+                jnp.dot(hidden, w_down, preferred_element_type=jnp.float32).astype(jnp.bfloat16),
+                1 + chunks + chunk,
+            )
+        )
+    residual = jnp.concatenate(residual_parts, axis=0).reshape(tokens.shape)
+    mlp_part = jnp.concatenate(mlp_parts, axis=0).reshape(tokens.shape)
     return (residual.astype(jnp.float32) + mlp_part).astype(jnp.bfloat16)
 
 

time: 422 us -> 439 us (1.040)
  Pallas kernels: 164 us -> 172 us
    pallas_call x3 -> x5, Pallas kernels: 87.1 us -> 101 us  [exchange(): pl.pallas_call(exchange_kernel, out_shape=jax.ShapeDtypeStruct(piece.shap...]
    pallas_call x1, Pallas kernels: 33 us -> 20.5 us  [attention(): pl.pallas_call(recent_kernel, grid_spec=pltpu.PrefetchScalarGridSpec(num_...]
    all_gather x2 -> x3, waiting for transfers between devices: 50.3 us -> 58.9 us  [gather_rows(): lax.all_gather(pair, 'y', axis=0, tiled=True)]
    pallas_call x1, Pallas kernels: 43.8 us -> 50.6 us  [attention(): pl.pallas_call(prompt_kernel, grid_spec=pltpu.PrefetchScalarGridSpec(num_...]
    reduce_scatter x1 -> x2, waiting for transfers between devices: 40.7 us -> 34.4 us  [scatter_rows(): part = lax.psum_scatter(split, 'y', scatter_dimension=0, tiled=True)]
    dot_general x1 -> x2, matrix products: 8.19 us -> 10.4 us  [body(): jnp.dot(hidden, w_down, preferred_element_type=jnp.float32)]
    reduce_scatter x1 -> x2, waiting for transfers between devices: 39.7 us -> 40.2 us  [reduce_rows(): part = lax.psum_scatter(split, 'y', scatter_dimension=0, tiled=True)]
  transfers between devices with their start and end apart: 6 -> 9, of which waited for: 5 -> 8; matrix products, arithmetic and copies ran while one was open for 13% -> 17% of each run, Pallas kernels for 8% -> 14%
where the time goes in v8:
time: 439 us; the launch traced here: 438 us
  Pallas kernels  172 us (39%)
  waiting for transfers between devices  139 us (32%)
  local copies, waits for them, and re-layouts  49.2 us (11%)
  matrix products  31.3 us (7%)
  other arithmetic  17.5 us (4%)
  starting transfers between devices  15 us (3%)
  between operations  13.8 us (3%)
    pallas_call x5, Pallas kernels, exchange(): pl.pallas_call(exchange_kernel, out_shape=jax.ShapeDtypeStruct(piece.shap...  101 us
    all_gather x3, waiting for transfers between devices, gather_rows(): lax.all_gather(pair, 'y', axis=0, tiled=True)  58.9 us
    pallas_call x1, Pallas kernels, attention(): pl.pallas_call(prompt_kernel, grid_spec=pltpu.PrefetchScalarGridSpec(num_...  50.6 us
    reduce_scatter x2, waiting for transfers between devices, reduce_rows(): part = lax.psum_scatter(split, 'y', scatter_dimension=0, tiled=True)  40.2 us
    reduce_scatter x2, waiting for transfers between devices, scatter_rows(): part = lax.psum_scatter(split, 'y', scatter_dimension=0, tiled=True)  34.4 us
    pallas_call x1, Pallas kernels, attention(): pl.pallas_call(recent_kernel, grid_spec=pltpu.PrefetchScalarGridSpec(num_...  20.5 us
    dot_general x2, matrix products, body(): jnp.dot(hidden, w_down, preferred_element_type=jnp.float32)  10.4 us
    concatenate x8, local copies, waits for them, and re-layouts, rotate(): jnp.concatenate([first_half * cosine - second_half * sine_part, second_ha...  10.1 us
  transfers between devices with their start and end apart: 9, of which 8 were waited for; matrix products, arithmetic and copies ran while one was open for 17% of the time, Pallas kernels for 14%

profile of v8, /device:TPU:65, one launch (start us, length us, event | category | flops | bytes accessed | tf_op | source)
XLA Modules:
  0.0 438.0 jit_solution(12060346434749427612)
XLA Ops:
  8.5 23.1 %shard_map.154 = bf16[128,1536]{1,0:T(8,128)(2,1)} custom-call(bf16[128,1536]{1,0:T(8,128)(2,1)} %reshape.237.piece_ref), custom_call_target="tpu_custom_call" | custom-call | tf_op jit(solution)/shard_map/pallas_call | solution.py:262
  34.8 7.8 %all-to-all-start = ((s32[32,1,2]{2,1,0:T(1,128)}), s32[32,1,2]{2,1,0:T(1,128)S(1)}, u32[]{:S(2)}, u32[]{:S(2)}) async-start(s32[32,1,2]{2,1,0:T(1,128)} %broadcast_in_dim.9), calls=%async_computation | async-start | bytes 32768 | tf_op jit(solution)/shard_map/all_to_all | solution.py:303
  42.7 5.1 %all-to-all-done = s32[32,1,2]{2,1,0:T(1,128)S(1)} async-done(((s32[32,1,2]{2,1,0:T(1,128)}), s32[32,1,2]{2,1,0:T(1,128)S(1)}, u32[]{:S(2)}, u32[]{:S(2)}) %all-to-all-start) | async-done | bytes 288 | tf_op jit(solution)/shard_map/all_to_all | solution.py:303
  50.8 4.0 broadcast_select_fusion
  54.8 7.0 %all-to-all-start.1 = ((bf16[32,2,2,128,96]{3,4,2,1,0:T(8,128)(2,1)}), bf16[32,2,2,128,96]{3,4,2,1,0:T(8,128)(2,1)}, u32[]{:S(2)}, u32[]{:S(2)}) async-start(bf16[32,2,2,128,96]{3,4,2,1,0:T(8,128)(2,1)} %broadcast_select_fusion), calls=%async_computation.1 | async-start | bytes 6291456 | tf_op jit(solution)/shard_map/all_to_all | solution.py:308
  61.9 3.9 copy.70.wk_ref
  70.5 8.3 %all-gather.4.cloned.1.call-done = bf16[8,128,1536]{2,1,0:T(8,128)(2,1)} async-done(((bf16[2,128,1536]{2,1,0:T(8,128)(2,1)}), bf16[8,128,1536]{2,1,0:T(8,128)(2,1)}) %all-gather.4.cloned.1.call-update) | async-done | bytes 3145744 | tf_op jit(solution)/shard_map/all_gather | solution.py:279
  78.8 7.2 %dot_general.41 = bf16[512,2,1536]{2,1,0:T(2,128)(2,1)} reshape(bf16[8,128,1536]{2,1,0:T(8,128)(2,1)} %all-gather.4.cloned.1.call-done) | data formatting | bytes 6291456 | tf_op jit(solution)/shard_map/dot_general | solution.py:351
  114.6 20.5 %shard_map.155 = (f32[2,1024,96]{2,1,0:T(8,128)}, f32[2,1024,1]{2,1,0:T(8,128)}, f32[2,1024,1]{2,1,0:T(8,128)}) custom-call(s32[2]{0:T(128)} %length_ref.3, bf16[2,1024,96]{2,1,0:T(8,128)(2,1)} %bitcast.105, bf16[2,4096,96]{2,1,0:T(8,128)(2,1)} %copy.70.wk_ref, bf16[2,4096,96]{2,1,0:T(8,128)(2,1)} %copy.71.wv_ref, bf16[2,512,96]{2,1,0:T(8,128)(2,1)} %bitcast.108, ...), custom_call_target="tpu_custom_call" | custom-call | flops 3623878656 | bytes 3538944 | tf_op jit(solution)/shard_map/pallas_call | solution.py:177
  135.1 6.2 %copy.72.pk_ref.pv_ref = bf16[32,2,2,128,96]{4,3,2,1,0:T(8,128)(2,1)} copy(bf16[32,2,2,128,96]{3,4,2,1,0:T(8,128)(2,1)} %all-to-all-done.1) | data formatting | bytes 6291456 | tf_op jit(solution)/shard_map/all_to_all | solution.py:308
  141.3 50.6 %shard_map.156 = bf16[2,1024,96]{2,1,0:T(8,128)(2,1)} custom-call(s32[2]{0:T(128)} %length_ref.3, bf16[2,1024,96]{2,1,0:T(8,128)(2,1)} %bitcast.106, bf16[32,2,2,128,96]{4,3,2,1,0:T(8,128)(2,1)} %copy.72.pk_ref.pv_ref, bf16[32,2,2,128,96]{4,3,2,1,0:T(8,128)(2,1)} %copy.72.pk_ref.pv_ref, f32[2,1024,96]{2,1,0:T(8,128)} %get-tuple-element.8.acc_in, ...), custom_call_target="tpu_custom_call" | custom-call | flops 3221225472 | bytes 3145728 | tf_op jit(solution)/shard_map/pallas_call | solution.py:211
  200.1 33.3 %reduce-scatter.5.cloned.1.call-done.piece_ref = bf16[2,64,1536]{2,1,0:T(8,128)(2,1)} async-done(((bf16[8,64,1536]{2,1,0:T(8,128)(2,1)}), bf16[2,64,1536]{2,1,0:T(8,128)(2,1)}) %reduce-scatter.5.cloned.1.call-update) | async-done | bytes 393232 | tf_op jit(solution)/shard_map/reduce_scatter | solution.py:286
  233.4 23.7 %shard_map.157 = bf16[2,64,1536]{2,1,0:T(8,128)(2,1)} custom-call(bf16[2,64,1536]{2,1,0:T(8,128)(2,1)} %reduce-scatter.5.cloned.1.call-done.piece_ref), custom_call_target="tpu_custom_call" | custom-call | tf_op jit(solution)/shard_map/pallas_call | solution.py:262
  257.1 6.9 %reduce-scatter.7.cloned.1.call-done.piece_ref = bf16[2,64,1536]{2,1,0:T(8,128)(2,1)} async-done(((bf16[8,64,1536]{2,1,0:T(8,128)(2,1)}), bf16[2,64,1536]{2,1,0:T(8,128)(2,1)}) %reduce-scatter.7.cloned.1.call-update) | async-done | bytes 393232 | tf_op jit(solution)/shard_map/reduce_scatter | solution.py:286
  264.0 23.7 %shard_map.158 = bf16[2,64,1536]{2,1,0:T(8,128)(2,1)} custom-call(bf16[2,64,1536]{2,1,0:T(8,128)(2,1)} %reduce-scatter.7.cloned.1.call-done.piece_ref), custom_call_target="tpu_custom_call" | custom-call | tf_op jit(solution)/shard_map/pallas_call | solution.py:262
  291.1 29.0 %all-gather.6.cloned.1.call-done = bf16[8,64,1536]{2,1,0:T(8,128)(2,1)} async-done(((bf16[2,64,1536]{2,1,0:T(8,128)(2,1)}), bf16[8,64,1536]{2,1,0:T(8,128)(2,1)}) %all-gather.6.cloned.1.call-update) | async-done | bytes 1572880 | tf_op jit(solution)/shard_map/all_gather | solution.py:279
  323.9 5.2 %convolution_convert_fusion.1 = bf16[512,1536]{1,0:T(8,128)(2,1)} fusion(bf16[512,1536]{1,0:T(8,128)(2,1)S(1)} %copy-done, bf16[512,1536]{1,0:T(8,128)(2,1)} %bitcast.115, bf16[1536,512]{1,0:T(8,128)(2,1)} %param.30, f32[512,512]{1,0:T(8,128)} %fusion.48), kind=kOutput, calls=%fused_computation.7 | convolution fusion | flops 1612972032 | bytes 7340032 | tf_op jit(solution)/shard_map/dot_general | solution.py:422
  329.2 21.7 %all-gather.8.cloned.1.call-done = bf16[8,64,1536]{2,1,0:T(8,128)(2,1)} async-done(((bf16[2,64,1536]{2,1,0:T(8,128)(2,1)}), bf16[8,64,1536]{2,1,0:T(8,128)(2,1)}) %all-gather.8.cloned.1.call-update) | async-done | bytes 1572880 | tf_op jit(solution)/shard_map/all_gather | solution.py:279
  350.9 3.9 fusion.49
  354.8 5.2 %convolution_convert_fusion = bf16[512,1536]{1,0:T(8,128)(2,1)} fusion(bf16[512,1536]{1,0:T(8,128)(2,1)S(1)} %copy-done, bf16[512,1536]{1,0:T(8,128)(2,1)} %bitcast.113, bf16[1536,512]{1,0:T(8,128)(2,1)} %param.30, f32[512,512]{1,0:T(8,128)} %fusion.49), kind=kOutput, calls=%fused_computation.6 | convolution fusion | flops 1612972032 | bytes 7340032 | tf_op jit(solution)/shard_map/dot_general | solution.py:422
  360.1 20.7 %reduce-scatter.9.cloned.1.call-done = bf16[2,64,1536]{2,1,0:T(8,128)(2,1)} async-done(((bf16[8,64,1536]{2,1,0:T(8,128)(2,1)}), bf16[2,64,1536]{2,1,0:T(8,128)(2,1)}) %reduce-scatter.9.cloned.1.call-update) | async-done | bytes 393232 | tf_op jit(solution)/shard_map/reduce_scatter | solution.py:294
  382.4 15.2 %shard_map.159 = bf16[64,1536]{1,0:T(8,128)(2,1)} custom-call(bf16[64,1536]{1,0:T(8,128)(2,1)} %dynamic-slice_bitcast_fusion.1.piece_ref), custom_call_target="tpu_custom_call" | custom-call | tf_op jit(solution)/shard_map/pallas_call | solution.py:262
  397.6 13.7 %reduce-scatter.11.cloned.1.call-done = bf16[2,64,1536]{2,1,0:T(8,128)(2,1)} async-done(((bf16[8,64,1536]{2,1,0:T(8,128)(2,1)}), bf16[2,64,1536]{2,1,0:T(8,128)(2,1)}) %reduce-scatter.11.cloned.1.call-update) | async-done | bytes 393232 | tf_op jit(solution)/shard_map/reduce_scatter | solution.py:294
  413.0 15.2 %shard_map.160 = bf16[64,1536]{1,0:T(8,128)(2,1)} custom-call(bf16[64,1536]{1,0:T(8,128)(2,1)} %dynamic-slice_bitcast_fusion.piece_ref), custom_call_target="tpu_custom_call" | custom-call | tf_op jit(solution)/shard_map/pallas_call | solution.py:262
  (95 shorter events, 63.4 us)
Async XLA Ops:
  6.5 317.4 %copy-start = (bf16[512,1536]{1,0:T(8,128)(2,1)S(1)}, bf16[512,1536]{1,0:T(8,128)(2,1)}, u32[]{:S(2)}) copy-start(bf16[512,1536]{1,0:T(8,128)(2,1)} %param.31) | copy-start | bytes 4718596
  6.5 72.2 %all-gather.4.cloned.1.call-start = ((), (), s32[]{:S(2)}) async-start(), calls=%async_computation.6 | async-start | bytes 3932160 | tf_op jit(solution)/shard_map/all_gather | solution.py:279
  8.5 24.5 %copy-start.8 = (f32[1536]{0:T(1024)S(1)}, f32[1536]{0:T(1024)}, u32[]{:S(2)}) copy-start(f32[1536]{0:T(1024)} %param.19) | copy-start | bytes 18436
  32.8 1.4 copy-start.10
  32.8 9.8 %copy-start.6 = (bf16[8,128,96]{1,2,0:T(8,128)(2,1)S(1)}, bf16[8,128,96]{1,2,0:T(8,128)(2,1)}, u32[]{:S(2)}) copy-start(bf16[8,128,96]{1,2,0:T(8,128)(2,1)} %param.27) | copy-start | bytes 589828
  32.8 9.8 %copy-start.7 = (bf16[8,128,96]{1,2,0:T(8,128)(2,1)S(1)}, bf16[8,128,96]{1,2,0:T(8,128)(2,1)}, u32[]{:S(2)}) copy-start(bf16[8,128,96]{1,2,0:T(8,128)(2,1)} %param.26) | copy-start | bytes 589828
  34.8 12.9 %all-to-all-start = ((s32[32,1,2]{2,1,0:T(1,128)}), s32[32,1,2]{2,1,0:T(1,128)S(1)}, u32[]{:S(2)}, u32[]{:S(2)}) async-start(s32[32,1,2]{2,1,0:T(1,128)} %broadcast_in_dim.9), calls=%async_computation | async-start | bytes 32768 | tf_op jit(solution)/shard_map/all_to_all | solution.py:303
  54.8 80.4 %all-to-all-start.1 = ((bf16[32,2,2,128,96]{3,4,2,1,0:T(8,128)(2,1)}), bf16[32,2,2,128,96]{3,4,2,1,0:T(8,128)(2,1)}, u32[]{:S(2)}, u32[]{:S(2)}) async-start(bf16[32,2,2,128,96]{3,4,2,1,0:T(8,128)(2,1)} %broadcast_select_fusion), calls=%async_computation.1 | async-start | bytes 6291456 | tf_op jit(solution)/shard_map/all_to_all | solution.py:308
  61.8 171.5 %reduce-scatter.5.cloned.1.call-start = ((), (), s32[]{:S(2)}) async-start(), calls=%async_computation.7 | async-start | bytes 1966080 | tf_op jit(solution)/shard_map/reduce_scatter | solution.py:286
  65.8 3.9 copy-start.12
  70.5 15.5 %copy-start.11 = (bf16[1536,192]{0,1:T(8,128)(2,1)S(1)}, bf16[1536,192]{0,1:T(8,128)(2,1)}, u32[]{:S(2)}) copy-start(bf16[1536,192]{0,1:T(8,128)(2,1)} %param.20) | copy-start | bytes 1769476
  191.9 4.5 %copy-start.1 = (bf16[192,1536]{1,0:T(8,128)(2,1)S(1)}, bf16[192,1536]{1,0:T(8,128)(2,1)}, u32[]{:S(2)}) copy-start(bf16[192,1536]{1,0:T(8,128)(2,1)} %param.23) | copy-start | bytes 1769476
  196.4 1.8 copy-start.3
  198.2 65.7 %reduce-scatter.7.cloned.1.call-start = ((), (), s32[]{:S(2)}) async-start(), calls=%async_computation.8 | async-start | bytes 1966080 | tf_op jit(solution)/shard_map/reduce_scatter | solution.py:286
  200.0 120.1 %all-gather.6.cloned.1.call-start = ((), (), s32[]{:S(2)}) async-start(), calls=%async_computation.9 | async-start | bytes 1966080 | tf_op jit(solution)/shard_map/all_gather | solution.py:279
  233.4 54.3 %copy-start.2 = (bf16[2,64,1536]{2,1,0:T(8,128)(2,1)S(1)}, bf16[2,64,1536]{2,1,0:T(8,128)(2,1)}, u32[]{:S(2)}) copy-start(bf16[2,64,1536]{2,1,0:T(8,128)(2,1)} %reduce-scatter.5.cloned.1.call-done.piece_ref) | copy-start | bytes 1179652
  287.6 1.7 copy-start.9
  290.5 60.5 %all-gather.8.cloned.1.call-start = ((), (), s32[]{:S(2)}) async-start(), calls=%async_computation.11 | async-start | bytes 1966080 | tf_op jit(solution)/shard_map/all_gather | solution.py:279
  291.1 89.7 %reduce-scatter.9.cloned.1.call-start = ((), (), s32[]{:S(2)}) async-start(), calls=%async_computation.10 | async-start | bytes 1966080 | tf_op jit(solution)/shard_map/reduce_scatter | solution.py:294
  329.2 82.1 %reduce-scatter.11.cloned.1.call-start = ((), (), s32[]{:S(2)}) async-start(), calls=%async_computation.12 | async-start | bytes 1966080 | tf_op jit(solution)/shard_map/reduce_scatter | solution.py:294
  380.8 47.4 %copy-start.4 = (bf16[2,64,1536]{2,1,0:T(8,128)(2,1)S(1)}, bf16[2,64,1536]{2,1,0:T(8,128)(2,1)}, u32[]{:S(2)}) copy-start(bf16[2,64,1536]{2,1,0:T(8,128)(2,1)} %reduce-scatter.9.cloned.1.call-done) | copy-start | bytes 1179652
  411.3 17.9 %copy-start.5 = (bf16[2,64,1536]{2,1,0:T(8,128)(2,1)S(1)}, bf16[2,64,1536]{2,1,0:T(8,128)(2,1)}, u32[]{:S(2)}) copy-start(bf16[2,64,1536]{2,1,0:T(8,128)(2,1)} %reduce-scatter.11.cloned.1.call-done) | copy-start | bytes 1179652
Sparse Core Ops, SparseCore 0:
  34.3 44.3 all-gather.3
  198.3 34.9 reduce-scatter.4
  235.9 27.9 reduce-scatter.6
  290.6 29.4 all-gather.5
  321.7 29.1 all-gather.7
  353.4 27.3 reduce-scatter.8
  383.3 27.9 reduce-scatter.10

commit v9 on v7

--- a/solution.py
+++ b/solution.py
@@ -49,12 +49,12 @@
 def absorber(q_ref, peak, total, acc):
     score_scale = 1.0 / math.sqrt(HEAD_SIZE)
 
-    def absorb(keys, values, visible):
+    def absorb(keys, values, visible, flipped=False):
         scores = (
             lax.dot_general(
                 q_ref[0],
                 keys,
-                (((1,), (1,)), ((), ())),
+                (((1,), (0 if flipped else 1,)), ((), ())),
                 preferred_element_type=jnp.float32,
             )
             * score_scale
@@ -66,8 +66,11 @@
         factor = jnp.exp(old_peak - new_peak)
         weights = jnp.exp(scores - new_peak)
         total[0] = total[0] * factor + jnp.sum(weights, axis=-1, keepdims=True)
-        acc[0] = acc[0] * factor + jnp.dot(
-            weights.astype(jnp.bfloat16), values, preferred_element_type=jnp.float32
+        acc[0] = acc[0] * factor + lax.dot_general(
+            weights.astype(jnp.bfloat16),
+            values,
+            (((1,), (1 if flipped else 0,)), ((), ())),
+            preferred_element_type=jnp.float32,
         )
         peak[0] = new_peak
 
@@ -110,6 +113,13 @@
     @pl.when(block == window_blocks)
     def _():
         absorb(nk_ref[0], nv_ref[0], cols <= rows)
+
+
+def flip(block_ref):
+    pieces = block_ref.shape[0]
+    if pieces == 1:
+        return block_ref[0, 0, 0]
+    return jnp.concatenate([block_ref[piece, 0, 0] for piece in range(pieces)], axis=1)
 
 
 def prompt_kernel(
@@ -137,19 +147,11 @@
     @pl.when(((block == 0) | (prompt_start + KEY_BLOCK - 1 > length)) & jnp.logical_not(whole))
     def _():
         spot = prompt_start + cols
-        absorb(
-            pk_ref[:, 0, 0].reshape(KEY_BLOCK, HEAD_SIZE),
-            pv_ref[:, 0, 0].reshape(KEY_BLOCK, HEAD_SIZE),
-            (spot < SINKS) | (spot > length + rows),
-        )
+        absorb(flip(pk_ref), flip(pv_ref), (spot < SINKS) | (spot > length + rows), True)
 
     @pl.when(whole)
     def _():
-        absorb(
-            pk_ref[:, 0, 0].reshape(KEY_BLOCK, HEAD_SIZE),
-            pv_ref[:, 0, 0].reshape(KEY_BLOCK, HEAD_SIZE),
-            None,
-        )
+        absorb(flip(pk_ref), flip(pv_ref), None, True)
 
     @pl.when(block == prompt_blocks - 1)
     def _():
@@ -196,17 +198,18 @@
         ),
     )(lengths, queries, window_k, window_v, new_k, new_v)
 
-    source_rows = prompt_kv.shape[3]
+    prompt_kv = jnp.swapaxes(prompt_kv, 3, 4)
+    source_rows = prompt_kv.shape[4]
     if source_rows <= KEY_BLOCK:
         prompt_spec = lambda half: pl.BlockSpec(
-            (KEY_BLOCK // source_rows, 1, 1, source_rows, width),
+            (KEY_BLOCK // source_rows, 1, 1, width, source_rows),
             lambda r, b, lens: (b, r, half, 0, 0),
         )
     else:
         per_source = source_rows // KEY_BLOCK
         prompt_spec = lambda half: pl.BlockSpec(
-            (1, 1, 1, KEY_BLOCK, width),
-            lambda r, b, lens: (b // per_source, r, half, b % per_source, 0),
+            (1, 1, 1, width, KEY_BLOCK),
+            lambda r, b, lens: (b // per_source, r, half, 0, b % per_source),
         )
     return pl.pallas_call(
         prompt_kernel,

time: 422 us -> 417 us (0.988)
  waiting for transfers between devices: 136 us -> 144 us
  Pallas kernels: 164 us -> 157 us
  local copies, waits for them, and re-layouts: 45.9 us -> 39.7 us
    pallas_call x1, Pallas kernels: 33 us -> 20.6 us  [attention(): pl.pallas_call(recent_kernel, grid_spec=pltpu.PrefetchScalarGridSpec(num_...]
    reduce_scatter x1, waiting for transfers between devices: 39.7 us -> 47.9 us  [reduce_rows(): part = lax.psum_scatter(split, 'y', scatter_dimension=0, tiled=True)]
    all_to_all x1 -> x0, local copies, waits for them, and re-layouts: 6.19 us -> none  [prompt_for_requests(): return lax.all_to_all(outgoing, 'dp', 0, 0, tiled=False)]
    pallas_call x1, Pallas kernels: 43.8 us -> 49.6 us  [attention(): pl.pallas_call(prompt_kernel, grid_spec=pltpu.PrefetchScalarGridSpec(num_...]
  transfers between devices with their start and end apart: 6 -> 6, of which waited for: 5 -> 5; matrix products, arithmetic and copies ran while one was open for 13% -> 13% of each run, Pallas kernels for 8% -> 5%
where the time goes in v9:
time: 417 us; the launch traced here: 416 us
  Pallas kernels  157 us (38%)
  waiting for transfers between devices  144 us (35%)
  local copies, waits for them, and re-layouts  39.7 us (10%)
  matrix products  27.1 us (6%)
  other arithmetic  19.3 us (5%)
  starting transfers between devices  14.9 us (4%)
  between operations  13.4 us (3%)
    pallas_call x3, Pallas kernels, exchange(): pl.pallas_call(exchange_kernel, out_shape=jax.ShapeDtypeStruct(piece.shap...  87.1 us
    all_gather x2, waiting for transfers between devices, gather_rows(): lax.all_gather(pair, 'y', axis=0, tiled=True)  50.3 us
    pallas_call x1, Pallas kernels, attention(): pl.pallas_call(prompt_kernel, grid_spec=pltpu.PrefetchScalarGridSpec(num_...  49.6 us
    reduce_scatter x1, waiting for transfers between devices, reduce_rows(): part = lax.psum_scatter(split, 'y', scatter_dimension=0, tiled=True)  47.9 us
    reduce_scatter x1, waiting for transfers between devices, scatter_rows(): part = lax.psum_scatter(split, 'y', scatter_dimension=0, tiled=True)  40.7 us
    pallas_call x1, Pallas kernels, attention(): pl.pallas_call(recent_kernel, grid_spec=pltpu.PrefetchScalarGridSpec(num_...  20.6 us
    concatenate x8, local copies, waits for them, and re-layouts, rotate(): jnp.concatenate([first_half * cosine - second_half * sine_part, second_ha...  10.1 us
  transfers between devices with their start and end apart: 6, of which 5 were waited for; matrix products, arithmetic and copies ran while one was open for 13% of the time, Pallas kernels for 5%

profile of v9, /device:TPU:65, one launch (start us, length us, event | category | flops | bytes accessed | tf_op | source)
XLA Modules:
  0.0 415.8 jit_solution(9749139880410852025)
XLA Ops:
  8.6 23.1 %shard_map.154 = bf16[128,1536]{1,0:T(8,128)(2,1)} custom-call(bf16[128,1536]{1,0:T(8,128)(2,1)} %reshape.214.piece_ref), custom_call_target="tpu_custom_call" | custom-call | tf_op jit(solution)/shard_map/pallas_call | solution.py:265
  34.9 7.8 %all-to-all-start = ((s32[32,1,2]{2,1,0:T(1,128)}), s32[32,1,2]{2,1,0:T(1,128)S(1)}, u32[]{:S(2)}, u32[]{:S(2)}) async-start(s32[32,1,2]{2,1,0:T(1,128)} %broadcast_in_dim.9), calls=%async_computation | async-start | bytes 32768 | tf_op jit(solution)/shard_map/all_to_all | solution.py:306
  42.7 5.1 %all-to-all-done = s32[32,1,2]{2,1,0:T(1,128)S(1)} async-done(((s32[32,1,2]{2,1,0:T(1,128)}), s32[32,1,2]{2,1,0:T(1,128)S(1)}, u32[]{:S(2)}, u32[]{:S(2)}) %all-to-all-start) | async-done | bytes 288 | tf_op jit(solution)/shard_map/all_to_all | solution.py:306
  48.3 2.6 gather_fusion
  50.9 4.0 broadcast_select_fusion
  54.9 7.0 %all-to-all-start.1 = ((bf16[32,2,2,128,96]{3,4,2,1,0:T(8,128)(2,1)}), bf16[32,2,2,128,96]{3,4,2,1,0:T(8,128)(2,1)}, u32[]{:S(2)}, u32[]{:S(2)}) async-start(bf16[32,2,2,128,96]{3,4,2,1,0:T(8,128)(2,1)} %broadcast_select_fusion), calls=%async_computation.1 | async-start | bytes 6291456 | tf_op jit(solution)/shard_map/all_to_all | solution.py:311
  62.0 3.9 copy.66.wk_ref
  65.8 3.9 copy.67.wv_ref
  70.6 8.2 %all-gather.3.cloned.1.call-done = bf16[8,128,1536]{2,1,0:T(8,128)(2,1)} async-done(((bf16[2,128,1536]{2,1,0:T(8,128)(2,1)}), bf16[8,128,1536]{2,1,0:T(8,128)(2,1)}) %all-gather.3.cloned.1.call-update) | async-done | bytes 3145744 | tf_op jit(solution)/shard_map/all_gather | solution.py:282
  78.8 7.2 %dot_general.29 = bf16[512,2,1536]{2,1,0:T(2,128)(2,1)} reshape(bf16[8,128,1536]{2,1,0:T(8,128)(2,1)} %all-gather.3.cloned.1.call-done) | data formatting | bytes 6291456 | tf_op jit(solution)/shard_map/dot_general | solution.py:354
  86.1 3.1 fusion
  93.9 3.0 fusion.11
  104.6 3.7 convolution_convert_fusion.2
  114.7 20.6 %shard_map.155 = (f32[2,1024,96]{2,1,0:T(8,128)}, f32[2,1024,1]{2,1,0:T(8,128)}, f32[2,1024,1]{2,1,0:T(8,128)}) custom-call(s32[2]{0:T(128)} %length_ref.3, bf16[2,1024,96]{2,1,0:T(8,128)(2,1)} %bitcast.81, bf16[2,4096,96]{2,1,0:T(8,128)(2,1)} %copy.66.wk_ref, bf16[2,4096,96]{2,1,0:T(8,128)(2,1)} %copy.67.wv_ref, bf16[2,512,96]{2,1,0:T(8,128)(2,1)} %bitcast.84, ...), custom_call_target="tpu_custom_call" | custom-call | flops 3623878656 | bytes 3538944 | tf_op jit(solution)/shard_map/pallas_call | solution.py:179
  135.3 49.6 %shard_map.156 = bf16[2,1024,96]{2,1,0:T(8,128)(2,1)} custom-call(s32[2]{0:T(128)} %length_ref.3, bf16[2,1024,96]{2,1,0:T(8,128)(2,1)} %bitcast.82, bf16[32,2,2,96,128]{4,3,2,1,0:T(8,128)(2,1)} %bitcast.13.pk_ref.pv_ref, bf16[32,2,2,96,128]{4,3,2,1,0:T(8,128)(2,1)} %bitcast.13.pk_ref.pv_ref, f32[2,1024,96]{2,1,0:T(8,128)} %get-tuple-element.8.acc_in, ...), custom_call_target="tpu_custom_call" | custom-call | flops 3221225472 | bytes 3145728 | tf_op jit(solution)/shard_map/pallas_call | solution.py:214
  186.8 3.7 convolution_convert_fusion
  190.6 47.9 %reduce-scatter.3.cloned.1.call-done.piece_ref = bf16[2,128,1536]{2,1,0:T(8,128)(2,1)} async-done(((bf16[8,128,1536]{2,1,0:T(8,128)(2,1)}), bf16[2,128,1536]{2,1,0:T(8,128)(2,1)}) %reduce-scatter.3.cloned.1.call-update) | async-done | bytes 786448 | tf_op jit(solution)/shard_map/reduce_scatter | solution.py:289
  238.5 40.5 %shard_map.157 = bf16[2,128,1536]{2,1,0:T(8,128)(2,1)} custom-call(bf16[2,128,1536]{2,1,0:T(8,128)(2,1)} %reduce-scatter.3.cloned.1.call-done.piece_ref), custom_call_target="tpu_custom_call" | custom-call | tf_op jit(solution)/shard_map/pallas_call | solution.py:265
  282.0 42.1 %all-gather.5.cloned.1.call-done = bf16[8,128,1536]{2,1,0:T(8,128)(2,1)} async-done(((bf16[2,128,1536]{2,1,0:T(8,128)(2,1)}), bf16[8,128,1536]{2,1,0:T(8,128)(2,1)}) %all-gather.5.cloned.1.call-update) | async-done | bytes 3145744 | tf_op jit(solution)/shard_map/all_gather | solution.py:282
  324.0 5.5 %fusion.38 = f32[1024,512]{1,0:T(8,128)} fusion(bf16[1024,1536]{1,0:T(8,128)(2,1)} %bitcast.88, bf16[1536,512]{1,0:T(8,128)(2,1)} %param.29), kind=kOutput, calls=%fused_computation.82 | convolution fusion | flops 1610612736 | bytes 6815744 | tf_op jit(solution)/shard_map/dot_general | solution.py:413
  329.5 8.2 %convolution_convert_fusion.1 = bf16[1024,1536]{1,0:T(8,128)(2,1)} fusion(bf16[512,1536]{1,0:T(8,128)(2,1)S(1)} %copy-done, f32[1024,512]{1,0:T(8,128)} %fusion.38, bf16[1024,1536]{1,0:T(8,128)(2,1)} %bitcast.89, bf16[1536,512]{1,0:T(8,128)(2,1)} %param.30), kind=kOutput, calls=%fused_computation.2 | convolution fusion | flops 3225944064 | bytes 11534336 | tf_op jit(solution)/shard_map/dot_general | solution.py:417
  338.3 40.7 %reduce-scatter.5.cloned.1.call-done = bf16[2,128,1536]{2,1,0:T(8,128)(2,1)} async-done(((bf16[8,128,1536]{2,1,0:T(8,128)(2,1)}), bf16[2,128,1536]{2,1,0:T(8,128)(2,1)}) %reduce-scatter.5.cloned.1.call-update) | async-done | bytes 786448 | tf_op jit(solution)/shard_map/reduce_scatter | solution.py:297
  380.7 23.6 %shard_map.158 = bf16[128,1536]{1,0:T(8,128)(2,1)} custom-call(bf16[128,1536]{1,0:T(8,128)(2,1)} %dynamic-slice_bitcast_fusion.piece_ref), custom_call_target="tpu_custom_call" | custom-call | tf_op jit(solution)/shard_map/pallas_call | solution.py:265
  406.9 2.3 add_convert_fusion
  (68 shorter events, 35.4 us)
Async XLA Ops:
  6.5 323.0 %copy-start = (bf16[512,1536]{1,0:T(8,128)(2,1)S(1)}, bf16[512,1536]{1,0:T(8,128)(2,1)}, u32[]{:S(2)}) copy-start(bf16[512,1536]{1,0:T(8,128)(2,1)} %param.31) | copy-start | bytes 4718596
  6.5 26.6 %copy-start.3 = (f32[1536]{0:T(1024)S(1)}, f32[1536]{0:T(1024)}, u32[]{:S(2)}) copy-start(f32[1536]{0:T(1024)} %param.19) | copy-start | bytes 18436
  6.5 72.3 %all-gather.3.cloned.1.call-start = ((), (), s32[]{:S(2)}) async-start(), calls=%async_computation.4 | async-start | bytes 3932160 | tf_op jit(solution)/shard_map/all_gather | solution.py:282
  31.6 2.7 copy-start.5
  31.6 11.0 %copy-start.1 = (bf16[8,128,96]{1,2,0:T(8,128)(2,1)S(1)}, bf16[8,128,96]{1,2,0:T(8,128)(2,1)}, u32[]{:S(2)}) copy-start(bf16[8,128,96]{1,2,0:T(8,128)(2,1)} %param.27) | copy-start | bytes 589828
  31.6 11.0 %copy-start.2 = (bf16[8,128,96]{1,2,0:T(8,128)(2,1)S(1)}, bf16[8,128,96]{1,2,0:T(8,128)(2,1)}, u32[]{:S(2)}) copy-start(bf16[8,128,96]{1,2,0:T(8,128)(2,1)} %param.26) | copy-start | bytes 589828
  34.9 12.9 %all-to-all-start = ((s32[32,1,2]{2,1,0:T(1,128)}), s32[32,1,2]{2,1,0:T(1,128)S(1)}, u32[]{:S(2)}, u32[]{:S(2)}) async-start(s32[32,1,2]{2,1,0:T(1,128)} %broadcast_in_dim.9), calls=%async_computation | async-start | bytes 32768 | tf_op jit(solution)/shard_map/all_to_all | solution.py:306
  54.9 80.4 %all-to-all-start.1 = ((bf16[32,2,2,128,96]{3,4,2,1,0:T(8,128)(2,1)}), bf16[32,2,2,128,96]{3,4,2,1,0:T(8,128)(2,1)}, u32[]{:S(2)}, u32[]{:S(2)}) async-start(bf16[32,2,2,128,96]{3,4,2,1,0:T(8,128)(2,1)} %broadcast_select_fusion), calls=%async_computation.1 | async-start | bytes 6291456 | tf_op jit(solution)/shard_map/all_to_all | solution.py:311
  61.9 176.5 %reduce-scatter.3.cloned.1.call-start = ((), (), s32[]{:S(2)}) async-start(), calls=%async_computation.5 | async-start | bytes 3932160 | tf_op jit(solution)/shard_map/reduce_scatter | solution.py:289
  65.8 3.9 copy-start.7
  70.6 15.5 %copy-start.6 = (bf16[1536,192]{0,1:T(8,128)(2,1)S(1)}, bf16[1536,192]{0,1:T(8,128)(2,1)}, u32[]{:S(2)}) copy-start(bf16[1536,192]{0,1:T(8,128)(2,1)} %param.20) | copy-start | bytes 1769476
  190.5 90.3 %copy-start.4 = (f32[1536]{0:T(1024)S(1)}, f32[1536]{0:T(1024)}, u32[]{:S(2)}) copy-start(f32[1536]{0:T(1024)} %param.28) | copy-start | bytes 18436
  190.5 133.5 %all-gather.5.cloned.1.call-start = ((), (), s32[]{:S(2)}) async-start(), calls=%async_computation.6 | async-start | bytes 3932160 | tf_op jit(solution)/shard_map/all_gather | solution.py:282
  281.9 97.1 %reduce-scatter.5.cloned.1.call-start = ((), (), s32[]{:S(2)}) async-start(), calls=%async_computation.7 | async-start | bytes 3932160 | tf_op jit(solution)/shard_map/reduce_scatter | solution.py:297
Sparse Core Ops, SparseCore 0:
  34.4 44.3 all-gather.2
  190.6 47.7 reduce-scatter.2
  282.0 41.9 all-gather.4
  337.9 41.0 reduce-scatter.4

commit v10 on v9

--- a/solution.py
+++ b/solution.py
@@ -344,33 +344,25 @@
     row_count = flattened_rows.shape[0] // local_reqs
     y_size = lax.axis_size("y")
     zh_size = lax.axis_size("zh")
-    gathered_row = jnp.arange(row_count, dtype=jnp.int32)
+    block_rows = local_rows * local_reqs
+    flat_row = jnp.arange(row_count * local_reqs, dtype=jnp.int32)
+    block_of_row = flat_row // block_rows
     token_of_row = (
-        (gathered_row // (zh_size * local_rows) + y_size * ((gathered_row // local_rows) % zh_size))
-        * local_rows
-        + gathered_row % local_rows
-    )
-    positions = PROMPT_TOKENS + cached_len[None, :] + token_of_row[:, None]
+        (block_of_row % zh_size) * y_size + block_of_row // zh_size
+    ) * local_rows + (flat_row % block_rows) // local_reqs
+    positions = PROMPT_TOKENS + jnp.take(cached_len, flat_row % local_reqs) + token_of_row
+    query_heads = query_cols // HEAD_SIZE
     project_queries = jnp.dot(flattened_rows, w_query, preferred_element_type=jnp.float32).reshape(
-        row_count, local_reqs, query_cols // HEAD_SIZE, HEAD_SIZE
+        row_count * local_reqs, query_heads, HEAD_SIZE
     )
     fresh_keys = jnp.dot(flattened_rows, key_matrix, preferred_element_type=jnp.float32).reshape(
-        row_count, local_reqs, key_heads, HEAD_SIZE
-    )
-    fresh_values = (
-        jnp.dot(flattened_rows, value_matrix, preferred_element_type=jnp.float32)
-        .astype(jnp.bfloat16)
-        .reshape(row_count, local_reqs, key_cols)
-    )
-    project_queries = (
-        rotate(project_queries, positions)
-        .astype(jnp.bfloat16)
-        .reshape(row_count, local_reqs, query_cols)
-    )
-    fresh_keys = (
-        rotate(fresh_keys, positions).astype(jnp.bfloat16).reshape(row_count, local_reqs, key_cols)
-    )
-    query_heads = query_cols // HEAD_SIZE
+        row_count * local_reqs, key_heads, HEAD_SIZE
+    )
+    fresh_values = jnp.dot(flattened_rows, value_matrix, preferred_element_type=jnp.float32).astype(
+        jnp.bfloat16
+    )
+    project_queries = rotate(project_queries, positions).astype(jnp.bfloat16)
+    fresh_keys = rotate(fresh_keys, positions).astype(jnp.bfloat16)
     grid_rows = (y_size, zh_size, local_rows, local_reqs)
     queries = (
         project_queries.reshape(grid_rows + (query_heads, HEAD_SIZE))

time: 417 us -> 409 us (0.981)
  local copies, waits for them, and re-layouts: 39.7 us -> 23.9 us
  waiting for transfers between devices: 144 us -> 150 us
    all_to_all x1, waiting for transfers between devices: 0.01 us -> 11.1 us  [prompt_for_requests(): return lax.all_to_all(outgoing, 'dp', 0, 0, tiled=False)]
    concatenate x8 -> x0, local copies, waits for them, and re-layouts: 10.1 us -> none  [rotate(): jnp.concatenate([first_half * cosine - second_half * sine_part, second_ha...]
    dot_general x1 -> x0, local copies, waits for them, and re-layouts: 7.22 us -> none  [body(): jnp.dot(flattened_rows, w_query, preferred_element_type=jnp.float32)]
  transfers between devices with their start and end apart: 6 -> 6, of which waited for: 5 -> 6; matrix products, arithmetic and copies ran while one was open for 13% -> 9% of each run, Pallas kernels for 5% -> 6%
where the time goes in v10:
time: 409 us; the launch traced here: 407 us
  Pallas kernels  160 us (39%)
  waiting for transfers between devices  150 us (37%)
  matrix products  26.3 us (6%)
  local copies, waits for them, and re-layouts  23.9 us (6%)
  other arithmetic  19.1 us (5%)
  starting transfers between devices  14.9 us (4%)
  between operations  13.4 us (3%)
    pallas_call x3, Pallas kernels, exchange(): pl.pallas_call(exchange_kernel, out_shape=jax.ShapeDtypeStruct(piece.shap...  87.1 us
    pallas_call x1, Pallas kernels, attention(): pl.pallas_call(prompt_kernel, grid_spec=pltpu.PrefetchScalarGridSpec(num_...  49.6 us
    all_gather x2, waiting for transfers between devices, gather_rows(): lax.all_gather(pair, 'y', axis=0, tiled=True)  48.4 us
    reduce_scatter x1, waiting for transfers between devices, reduce_rows(): part = lax.psum_scatter(split, 'y', scatter_dimension=0, tiled=True)  44.3 us
    reduce_scatter x1, waiting for transfers between devices, scatter_rows(): part = lax.psum_scatter(split, 'y', scatter_dimension=0, tiled=True)  40.7 us
    pallas_call x1, Pallas kernels, attention(): pl.pallas_call(recent_kernel, grid_spec=pltpu.PrefetchScalarGridSpec(num_...  23.4 us
    all_to_all x1, waiting for transfers between devices, prompt_for_requests(): return lax.all_to_all(outgoing, 'dp', 0, 0, tiled=False)  11.1 us
    dot_general x1, matrix products, body(): jnp.dot(hidden, w_down, preferred_element_type=jnp.float32)  8.19 us
  transfers between devices with their start and end apart: 6, of which 6 were waited for; matrix products, arithmetic and copies ran while one was open for 9% of the time, Pallas kernels for 6%

profile of v10, /device:TPU:65, one launch (start us, length us, event | category | flops | bytes accessed | tf_op | source)
XLA Modules:
  0.0 407.4 jit_solution(13014817610055690641)
XLA Ops:
  8.6 23.1 %shard_map.154 = bf16[128,1536]{1,0:T(8,128)(2,1)} custom-call(bf16[128,1536]{1,0:T(8,128)(2,1)} %reshape.350.piece_ref), custom_call_target="tpu_custom_call" | custom-call | tf_op jit(solution)/shard_map/pallas_call | solution.py:265
  34.9 7.8 %all-to-all-start = ((s32[32,1,2]{2,1,0:T(1,128)}), s32[32,1,2]{2,1,0:T(1,128)S(1)}, u32[]{:S(2)}, u32[]{:S(2)}) async-start(s32[32,1,2]{2,1,0:T(1,128)} %broadcast_in_dim.16), calls=%async_computation | async-start | bytes 32768 | tf_op jit(solution)/shard_map/all_to_all | solution.py:306
  42.8 5.1 %all-to-all-done = s32[32,1,2]{2,1,0:T(1,128)S(1)} async-done(((s32[32,1,2]{2,1,0:T(1,128)}), s32[32,1,2]{2,1,0:T(1,128)S(1)}, u32[]{:S(2)}, u32[]{:S(2)}) %all-to-all-start) | async-done | bytes 288 | tf_op jit(solution)/shard_map/all_to_all | solution.py:306
  48.3 2.6 gather_fusion
  50.9 4.0 broadcast_select_fusion
  54.9 7.0 %all-to-all-start.1 = ((bf16[32,2,2,128,96]{3,4,2,1,0:T(8,128)(2,1)}), bf16[32,2,2,128,96]{3,4,2,1,0:T(8,128)(2,1)}, u32[]{:S(2)}, u32[]{:S(2)}) async-start(bf16[32,2,2,128,96]{3,4,2,1,0:T(8,128)(2,1)} %broadcast_select_fusion), calls=%async_computation.1 | async-start | bytes 6291456 | tf_op jit(solution)/shard_map/all_to_all | solution.py:311
  62.0 3.8 copy.51.wk_ref
  65.8 3.9 copy.52.wv_ref
  72.5 6.4 %all-gather.3.cloned.1.call-done = bf16[8,128,1536]{2,1,0:T(8,128)(2,1)} async-done(((bf16[2,128,1536]{2,1,0:T(8,128)(2,1)}), bf16[8,128,1536]{2,1,0:T(8,128)(2,1)}) %all-gather.3.cloned.1.call-update) | async-done | bytes 3145744 | tf_op jit(solution)/shard_map/all_gather | solution.py:282
  78.9 3.0 fusion.49
  86.6 3.0 convolution_bitcast_fusion
  92.2 3.0 convolution_convert_fusion.2
  96.1 23.4 %shard_map.155 = (f32[2,1024,96]{2,1,0:T(8,128)}, f32[2,1024,1]{2,1,0:T(8,128)}, f32[2,1024,1]{2,1,0:T(8,128)}) custom-call(s32[2]{0:T(128)} %length_ref.3, bf16[2,1024,96]{2,1,0:T(8,128)(2,1)} %bitcast.76, bf16[2,4096,96]{2,1,0:T(8,128)(2,1)} %copy.51.wk_ref, bf16[2,4096,96]{2,1,0:T(8,128)(2,1)} %copy.52.wv_ref, bf16[2,512,96]{2,1,0:T(8,128)(2,1)} %bitcast.79, ...), custom_call_target="tpu_custom_call" | custom-call | flops 3623878656 | bytes 3538944 | tf_op jit(solution)/shard_map/pallas_call | solution.py:179
  119.5 11.1 %all-to-all-done.1 = bf16[32,2,2,128,96]{3,4,2,1,0:T(8,128)(2,1)} async-done(((bf16[32,2,2,128,96]{3,4,2,1,0:T(8,128)(2,1)}), bf16[32,2,2,128,96]{3,4,2,1,0:T(8,128)(2,1)}, u32[]{:S(2)}, u32[]{:S(2)}) %all-to-all-start.1) | async-done | bytes 3145760 | tf_op jit(solution)/shard_map/all_to_all | solution.py:311
  130.5 49.6 %shard_map.156 = bf16[2,1024,96]{2,1,0:T(8,128)(2,1)} custom-call(s32[2]{0:T(128)} %length_ref.3, bf16[2,1024,96]{2,1,0:T(8,128)(2,1)} %bitcast.77, bf16[32,2,2,96,128]{4,3,2,1,0:T(8,128)(2,1)} %bitcast.18.pk_ref.pv_ref, bf16[32,2,2,96,128]{4,3,2,1,0:T(8,128)(2,1)} %bitcast.18.pk_ref.pv_ref, f32[2,1024,96]{2,1,0:T(8,128)} %get-tuple-element.8.acc_in, ...), custom_call_target="tpu_custom_call" | custom-call | flops 3221225472 | bytes 3145728 | tf_op jit(solution)/shard_map/pallas_call | solution.py:214
  182.1 3.7 convolution_convert_fusion
  185.9 44.3 %reduce-scatter.3.cloned.1.call-done.piece_ref = bf16[2,128,1536]{2,1,0:T(8,128)(2,1)} async-done(((bf16[8,128,1536]{2,1,0:T(8,128)(2,1)}), bf16[2,128,1536]{2,1,0:T(8,128)(2,1)}) %reduce-scatter.3.cloned.1.call-update) | async-done | bytes 786448 | tf_op jit(solution)/shard_map/reduce_scatter | solution.py:289
  230.2 40.5 %shard_map.157 = bf16[2,128,1536]{2,1,0:T(8,128)(2,1)} custom-call(bf16[2,128,1536]{2,1,0:T(8,128)(2,1)} %reduce-scatter.3.cloned.1.call-done.piece_ref), custom_call_target="tpu_custom_call" | custom-call | tf_op jit(solution)/shard_map/pallas_call | solution.py:265
  273.7 42.0 %all-gather.5.cloned.1.call-done = bf16[8,128,1536]{2,1,0:T(8,128)(2,1)} async-done(((bf16[2,128,1536]{2,1,0:T(8,128)(2,1)}), bf16[8,128,1536]{2,1,0:T(8,128)(2,1)}) %all-gather.5.cloned.1.call-update) | async-done | bytes 3145744 | tf_op jit(solution)/shard_map/all_gather | solution.py:282
  315.7 5.5 %fusion.50 = f32[1024,512]{1,0:T(8,128)} fusion(bf16[1024,1536]{1,0:T(8,128)(2,1)} %bitcast.84, bf16[1536,512]{1,0:T(8,128)(2,1)} %param.29), kind=kOutput, calls=%fused_computation.104 | convolution fusion | flops 1610612736 | bytes 6815744 | tf_op jit(solution)/shard_map/dot_general | solution.py:405
  321.2 8.2 %convolution_convert_fusion.1 = bf16[1024,1536]{1,0:T(8,128)(2,1)} fusion(bf16[512,1536]{1,0:T(8,128)(2,1)S(1)} %copy-done, f32[1024,512]{1,0:T(8,128)} %fusion.50, bf16[1024,1536]{1,0:T(8,128)(2,1)} %bitcast.85, bf16[1536,512]{1,0:T(8,128)(2,1)} %param.30), kind=kOutput, calls=%fused_computation.2 | convolution fusion | flops 3225944064 | bytes 11534336 | tf_op jit(solution)/shard_map/dot_general | solution.py:409
  330.0 40.7 %reduce-scatter.5.cloned.1.call-done = bf16[2,128,1536]{2,1,0:T(8,128)(2,1)} async-done(((bf16[8,128,1536]{2,1,0:T(8,128)(2,1)}), bf16[2,128,1536]{2,1,0:T(8,128)(2,1)}) %reduce-scatter.5.cloned.1.call-update) | async-done | bytes 786448 | tf_op jit(solution)/shard_map/reduce_scatter | solution.py:297
  372.4 23.6 %shard_map.158 = bf16[128,1536]{1,0:T(8,128)(2,1)} custom-call(bf16[128,1536]{1,0:T(8,128)(2,1)} %dynamic-slice_bitcast_fusion.piece_ref), custom_call_target="tpu_custom_call" | custom-call | tf_op jit(solution)/shard_map/pallas_call | solution.py:265
  398.6 2.3 add_convert_fusion
  (69 shorter events, 26.5 us)
Async XLA Ops:
  6.5 314.7 %copy-start = (bf16[512,1536]{1,0:T(8,128)(2,1)S(1)}, bf16[512,1536]{1,0:T(8,128)(2,1)}, u32[]{:S(2)}) copy-start(bf16[512,1536]{1,0:T(8,128)(2,1)} %param.31) | copy-start | bytes 4718596
  6.5 26.6 %copy-start.5 = (f32[1536]{0:T(1024)S(1)}, f32[1536]{0:T(1024)}, u32[]{:S(2)}) copy-start(f32[1536]{0:T(1024)} %param.19) | copy-start | bytes 18436
  6.5 72.3 %all-gather.3.cloned.1.call-start = ((), (), s32[]{:S(2)}) async-start(), calls=%async_computation.4 | async-start | bytes 3932160 | tf_op jit(solution)/shard_map/all_gather | solution.py:282
  31.6 2.7 copy-start.8
  31.6 11.1 %copy-start.3 = (bf16[8,128,96]{1,2,0:T(8,128)(2,1)S(1)}, bf16[8,128,96]{1,2,0:T(8,128)(2,1)}, u32[]{:S(2)}) copy-start(bf16[8,128,96]{1,2,0:T(8,128)(2,1)} %param.27) | copy-start | bytes 589828
  31.6 11.1 %copy-start.4 = (bf16[8,128,96]{1,2,0:T(8,128)(2,1)S(1)}, bf16[8,128,96]{1,2,0:T(8,128)(2,1)}, u32[]{:S(2)}) copy-start(bf16[8,128,96]{1,2,0:T(8,128)(2,1)} %param.26) | copy-start | bytes 589828
  34.9 12.9 %all-to-all-start = ((s32[32,1,2]{2,1,0:T(1,128)}), s32[32,1,2]{2,1,0:T(1,128)S(1)}, u32[]{:S(2)}, u32[]{:S(2)}) async-start(s32[32,1,2]{2,1,0:T(1,128)} %broadcast_in_dim.16), calls=%async_computation | async-start | bytes 32768 | tf_op jit(solution)/shard_map/all_to_all | solution.py:306
  54.9 75.7 %all-to-all-start.1 = ((bf16[32,2,2,128,96]{3,4,2,1,0:T(8,128)(2,1)}), bf16[32,2,2,128,96]{3,4,2,1,0:T(8,128)(2,1)}, u32[]{:S(2)}, u32[]{:S(2)}) async-start(bf16[32,2,2,128,96]{3,4,2,1,0:T(8,128)(2,1)} %broadcast_select_fusion), calls=%async_computation.1 | async-start | bytes 6291456 | tf_op jit(solution)/shard_map/all_to_all | solution.py:311
  61.9 168.2 %reduce-scatter.3.cloned.1.call-start = ((), (), s32[]{:S(2)}) async-start(), calls=%async_computation.5 | async-start | bytes 3932160 | tf_op jit(solution)/shard_map/reduce_scatter | solution.py:289
  65.8 3.9 copy-start.7
  65.8 13.0 %copy-start.9 = (bf16[1536,192]{0,1:T(8,128)(2,1)S(1)}, bf16[1536,192]{0,1:T(8,128)(2,1)}, u32[]{:S(2)}) copy-start(bf16[1536,192]{0,1:T(8,128)(2,1)} %param.20) | copy-start | bytes 1769476
  84.2 2.4 copy-start.1
  89.5 2.7 copy-start.2
  185.8 86.7 %copy-start.6 = (f32[1536]{0:T(1024)S(1)}, f32[1536]{0:T(1024)}, u32[]{:S(2)}) copy-start(f32[1536]{0:T(1024)} %param.28) | copy-start | bytes 18436
  185.8 129.9 %all-gather.5.cloned.1.call-start = ((), (), s32[]{:S(2)}) async-start(), calls=%async_computation.6 | async-start | bytes 3932160 | tf_op jit(solution)/shard_map/all_gather | solution.py:282
  273.6 97.0 %reduce-scatter.5.cloned.1.call-start = ((), (), s32[]{:S(2)}) async-start(), calls=%async_computation.7 | async-start | bytes 3932160 | tf_op jit(solution)/shard_map/reduce_scatter | solution.py:297
Sparse Core Ops, SparseCore 0:
  34.4 44.3 all-gather.2
  185.9 44.1 reduce-scatter.2
  273.7 41.9 all-gather.4
  329.6 41.0 reduce-scatter.4

commit v11 on v10

--- a/solution.py
+++ b/solution.py
@@ -272,9 +272,9 @@
     )(piece)
 
 
-def pair_rows(piece, call_id):
+def pair_rows(piece):
     upper = lax.axis_index("zh") == 1
-    other = exchange(piece, call_id)
+    other = lax.ppermute(piece, "zh", perm=[(0, 1), (1, 0)])
     return jnp.stack([jnp.where(upper, other, piece), jnp.where(upper, piece, other)])
 
 
@@ -337,7 +337,7 @@
     key_heads = key_cols // HEAD_SIZE
     query_group_width = query_cols // key_cols
     score_scale = 1.0 / math.sqrt(HEAD_SIZE)
-    token_pair = pair_rows(tokens.reshape(local_rows * local_reqs, MODEL_WIDTH), 0)
+    token_pair = pair_rows(tokens.reshape(local_rows * local_reqs, MODEL_WIDTH))
     source = norm_rows(token_pair, attn_gain)
     offset = 0
     flattened_rows = gather_rows(source)

time: 409 us -> 397 us (0.971)
  Pallas kernels: 160 us -> 137 us
  waiting for transfers between devices: 150 us -> 156 us
  starting transfers between devices: 14.9 us -> 19.6 us
    pallas_call x3 -> x2, Pallas kernels: 87.1 us -> 64.1 us  [exchange(): pl.pallas_call(exchange_kernel, out_shape=jax.ShapeDtypeStruct(piece.shap...]
    all_to_all x1, waiting for transfers between devices: 11.1 us -> 0.01 us  [prompt_for_requests(): return lax.all_to_all(outgoing, 'dp', 0, 0, tiled=False)]
    all_gather x2, waiting for transfers between devices: 48.4 us -> 59.5 us  [gather_rows(): lax.all_gather(pair, 'y', axis=0, tiled=True)]
    all_to_all x1, waiting for transfers between devices: 5.11 us -> 10.8 us  [prompt_for_requests(): lax.all_to_all(jnp.broadcast_to(prompt_group[None], (dp_size,) + prompt_g...]
    ppermute x0 -> x1, starting transfers between devices: none -> 5.2 us  [pair_rows(): other = lax.ppermute(piece, 'zh', perm=[(0, 1), (1, 0)])]
  transfers between devices with their start and end apart: 6 -> 7, of which waited for: 6 -> 5; matrix products, arithmetic and copies ran while one was open for 9% -> 9% of each run, Pallas kernels for 6% -> 6%
where the time goes in v11:
time: 397 us; the launch traced here: 395 us
  waiting for transfers between devices  156 us (39%)
  Pallas kernels  137 us (35%)
  matrix products  26.3 us (7%)
  local copies, waits for them, and re-layouts  23.9 us (6%)
  starting transfers between devices  19.6 us (5%)
  other arithmetic  18.9 us (5%)
  between operations  13.4 us (3%)
    pallas_call x2, Pallas kernels, exchange(): pl.pallas_call(exchange_kernel, out_shape=jax.ShapeDtypeStruct(piece.shap...  64.1 us
    all_gather x2, waiting for transfers between devices, gather_rows(): lax.all_gather(pair, 'y', axis=0, tiled=True)  59.5 us
    pallas_call x1, Pallas kernels, attention(): pl.pallas_call(prompt_kernel, grid_spec=pltpu.PrefetchScalarGridSpec(num_...  49.6 us
    reduce_scatter x1, waiting for transfers between devices, reduce_rows(): part = lax.psum_scatter(split, 'y', scatter_dimension=0, tiled=True)  45.2 us
    reduce_scatter x1, waiting for transfers between devices, scatter_rows(): part = lax.psum_scatter(split, 'y', scatter_dimension=0, tiled=True)  40.7 us
    pallas_call x1, Pallas kernels, attention(): pl.pallas_call(recent_kernel, grid_spec=pltpu.PrefetchScalarGridSpec(num_...  23.4 us
    all_to_all x1, waiting for transfers between devices, prompt_for_requests(): lax.all_to_all(jnp.broadcast_to(prompt_group[None], (dp_size,) + prompt_g...  10.8 us
    dot_general x1, matrix products, body(): jnp.dot(hidden, w_down, preferred_element_type=jnp.float32)  8.21 us
  transfers between devices with their start and end apart: 7, of which 5 were waited for; matrix products, arithmetic and copies ran while one was open for 9% of the time, Pallas kernels for 6%

profile of v11, /device:TPU:65, one launch (start us, length us, event | category | flops | bytes accessed | tf_op | source)
XLA Modules:
  0.0 395.4 jit_solution(18087647120025305002)
XLA Ops:
  7.8 5.2 %collective-permute-start = (bf16[128,1536]{1,0:T(8,128)(2,1)S(1)}, bf16[128,1536]{1,0:T(8,128)(2,1)S(1)}, u32[]{:S(2)}, u32[]{:S(2)}) collective-permute-start(bf16[128,1536]{1,0:T(8,128)(2,1)S(1)} %reshape.350), channel_id=1, source_target_pairs={{0,4},{4,0},{1,5},{5,1},{2,6},{6,2},{3,7},{7,3},{8,12},{12,8},{9,1... | collective-permute-start | bytes 1179656 | tf_op jit(solution)/shard_map/ppermute | solution.py:277
  14.3 7.9 %all-to-all-start = ((s32[32,1,2]{2,1,0:T(1,128)}), s32[32,1,2]{2,1,0:T(1,128)S(1)}, u32[]{:S(2)}, u32[]{:S(2)}) async-start(s32[32,1,2]{2,1,0:T(1,128)} %broadcast_in_dim.16), calls=%async_computation | async-start | bytes 32768 | tf_op jit(solution)/shard_map/all_to_all | solution.py:306
  23.3 10.8 %all-to-all-done = s32[32,1,2]{2,1,0:T(1,128)S(1)} async-done(((s32[32,1,2]{2,1,0:T(1,128)}), s32[32,1,2]{2,1,0:T(1,128)S(1)}, u32[]{:S(2)}, u32[]{:S(2)}) %all-to-all-start) | async-done | bytes 288 | tf_op jit(solution)/shard_map/all_to_all | solution.py:306
  36.0 2.6 gather_fusion
  38.5 3.9 broadcast_select_fusion
  42.5 6.4 %all-to-all-start.1 = ((bf16[32,2,2,128,96]{3,4,2,1,0:T(8,128)(2,1)}), bf16[32,2,2,128,96]{3,4,2,1,0:T(8,128)(2,1)}, u32[]{:S(2)}, u32[]{:S(2)}) async-start(bf16[32,2,2,128,96]{3,4,2,1,0:T(8,128)(2,1)} %broadcast_select_fusion), calls=%async_computation.1 | async-start | bytes 6291456 | tf_op jit(solution)/shard_map/all_to_all | solution.py:311
  48.9 3.9 copy.51.wk_ref
  52.8 3.9 copy.52.wv_ref
  59.5 17.4 %all-gather.3.cloned.1.call-done = bf16[8,128,1536]{2,1,0:T(8,128)(2,1)} async-done(((bf16[2,128,1536]{2,1,0:T(8,128)(2,1)}), bf16[8,128,1536]{2,1,0:T(8,128)(2,1)}) %all-gather.3.cloned.1.call-update) | async-done | bytes 3145744 | tf_op jit(solution)/shard_map/all_gather | solution.py:282
  76.9 3.0 fusion.49
  84.6 3.0 convolution_bitcast_fusion
  90.2 3.0 convolution_convert_fusion.2
  94.1 23.4 %shard_map.154 = (f32[2,1024,96]{2,1,0:T(8,128)}, f32[2,1024,1]{2,1,0:T(8,128)}, f32[2,1024,1]{2,1,0:T(8,128)}) custom-call(s32[2]{0:T(128)} %length_ref.3, bf16[2,1024,96]{2,1,0:T(8,128)(2,1)} %bitcast.76, bf16[2,4096,96]{2,1,0:T(8,128)(2,1)} %copy.51.wk_ref, bf16[2,4096,96]{2,1,0:T(8,128)(2,1)} %copy.52.wv_ref, bf16[2,512,96]{2,1,0:T(8,128)(2,1)} %bitcast.79, ...), custom_call_target="tpu_custom_call" | custom-call | flops 3623878656 | bytes 3538944 | tf_op jit(solution)/shard_map/pallas_call | solution.py:179
  117.5 49.6 %shard_map.155 = bf16[2,1024,96]{2,1,0:T(8,128)(2,1)} custom-call(s32[2]{0:T(128)} %length_ref.3, bf16[2,1024,96]{2,1,0:T(8,128)(2,1)} %bitcast.77, bf16[32,2,2,96,128]{4,3,2,1,0:T(8,128)(2,1)} %bitcast.18.pk_ref.pv_ref, bf16[32,2,2,96,128]{4,3,2,1,0:T(8,128)(2,1)} %bitcast.18.pk_ref.pv_ref, f32[2,1024,96]{2,1,0:T(8,128)} %get-tuple-element.8.acc_in, ...), custom_call_target="tpu_custom_call" | custom-call | flops 3221225472 | bytes 3145728 | tf_op jit(solution)/shard_map/pallas_call | solution.py:214
  169.1 3.7 convolution_convert_fusion
  172.8 45.2 %reduce-scatter.3.cloned.1.call-done.piece_ref = bf16[2,128,1536]{2,1,0:T(8,128)(2,1)} async-done(((bf16[8,128,1536]{2,1,0:T(8,128)(2,1)}), bf16[2,128,1536]{2,1,0:T(8,128)(2,1)}) %reduce-scatter.3.cloned.1.call-update) | async-done | bytes 786448 | tf_op jit(solution)/shard_map/reduce_scatter | solution.py:289
  218.1 40.5 %shard_map.156 = bf16[2,128,1536]{2,1,0:T(8,128)(2,1)} custom-call(bf16[2,128,1536]{2,1,0:T(8,128)(2,1)} %reduce-scatter.3.cloned.1.call-done.piece_ref), custom_call_target="tpu_custom_call" | custom-call | tf_op jit(solution)/shard_map/pallas_call | solution.py:265
  258.5 1.8 fusion
  261.6 42.0 %all-gather.5.cloned.1.call-done = bf16[8,128,1536]{2,1,0:T(8,128)(2,1)} async-done(((bf16[2,128,1536]{2,1,0:T(8,128)(2,1)}), bf16[8,128,1536]{2,1,0:T(8,128)(2,1)}) %all-gather.5.cloned.1.call-update) | async-done | bytes 3145744 | tf_op jit(solution)/shard_map/all_gather | solution.py:282
  303.7 5.5 %fusion.50 = f32[1024,512]{1,0:T(8,128)} fusion(bf16[1024,1536]{1,0:T(8,128)(2,1)} %bitcast.84, bf16[1536,512]{1,0:T(8,128)(2,1)} %param.29), kind=kOutput, calls=%fused_computation.104 | convolution fusion | flops 1610612736 | bytes 6815744 | tf_op jit(solution)/shard_map/dot_general | solution.py:405
  309.2 8.2 %convolution_convert_fusion.1 = bf16[1024,1536]{1,0:T(8,128)(2,1)} fusion(bf16[512,1536]{1,0:T(8,128)(2,1)S(1)} %copy-done, f32[1024,512]{1,0:T(8,128)} %fusion.50, bf16[1024,1536]{1,0:T(8,128)(2,1)} %bitcast.85, bf16[1536,512]{1,0:T(8,128)(2,1)} %param.30), kind=kOutput, calls=%fused_computation.2 | convolution fusion | flops 3225944064 | bytes 11534336 | tf_op jit(solution)/shard_map/dot_general | solution.py:409
  317.9 40.7 %reduce-scatter.5.cloned.1.call-done = bf16[2,128,1536]{2,1,0:T(8,128)(2,1)} async-done(((bf16[8,128,1536]{2,1,0:T(8,128)(2,1)}), bf16[2,128,1536]{2,1,0:T(8,128)(2,1)}) %reduce-scatter.5.cloned.1.call-update) | async-done | bytes 786448 | tf_op jit(solution)/shard_map/reduce_scatter | solution.py:297
  360.4 23.6 %shard_map.157 = bf16[128,1536]{1,0:T(8,128)(2,1)} custom-call(bf16[128,1536]{1,0:T(8,128)(2,1)} %dynamic-slice_bitcast_fusion.piece_ref), custom_call_target="tpu_custom_call" | custom-call | tf_op jit(solution)/shard_map/pallas_call | solution.py:265
  386.6 2.3 add_convert_fusion
  (64 shorter events, 24.5 us)
Async XLA Ops:
  6.5 302.6 %copy-start = (bf16[512,1536]{1,0:T(8,128)(2,1)S(1)}, bf16[512,1536]{1,0:T(8,128)(2,1)}, u32[]{:S(2)}) copy-start(bf16[512,1536]{1,0:T(8,128)(2,1)} %param.31) | copy-start | bytes 4718596
  6.5 28.1 %copy-start.3 = (f32[1536]{0:T(1024)S(1)}, f32[1536]{0:T(1024)}, u32[]{:S(2)}) copy-start(f32[1536]{0:T(1024)} %param.19) | copy-start | bytes 18436
  7.8 26.5 %collective-permute-start = (bf16[128,1536]{1,0:T(8,128)(2,1)S(1)}, bf16[128,1536]{1,0:T(8,128)(2,1)S(1)}, u32[]{:S(2)}, u32[]{:S(2)}) collective-permute-start(bf16[128,1536]{1,0:T(8,128)(2,1)S(1)} %reshape.350), channel_id=1, source_target_pairs={{0,4},{4,0},{1,5},{5,1},{2,6},{6,2},{3,7},{7,3},{8,12},{12,8},{9,1... | collective-permute-start | bytes 1179656 | tf_op jit(solution)/shard_map/ppermute | solution.py:277
  14.3 19.8 %all-to-all-start = ((s32[32,1,2]{2,1,0:T(1,128)}), s32[32,1,2]{2,1,0:T(1,128)S(1)}, u32[]{:S(2)}, u32[]{:S(2)}) async-start(s32[32,1,2]{2,1,0:T(1,128)} %broadcast_in_dim.16), calls=%async_computation | async-start | bytes 32768 | tf_op jit(solution)/shard_map/all_to_all | solution.py:306
  22.2 54.7 %all-gather.3.cloned.1.call-start = ((), (), s32[]{:S(2)}) async-start(), calls=%async_computation.4 | async-start | bytes 3932160 | tf_op jit(solution)/shard_map/all_gather | solution.py:282
  42.5 75.1 %all-to-all-start.1 = ((bf16[32,2,2,128,96]{3,4,2,1,0:T(8,128)(2,1)}), bf16[32,2,2,128,96]{3,4,2,1,0:T(8,128)(2,1)}, u32[]{:S(2)}, u32[]{:S(2)}) async-start(bf16[32,2,2,128,96]{3,4,2,1,0:T(8,128)(2,1)} %broadcast_select_fusion), calls=%async_computation.1 | async-start | bytes 6291456 | tf_op jit(solution)/shard_map/all_to_all | solution.py:311
  48.9 169.2 %reduce-scatter.3.cloned.1.call-start = ((), (), s32[]{:S(2)}) async-start(), calls=%async_computation.5 | async-start | bytes 3932160 | tf_op jit(solution)/shard_map/reduce_scatter | solution.py:289
  52.8 3.9 copy-start.5
  52.8 24.1 %copy-start.6 = (bf16[1536,192]{0,1:T(8,128)(2,1)S(1)}, bf16[1536,192]{0,1:T(8,128)(2,1)}, u32[]{:S(2)}) copy-start(bf16[1536,192]{0,1:T(8,128)(2,1)} %param.20) | copy-start | bytes 1769476
  82.2 2.4 copy-start.1
  87.6 2.7 copy-start.2
  172.8 87.6 %copy-start.4 = (f32[1536]{0:T(1024)S(1)}, f32[1536]{0:T(1024)}, u32[]{:S(2)}) copy-start(f32[1536]{0:T(1024)} %param.28) | copy-start | bytes 18436
  172.8 130.9 %all-gather.5.cloned.1.call-start = ((), (), s32[]{:S(2)}) async-start(), calls=%async_computation.6 | async-start | bytes 3932160 | tf_op jit(solution)/shard_map/all_gather | solution.py:282
  261.6 97.1 %reduce-scatter.5.cloned.1.call-start = ((), (), s32[]{:S(2)}) async-start(), calls=%async_computation.7 | async-start | bytes 3932160 | tf_op jit(solution)/shard_map/reduce_scatter | solution.py:297
Sparse Core Ops, SparseCore 0:
  36.0 40.8 all-gather.2
  172.9 45.1 reduce-scatter.2
  261.7 41.9 all-gather.4
  317.5 41.0 reduce-scatter.4

commit v12 on v11

--- a/solution.py
+++ b/solution.py
@@ -287,7 +287,7 @@
     zh_size = lax.axis_size("zh")
     split = full.reshape((y_size * zh_size, full.shape[0] // (y_size * zh_size)) + full.shape[1:])
     part = lax.psum_scatter(split, "y", scatter_dimension=0, tiled=True)
-    return part.astype(jnp.float32) + exchange(part, call_id).astype(jnp.float32)
+    return part.astype(jnp.float32) + lax.ppermute(part, "zh", perm=[(0, 1), (1, 0)]).astype(jnp.float32)
 
 
 def scatter_rows(full, call_id):
@@ -298,7 +298,9 @@
     me = lax.axis_index("zh")
     mine = lax.dynamic_index_in_dim(part, me, 0, keepdims=False)
     outgoing = lax.dynamic_index_in_dim(part, 1 - me, 0, keepdims=False)
-    return mine.astype(jnp.float32) + exchange(outgoing, call_id).astype(jnp.float32)
+    return mine.astype(jnp.float32) + lax.ppermute(outgoing, "zh", perm=[(0, 1), (1, 0)]).astype(
+        jnp.float32
+    )
 
 
 def prompt_for_requests(prompt_keys, prompt_values, prompt_group):

time: 397 us -> 398 us (level)
  Pallas kernels: 137 us -> 73 us
  waiting for transfers between devices: 156 us -> 212 us
  starting transfers between devices: 19.6 us -> 26.9 us
    pallas_call x2 -> x0, Pallas kernels: 64.1 us -> none  [exchange(): pl.pallas_call(exchange_kernel, out_shape=jax.ShapeDtypeStruct(piece.shap...]
    ppermute x0 -> x2, waiting for transfers between devices: none -> 56.1 us  [the longest x1 36.7 us: reduce_rows(): lax.ppermute(part, 'zh', perm=[(0, 1), (1, 0)]).astype(jnp.float32)]
    ppermute x0 -> x2, starting transfers between devices: none -> 7.3 us  [the longest x1 3.66 us: reduce_rows(): lax.ppermute(part, 'zh', perm=[(0, 1), (1, 0)]).astype(jnp.float32)]
  transfers between devices with their start and end apart: 7 -> 9, of which waited for: 5 -> 7; matrix products, arithmetic and copies ran while one was open for 9% -> 10% of each run, Pallas kernels for 6% -> 6%
where the time goes in v12:
time: 398 us; the launch traced here: 397 us
  waiting for transfers between devices  212 us (53%)
  Pallas kernels  73 us (18%)
  starting transfers between devices  26.9 us (7%)
  local copies, waits for them, and re-layouts  26.4 us (7%)
  matrix products  26.4 us (7%)
  other arithmetic  19.6 us (5%)
  between operations  13.3 us (3%)
    all_gather x2, waiting for transfers between devices, gather_rows(): lax.all_gather(pair, 'y', axis=0, tiled=True)  59.5 us
    pallas_call x1, Pallas kernels, attention(): pl.pallas_call(prompt_kernel, grid_spec=pltpu.PrefetchScalarGridSpec(num_...  49.6 us
    reduce_scatter x1, waiting for transfers between devices, reduce_rows(): part = lax.psum_scatter(split, 'y', scatter_dimension=0, tiled=True)  43.9 us
    reduce_scatter x1, waiting for transfers between devices, scatter_rows(): part = lax.psum_scatter(split, 'y', scatter_dimension=0, tiled=True)  41.2 us
    ppermute x1, waiting for transfers between devices, reduce_rows(): lax.ppermute(part, 'zh', perm=[(0, 1), (1, 0)]).astype(jnp.float32)  36.7 us
    pallas_call x1, Pallas kernels, attention(): pl.pallas_call(recent_kernel, grid_spec=pltpu.PrefetchScalarGridSpec(num_...  23.4 us
    ppermute x1, waiting for transfers between devices, scatter_rows(): lax.ppermute(outgoing, 'zh', perm=[(0, 1), (1, 0)]).astype(jnp.float32)  19.4 us
    all_to_all x1, waiting for transfers between devices, prompt_for_requests(): lax.all_to_all(jnp.broadcast_to(prompt_group[None], (dp_size,) + prompt_g...  10.8 us
  transfers between devices with their start and end apart: 9, of which 7 were waited for; matrix products, arithmetic and copies ran while one was open for 10% of the time, Pallas kernels for 6%

profile of v12, /device:TPU:65, one launch (start us, length us, event | category | flops | bytes accessed | tf_op | source)
XLA Modules:
  0.0 397.3 jit_solution(5673420034561995477)
XLA Ops:
  7.8 5.2 %collective-permute-start = (bf16[128,1536]{1,0:T(8,128)(2,1)S(1)}, bf16[128,1536]{1,0:T(8,128)(2,1)S(1)}, u32[]{:S(2)}, u32[]{:S(2)}) collective-permute-start(bf16[128,1536]{1,0:T(8,128)(2,1)S(1)} %reshape.350), channel_id=1, source_target_pairs={{0,4},{4,0},{1,5},{5,1},{2,6},{6,2},{3,7},{7,3},{8,12},{12,8},{9,1... | collective-permute-start | bytes 1179656 | tf_op jit(solution)/shard_map/ppermute | solution.py:277
  14.3 7.9 %all-to-all-start = ((s32[32,1,2]{2,1,0:T(1,128)}), s32[32,1,2]{2,1,0:T(1,128)S(1)}, u32[]{:S(2)}, u32[]{:S(2)}) async-start(s32[32,1,2]{2,1,0:T(1,128)} %broadcast_in_dim.16), calls=%async_computation | async-start | bytes 32768 | tf_op jit(solution)/shard_map/all_to_all | solution.py:308
  23.3 10.8 %all-to-all-done = s32[32,1,2]{2,1,0:T(1,128)S(1)} async-done(((s32[32,1,2]{2,1,0:T(1,128)}), s32[32,1,2]{2,1,0:T(1,128)S(1)}, u32[]{:S(2)}, u32[]{:S(2)}) %all-to-all-start) | async-done | bytes 288 | tf_op jit(solution)/shard_map/all_to_all | solution.py:308
  36.0 2.6 gather_fusion
  38.6 3.9 broadcast_select_fusion
  42.5 6.4 %all-to-all-start.1 = ((bf16[32,2,2,128,96]{3,4,2,1,0:T(8,128)(2,1)}), bf16[32,2,2,128,96]{3,4,2,1,0:T(8,128)(2,1)}, u32[]{:S(2)}, u32[]{:S(2)}) async-start(bf16[32,2,2,128,96]{3,4,2,1,0:T(8,128)(2,1)} %broadcast_select_fusion), calls=%async_computation.1 | async-start | bytes 6291456 | tf_op jit(solution)/shard_map/all_to_all | solution.py:313
  48.9 3.9 copy.51.wk_ref
  52.8 3.9 copy.52.wv_ref
  59.5 17.4 %all-gather.3.cloned.1.call-done = bf16[8,128,1536]{2,1,0:T(8,128)(2,1)} async-done(((bf16[2,128,1536]{2,1,0:T(8,128)(2,1)}), bf16[8,128,1536]{2,1,0:T(8,128)(2,1)}) %all-gather.3.cloned.1.call-update) | async-done | bytes 3145744 | tf_op jit(solution)/shard_map/all_gather | solution.py:282
  76.9 3.1 fusion.49
  86.4 3.0 convolution_bitcast_fusion
  92.0 3.0 convolution_convert_fusion.2
  95.9 23.4 %shard_map.154 = (f32[2,1024,96]{2,1,0:T(8,128)}, f32[2,1024,1]{2,1,0:T(8,128)}, f32[2,1024,1]{2,1,0:T(8,128)}) custom-call(s32[2]{0:T(128)} %length_ref.3, bf16[2,1024,96]{2,1,0:T(8,128)(2,1)} %bitcast.76, bf16[2,4096,96]{2,1,0:T(8,128)(2,1)} %copy.51.wk_ref, bf16[2,4096,96]{2,1,0:T(8,128)(2,1)} %copy.52.wv_ref, bf16[2,512,96]{2,1,0:T(8,128)(2,1)} %bitcast.79, ...), custom_call_target="tpu_custom_call" | custom-call | flops 3623878656 | bytes 3538944 | tf_op jit(solution)/shard_map/pallas_call | solution.py:179
  119.3 49.6 %shard_map.155 = bf16[2,1024,96]{2,1,0:T(8,128)(2,1)} custom-call(s32[2]{0:T(128)} %length_ref.3, bf16[2,1024,96]{2,1,0:T(8,128)(2,1)} %bitcast.77, bf16[32,2,2,96,128]{4,3,2,1,0:T(8,128)(2,1)} %bitcast.18.pk_ref.pv_ref, bf16[32,2,2,96,128]{4,3,2,1,0:T(8,128)(2,1)} %bitcast.18.pk_ref.pv_ref, f32[2,1024,96]{2,1,0:T(8,128)} %get-tuple-element.8.acc_in, ...), custom_call_target="tpu_custom_call" | custom-call | flops 3221225472 | bytes 3145728 | tf_op jit(solution)/shard_map/pallas_call | solution.py:214
  172.6 3.7 convolution_convert_fusion
  176.4 43.9 %reduce-scatter.3.cloned.1.call-done = bf16[2,128,1536]{2,1,0:T(8,128)(2,1)} async-done(((bf16[8,128,1536]{2,1,0:T(8,128)(2,1)}), bf16[2,128,1536]{2,1,0:T(8,128)(2,1)}) %reduce-scatter.3.cloned.1.call-update) | async-done | bytes 786448 | tf_op jit(solution)/shard_map/reduce_scatter | solution.py:289
  220.4 3.7 collective-permute-start.1
  224.0 36.7 %collective-permute-done.1 = bf16[2,128,1536]{2,1,0:T(8,128)(2,1)S(1)} collective-permute-done((bf16[2,128,1536]{2,1,0:T(8,128)(2,1)}, bf16[2,128,1536]{2,1,0:T(8,128)(2,1)S(1)}, u32[]{:S(2)}, u32[]{:S(2)}) %collective-permute-start.1) | collective-permute-done | bytes 786464 | tf_op jit(solution)/shard_map/ppermute | solution.py:290
  263.5 42.0 %all-gather.5.cloned.1.call-done = bf16[8,128,1536]{2,1,0:T(8,128)(2,1)} async-done(((bf16[2,128,1536]{2,1,0:T(8,128)(2,1)}), bf16[8,128,1536]{2,1,0:T(8,128)(2,1)}) %all-gather.5.cloned.1.call-update) | async-done | bytes 3145744 | tf_op jit(solution)/shard_map/all_gather | solution.py:282
  305.6 5.5 %fusion.50 = f32[1024,512]{1,0:T(8,128)} fusion(bf16[1024,1536]{1,0:T(8,128)(2,1)} %bitcast.84, bf16[1536,512]{1,0:T(8,128)(2,1)} %param.29), kind=kOutput, calls=%fused_computation.104 | convolution fusion | flops 1610612736 | bytes 6815744 | tf_op jit(solution)/shard_map/dot_general | solution.py:407
  311.1 8.2 %convolution_convert_fusion.1 = bf16[1024,1536]{1,0:T(8,128)(2,1)} fusion(bf16[512,1536]{1,0:T(8,128)(2,1)S(1)} %copy-done, f32[1024,512]{1,0:T(8,128)} %fusion.50, bf16[1024,1536]{1,0:T(8,128)(2,1)} %bitcast.85, bf16[1536,512]{1,0:T(8,128)(2,1)} %param.30), kind=kOutput, calls=%fused_computation.2 | convolution fusion | flops 3225944064 | bytes 11534336 | tf_op jit(solution)/shard_map/dot_general | solution.py:411
  319.3 41.2 %reduce-scatter.5.cloned.1.call-done = bf16[2,128,1536]{2,1,0:T(8,128)(2,1)} async-done(((bf16[8,128,1536]{2,1,0:T(8,128)(2,1)}), bf16[2,128,1536]{2,1,0:T(8,128)(2,1)}) %reduce-scatter.5.cloned.1.call-update) | async-done | bytes 786448 | tf_op jit(solution)/shard_map/reduce_scatter | solution.py:297
  362.3 3.6 collective-permute-start.2
  366.5 19.4 %collective-permute-done.2 = bf16[128,1536]{1,0:T(8,128)(2,1)} collective-permute-done((bf16[128,1536]{1,0:T(8,128)(2,1)}, bf16[128,1536]{1,0:T(8,128)(2,1)}, u32[]{:S(2)}, u32[]{:S(2)}) %collective-permute-start.2) | collective-permute-done | bytes 393248 | tf_op jit(solution)/shard_map/ppermute | solution.py:301
  (66 shorter events, 32.0 us)
Async XLA Ops:
  6.5 304.5 %copy-start = (bf16[512,1536]{1,0:T(8,128)(2,1)S(1)}, bf16[512,1536]{1,0:T(8,128)(2,1)}, u32[]{:S(2)}) copy-start(bf16[512,1536]{1,0:T(8,128)(2,1)} %param.31) | copy-start | bytes 4718596
  6.5 28.1 %copy-start.3 = (f32[1536]{0:T(1024)S(1)}, f32[1536]{0:T(1024)}, u32[]{:S(2)}) copy-start(f32[1536]{0:T(1024)} %param.19) | copy-start | bytes 18436
  7.8 26.5 %collective-permute-start = (bf16[128,1536]{1,0:T(8,128)(2,1)S(1)}, bf16[128,1536]{1,0:T(8,128)(2,1)S(1)}, u32[]{:S(2)}, u32[]{:S(2)}) collective-permute-start(bf16[128,1536]{1,0:T(8,128)(2,1)S(1)} %reshape.350), channel_id=1, source_target_pairs={{0,4},{4,0},{1,5},{5,1},{2,6},{6,2},{3,7},{7,3},{8,12},{12,8},{9,1... | collective-permute-start | bytes 1179656 | tf_op jit(solution)/shard_map/ppermute | solution.py:277
  14.3 19.8 %all-to-all-start = ((s32[32,1,2]{2,1,0:T(1,128)}), s32[32,1,2]{2,1,0:T(1,128)S(1)}, u32[]{:S(2)}, u32[]{:S(2)}) async-start(s32[32,1,2]{2,1,0:T(1,128)} %broadcast_in_dim.16), calls=%async_computation | async-start | bytes 32768 | tf_op jit(solution)/shard_map/all_to_all | solution.py:308
  22.2 54.7 %all-gather.3.cloned.1.call-start = ((), (), s32[]{:S(2)}) async-start(), calls=%async_computation.4 | async-start | bytes 3932160 | tf_op jit(solution)/shard_map/all_gather | solution.py:282
  42.5 76.8 %all-to-all-start.1 = ((bf16[32,2,2,128,96]{3,4,2,1,0:T(8,128)(2,1)}), bf16[32,2,2,128,96]{3,4,2,1,0:T(8,128)(2,1)}, u32[]{:S(2)}, u32[]{:S(2)}) async-start(bf16[32,2,2,128,96]{3,4,2,1,0:T(8,128)(2,1)} %broadcast_select_fusion), calls=%async_computation.1 | async-start | bytes 6291456 | tf_op jit(solution)/shard_map/all_to_all | solution.py:313
  48.9 171.5 %reduce-scatter.3.cloned.1.call-start = ((), (), s32[]{:S(2)}) async-start(), calls=%async_computation.5 | async-start | bytes 3932160 | tf_op jit(solution)/shard_map/reduce_scatter | solution.py:289
  52.8 3.9 copy-start.5
  52.8 24.1 %copy-start.6 = (bf16[1536,192]{0,1:T(8,128)(2,1)S(1)}, bf16[1536,192]{0,1:T(8,128)(2,1)}, u32[]{:S(2)}) copy-start(bf16[1536,192]{0,1:T(8,128)(2,1)} %param.20) | copy-start | bytes 1769476
  80.7 5.7 %copy-start.1 = (bf16[1536,96]{0,1:T(8,128)(2,1)S(1)}, bf16[1536,96]{0,1:T(8,128)(2,1)}, u32[]{:S(2)}) copy-start(bf16[1536,96]{0,1:T(8,128)(2,1)} %param.21) | copy-start | bytes 884740
  89.4 2.7 copy-start.2
  176.4 86.0 %copy-start.4 = (f32[1536]{0:T(1024)S(1)}, f32[1536]{0:T(1024)}, u32[]{:S(2)}) copy-start(f32[1536]{0:T(1024)} %param.28) | copy-start | bytes 18436
  176.4 129.2 %all-gather.5.cloned.1.call-start = ((), (), s32[]{:S(2)}) async-start(), calls=%async_computation.6 | async-start | bytes 3932160 | tf_op jit(solution)/shard_map/all_gather | solution.py:282
  220.4 40.4 %collective-permute-start.1 = (bf16[2,128,1536]{2,1,0:T(8,128)(2,1)}, bf16[2,128,1536]{2,1,0:T(8,128)(2,1)S(1)}, u32[]{:S(2)}, u32[]{:S(2)}) collective-permute-start(bf16[2,128,1536]{2,1,0:T(8,128)(2,1)} %reduce-scatter.3.cloned.1.call-done), channel_id=1, source_target_pairs={{0,4},{4,0},{1,5},{5,1},{2,6},{6,2},{3,7},{7,3},{8,12},{12,8},{9,1... | collective-permute-start | bytes 2359304 | tf_op jit(solution)/shard_map/ppermute | solution.py:290
  263.5 97.0 %reduce-scatter.5.cloned.1.call-start = ((), (), s32[]{:S(2)}) async-start(), calls=%async_computation.7 | async-start | bytes 3932160 | tf_op jit(solution)/shard_map/reduce_scatter | solution.py:297
  362.3 23.6 %collective-permute-start.2 = (bf16[128,1536]{1,0:T(8,128)(2,1)}, bf16[128,1536]{1,0:T(8,128)(2,1)}, u32[]{:S(2)}, u32[]{:S(2)}) collective-permute-start(bf16[128,1536]{1,0:T(8,128)(2,1)} %dynamic-slice_bitcast_fusion), channel_id=1, source_target_pairs={{0,4},{4,0},{1,5},{5,1},{2,6},{6,2},{3,7},{7,3},{8,12},{12,8},{9,1... | collective-permute-start | bytes 1179656 | tf_op jit(solution)/shard_map/ppermute | solution.py:301
Sparse Core Ops, SparseCore 0:
  36.0 40.8 all-gather.2
  176.5 43.8 reduce-scatter.2
  263.6 41.9 all-gather.4
  319.4 41.0 reduce-scatter.4

commit v13 on v11

--- a/solution.py
+++ b/solution.py
@@ -43,7 +43,7 @@
     )
 
 
-KEY_BLOCK = 512
+KEY_BLOCK = 1024
 
 
 def absorber(q_ref, peak, total, acc):
@@ -112,7 +112,9 @@
 
     @pl.when(block == window_blocks)
     def _():
-        absorb(nk_ref[0], nv_ref[0], cols <= rows)
+        fresh_shape = (row_count, FRESH_TOKENS)
+        fresh_rows = lax.rem(lax.broadcasted_iota(jnp.int32, fresh_shape, 0), FRESH_TOKENS)
+        absorb(nk_ref[0], nv_ref[0], lax.broadcasted_iota(jnp.int32, fresh_shape, 1) <= fresh_rows)
 
 
 def flip(block_ref):
@@ -185,8 +187,8 @@
                 pl.BlockSpec((1, row_count, width), fixed_pick),
                 key_spec(window_pick),
                 key_spec(window_pick),
-                key_spec(fixed_pick),
-                key_spec(fixed_pick),
+                pl.BlockSpec((1, FRESH_TOKENS, width), fixed_pick),
+                pl.BlockSpec((1, FRESH_TOKENS, width), fixed_pick),
             ],
             out_specs=state_specs,
         ),

time: 397 us -> 369 us (0.929)
  Pallas kernels: 137 us -> 106 us
  waiting for transfers between devices: 156 us -> 160 us
    pallas_call x1, Pallas kernels: 49.6 us -> 25.3 us  [attention(): pl.pallas_call(prompt_kernel, grid_spec=pltpu.PrefetchScalarGridSpec(num_...]
    pallas_call x1, Pallas kernels: 23.4 us -> 16.3 us  [attention(): pl.pallas_call(recent_kernel, grid_spec=pltpu.PrefetchScalarGridSpec(num_...]
    all_to_all x1, waiting for transfers between devices: 0.01 us -> 7.06 us  [prompt_for_requests(): return lax.all_to_all(outgoing, 'dp', 0, 0, tiled=False)]
  transfers between devices with their start and end apart: 7 -> 7, of which waited for: 5 -> 6; matrix products, arithmetic and copies ran while one was open for 9% -> 10% of each run, Pallas kernels for 6% -> 4%
where the time goes in v13:
time: 369 us; the launch traced here: 368 us
  waiting for transfers between devices  160 us (43%)
  Pallas kernels  106 us (29%)
  matrix products  26.3 us (7%)
  local copies, waits for them, and re-layouts  23.9 us (6%)
  starting transfers between devices  19.9 us (5%)
  other arithmetic  18.9 us (5%)
  between operations  13.4 us (4%)
    pallas_call x2, Pallas kernels, exchange(): pl.pallas_call(exchange_kernel, out_shape=jax.ShapeDtypeStruct(piece.shap...  64.1 us
    all_gather x2, waiting for transfers between devices, gather_rows(): lax.all_gather(pair, 'y', axis=0, tiled=True)  59.2 us
    reduce_scatter x1, waiting for transfers between devices, reduce_rows(): part = lax.psum_scatter(split, 'y', scatter_dimension=0, tiled=True)  42 us
    reduce_scatter x1, waiting for transfers between devices, scatter_rows(): part = lax.psum_scatter(split, 'y', scatter_dimension=0, tiled=True)  40.7 us
    pallas_call x1, Pallas kernels, attention(): pl.pallas_call(prompt_kernel, grid_spec=pltpu.PrefetchScalarGridSpec(num_...  25.3 us
    pallas_call x1, Pallas kernels, attention(): pl.pallas_call(recent_kernel, grid_spec=pltpu.PrefetchScalarGridSpec(num_...  16.3 us
    all_to_all x1, waiting for transfers between devices, prompt_for_requests(): lax.all_to_all(jnp.broadcast_to(prompt_group[None], (dp_size,) + prompt_g...  10.8 us
    dot_general x1, matrix products, body(): jnp.dot(hidden, w_down, preferred_element_type=jnp.float32)  8.2 us
  transfers between devices with their start and end apart: 7, of which 6 were waited for; matrix products, arithmetic and copies ran while one was open for 10% of the time, Pallas kernels for 4%

profile of v13, /device:TPU:65, one launch (start us, length us, event | category | flops | bytes accessed | tf_op | source)
XLA Modules:
  0.0 367.7 jit_solution(7045675635237297149)
XLA Ops:
  7.8 5.2 %collective-permute-start = (bf16[128,1536]{1,0:T(8,128)(2,1)S(1)}, bf16[128,1536]{1,0:T(8,128)(2,1)S(1)}, u32[]{:S(2)}, u32[]{:S(2)}) collective-permute-start(bf16[128,1536]{1,0:T(8,128)(2,1)S(1)} %reshape.350), channel_id=1, source_target_pairs={{0,4},{4,0},{1,5},{5,1},{2,6},{6,2},{3,7},{7,3},{8,12},{12,8},{9,1... | collective-permute-start | bytes 1179656 | tf_op jit(solution)/shard_map/ppermute | solution.py:279
  14.3 7.9 %all-to-all-start = ((s32[32,1,2]{2,1,0:T(1,128)}), s32[32,1,2]{2,1,0:T(1,128)S(1)}, u32[]{:S(2)}, u32[]{:S(2)}) async-start(s32[32,1,2]{2,1,0:T(1,128)} %broadcast_in_dim.16), calls=%async_computation | async-start | bytes 32768 | tf_op jit(solution)/shard_map/all_to_all | solution.py:308
  23.3 10.8 %all-to-all-done = s32[32,1,2]{2,1,0:T(1,128)S(1)} async-done(((s32[32,1,2]{2,1,0:T(1,128)}), s32[32,1,2]{2,1,0:T(1,128)S(1)}, u32[]{:S(2)}, u32[]{:S(2)}) %all-to-all-start) | async-done | bytes 288 | tf_op jit(solution)/shard_map/all_to_all | solution.py:308
  36.0 2.6 gather_fusion
  38.5 3.9 %broadcast_select_fusion = bf16[32,2,2,128,96]{3,4,2,1,0:T(8,128)(2,1)} fusion(bf16[32,2,2,128,96]{3,4,2,1,0:T(8,128)(2,1)} %bitcast.68, pred[32,2]{1,0:T(8,128)(4,1)S(1)} %copy.43), kind=kLoop, calls=%fused_computation.3 | loop fusion | flops 1572864 | bytes 6291520 | tf_op jit(solution)/shard_map/jit(_take)/select_n | solution.py:312
  42.5 6.4 %all-to-all-start.1 = ((bf16[32,2,2,128,96]{3,4,2,1,0:T(8,128)(2,1)}), bf16[32,2,2,128,96]{3,4,2,1,0:T(8,128)(2,1)}, u32[]{:S(2)}, u32[]{:S(2)}) async-start(bf16[32,2,2,128,96]{3,4,2,1,0:T(8,128)(2,1)} %broadcast_select_fusion), calls=%async_computation.1 | async-start | bytes 6291456 | tf_op jit(solution)/shard_map/all_to_all | solution.py:313
  48.9 3.9 %copy.51.wk_ref = bf16[2,4096,96]{2,1,0:T(8,128)(2,1)} copy(bf16[2,4096,96]{1,2,0:T(8,128)(2,1)} %param.24) | data formatting | bytes 3145728 | tf_op args[8]
  52.8 3.9 %copy.52.wv_ref = bf16[2,4096,96]{2,1,0:T(8,128)(2,1)} copy(bf16[2,4096,96]{1,2,0:T(8,128)(2,1)} %param.25) | data formatting | bytes 3145728 | tf_op args[9]
  59.5 17.4 %all-gather.3.cloned.1.call-done = bf16[8,128,1536]{2,1,0:T(8,128)(2,1)} async-done(((bf16[2,128,1536]{2,1,0:T(8,128)(2,1)}), bf16[8,128,1536]{2,1,0:T(8,128)(2,1)}) %all-gather.3.cloned.1.call-update) | async-done | bytes 3145744 | tf_op jit(solution)/shard_map/all_gather | solution.py:284
  76.9 3.0 fusion.49
  84.6 3.0 convolution_bitcast_fusion
  90.2 3.0 convolution_convert_fusion.2
  94.1 16.3 %shard_map.154 = (f32[2,1024,96]{2,1,0:T(8,128)}, f32[2,1024,1]{2,1,0:T(8,128)}, f32[2,1024,1]{2,1,0:T(8,128)}) custom-call(s32[2]{0:T(128)} %length_ref.3, bf16[2,1024,96]{2,1,0:T(8,128)(2,1)} %bitcast.76, bf16[2,4096,96]{2,1,0:T(8,128)(2,1)} %copy.51.wk_ref, bf16[2,4096,96]{2,1,0:T(8,128)(2,1)} %copy.52.wv_ref, bf16[2,512,96]{2,1,0:T(8,128)(2,1)} %bitcast.79, ...), custom_call_target="tpu_custom_call" | custom-call | flops 3623878656 | bytes 3538944 | tf_op jit(solution)/shard_map/pallas_call | solution.py:181
  110.4 7.1 %all-to-all-done.1 = bf16[32,2,2,128,96]{3,4,2,1,0:T(8,128)(2,1)} async-done(((bf16[32,2,2,128,96]{3,4,2,1,0:T(8,128)(2,1)}), bf16[32,2,2,128,96]{3,4,2,1,0:T(8,128)(2,1)}, u32[]{:S(2)}, u32[]{:S(2)}) %all-to-all-start.1) | async-done | bytes 3145760 | tf_op jit(solution)/shard_map/all_to_all | solution.py:313
  117.5 25.3 %shard_map.155 = bf16[2,1024,96]{2,1,0:T(8,128)(2,1)} custom-call(s32[2]{0:T(128)} %length_ref.3, bf16[2,1024,96]{2,1,0:T(8,128)(2,1)} %bitcast.77, bf16[32,2,2,96,128]{4,3,2,1,0:T(8,128)(2,1)} %bitcast.18.pk_ref.pv_ref, bf16[32,2,2,96,128]{4,3,2,1,0:T(8,128)(2,1)} %bitcast.18.pk_ref.pv_ref, f32[2,1024,96]{2,1,0:T(8,128)} %get-tuple-element.8.acc_in, ...), custom_call_target="tpu_custom_call" | custom-call | flops 3221225472 | bytes 3145728 | tf_op jit(solution)/shard_map/pallas_call | solution.py:216
  144.7 3.7 %convolution_convert_fusion = bf16[1024,1536]{1,0:T(8,128)(2,1)} fusion(bf16[1024,192]{1,0:T(8,128)(2,1)S(1)} %reshape_reshape.3, bf16[192,1536]{1,0:T(8,128)(2,1)} %param.23), kind=kOutput, calls=%fused_computation.1 | convolution fusion | flops 605552640 | bytes 4128768 | tf_op jit(solution)/shard_map/dot_general | solution.py:395
  148.4 42.0 %reduce-scatter.3.cloned.1.call-done.piece_ref = bf16[2,128,1536]{2,1,0:T(8,128)(2,1)} async-done(((bf16[8,128,1536]{2,1,0:T(8,128)(2,1)}), bf16[2,128,1536]{2,1,0:T(8,128)(2,1)}) %reduce-scatter.3.cloned.1.call-update) | async-done | bytes 786448 | tf_op jit(solution)/shard_map/reduce_scatter | solution.py:291
  190.4 40.5 %shard_map.156 = bf16[2,128,1536]{2,1,0:T(8,128)(2,1)} custom-call(bf16[2,128,1536]{2,1,0:T(8,128)(2,1)} %reduce-scatter.3.cloned.1.call-done.piece_ref), custom_call_target="tpu_custom_call" | custom-call | tf_op jit(solution)/shard_map/pallas_call | solution.py:267
  234.2 41.8 %all-gather.5.cloned.1.call-done = bf16[8,128,1536]{2,1,0:T(8,128)(2,1)} async-done(((bf16[2,128,1536]{2,1,0:T(8,128)(2,1)}), bf16[8,128,1536]{2,1,0:T(8,128)(2,1)}) %all-gather.5.cloned.1.call-update) | async-done | bytes 3145744 | tf_op jit(solution)/shard_map/all_gather | solution.py:284
  276.0 5.5 %fusion.50 = f32[1024,512]{1,0:T(8,128)} fusion(bf16[1024,1536]{1,0:T(8,128)(2,1)} %bitcast.84, bf16[1536,512]{1,0:T(8,128)(2,1)} %param.29), kind=kOutput, calls=%fused_computation.104 | convolution fusion | flops 1610612736 | bytes 6815744 | tf_op jit(solution)/shard_map/dot_general | solution.py:407
  281.5 8.2 %convolution_convert_fusion.1 = bf16[1024,1536]{1,0:T(8,128)(2,1)} fusion(bf16[512,1536]{1,0:T(8,128)(2,1)S(1)} %copy-done, f32[1024,512]{1,0:T(8,128)} %fusion.50, bf16[1024,1536]{1,0:T(8,128)(2,1)} %bitcast.85, bf16[1536,512]{1,0:T(8,128)(2,1)} %param.30), kind=kOutput, calls=%fused_computation.2 | convolution fusion | flops 3225944064 | bytes 11534336 | tf_op jit(solution)/shard_map/dot_general | solution.py:411
  290.3 40.7 %reduce-scatter.5.cloned.1.call-done = bf16[2,128,1536]{2,1,0:T(8,128)(2,1)} async-done(((bf16[8,128,1536]{2,1,0:T(8,128)(2,1)}), bf16[2,128,1536]{2,1,0:T(8,128)(2,1)}) %reduce-scatter.5.cloned.1.call-update) | async-done | bytes 786448 | tf_op jit(solution)/shard_map/reduce_scatter | solution.py:299
  332.7 23.6 %shard_map.157 = bf16[128,1536]{1,0:T(8,128)(2,1)} custom-call(bf16[128,1536]{1,0:T(8,128)(2,1)} %dynamic-slice_bitcast_fusion.piece_ref), custom_call_target="tpu_custom_call" | custom-call | tf_op jit(solution)/shard_map/pallas_call | solution.py:267
  358.9 2.3 add_convert_fusion
  (64 shorter events, 26.6 us)
Async XLA Ops:
  6.5 275.0 %copy-start = (bf16[512,1536]{1,0:T(8,128)(2,1)S(1)}, bf16[512,1536]{1,0:T(8,128)(2,1)}, u32[]{:S(2)}) copy-start(bf16[512,1536]{1,0:T(8,128)(2,1)} %param.31) | copy-start | bytes 4718596
  6.5 28.1 %copy-start.3 = (f32[1536]{0:T(1024)S(1)}, f32[1536]{0:T(1024)}, u32[]{:S(2)}) copy-start(f32[1536]{0:T(1024)} %param.19) | copy-start | bytes 18436
  7.8 26.5 %collective-permute-start = (bf16[128,1536]{1,0:T(8,128)(2,1)S(1)}, bf16[128,1536]{1,0:T(8,128)(2,1)S(1)}, u32[]{:S(2)}, u32[]{:S(2)}) collective-permute-start(bf16[128,1536]{1,0:T(8,128)(2,1)S(1)} %reshape.350), channel_id=1, source_target_pairs={{0,4},{4,0},{1,5},{5,1},{2,6},{6,2},{3,7},{7,3},{8,12},{12,8},{9,1... | collective-permute-start | bytes 1179656 | tf_op jit(solution)/shard_map/ppermute | solution.py:279
  14.3 19.8 %all-to-all-start = ((s32[32,1,2]{2,1,0:T(1,128)}), s32[32,1,2]{2,1,0:T(1,128)S(1)}, u32[]{:S(2)}, u32[]{:S(2)}) async-start(s32[32,1,2]{2,1,0:T(1,128)} %broadcast_in_dim.16), calls=%async_computation | async-start | bytes 32768 | tf_op jit(solution)/shard_map/all_to_all | solution.py:308
  22.2 54.7 %all-gather.3.cloned.1.call-start = ((), (), s32[]{:S(2)}) async-start(), calls=%async_computation.4 | async-start | bytes 3932160 | tf_op jit(solution)/shard_map/all_gather | solution.py:284
  42.5 75.0 %all-to-all-start.1 = ((bf16[32,2,2,128,96]{3,4,2,1,0:T(8,128)(2,1)}), bf16[32,2,2,128,96]{3,4,2,1,0:T(8,128)(2,1)}, u32[]{:S(2)}, u32[]{:S(2)}) async-start(bf16[32,2,2,128,96]{3,4,2,1,0:T(8,128)(2,1)} %broadcast_select_fusion), calls=%async_computation.1 | async-start | bytes 6291456 | tf_op jit(solution)/shard_map/all_to_all | solution.py:313
  48.9 141.5 %reduce-scatter.3.cloned.1.call-start = ((), (), s32[]{:S(2)}) async-start(), calls=%async_computation.5 | async-start | bytes 3932160 | tf_op jit(solution)/shard_map/reduce_scatter | solution.py:291
  52.8 3.9 %copy-start.5 = (s32[2]{0:T(128)S(1)}, s32[2]{0:T(128)}, u32[]{:S(2)}) copy-start(s32[2]{0:T(128)} %length_ref.3) | copy-start | bytes 28
  52.8 24.1 %copy-start.6 = (bf16[1536,192]{0,1:T(8,128)(2,1)S(1)}, bf16[1536,192]{0,1:T(8,128)(2,1)}, u32[]{:S(2)}) copy-start(bf16[1536,192]{0,1:T(8,128)(2,1)} %param.20) | copy-start | bytes 1769476
  82.2 2.4 copy-start.1
  87.6 2.7 copy-start.2
  148.4 84.3 %copy-start.4 = (f32[1536]{0:T(1024)S(1)}, f32[1536]{0:T(1024)}, u32[]{:S(2)}) copy-start(f32[1536]{0:T(1024)} %param.28) | copy-start | bytes 18436
  148.4 127.6 %all-gather.5.cloned.1.call-start = ((), (), s32[]{:S(2)}) async-start(), calls=%async_computation.6 | async-start | bytes 3932160 | tf_op jit(solution)/shard_map/all_gather | solution.py:284
  233.9 97.0 %reduce-scatter.5.cloned.1.call-start = ((), (), s32[]{:S(2)}) async-start(), calls=%async_computation.7 | async-start | bytes 3932160 | tf_op jit(solution)/shard_map/reduce_scatter | solution.py:299
Sparse Core Ops, SparseCore 0:
  36.0 40.8 all-gather.2
  148.5 41.8 reduce-scatter.2
  234.0 41.9 all-gather.4
  289.8 41.0 reduce-scatter.4
